TPU v7x, 32 devices: a whole 2x2x4 slice. The times are simulated.
32 devices in a mesh: dp: 16 (over z, y, x), head: 2 (over core).
Axes of the slice: x: 2, y: 2, z: 4, core: 2. Of those that a mesh axis runs over, the one named last changes fastest.
Arguments:
- rows_in: bfloat16 [32, 1024, 128], P(('dp', 'head')), may hold values from -6 to 6
- feat_mask: int32 [32, 128], P(('dp', 'head')), may hold values 0 or 1
- counts: int32 [32], replicated, may hold values from 64 to 768, as said below
- ctx_vals: float32 [32, 768], P(('dp', 'head')), may hold values from -6 to 6
- targets: int32 [32, 256], P(('dp', 'head')), may hold values from 0 to 511
- query_mask: int32 [32, 256], P(('dp', 'head')), may hold values from 0 to 1, as said below
- w_emb: float32 [128, 768], replicated, may hold values from -0.5 to 0.5
- m_emb: float32 [128, 768], replicated, may hold values from -1.5258789e-05 to 1.5258789e-05
- a_emb: float32 [128, 768], replicated, may hold values from -0.5 to 0.5
- vectors: float32 [16, 768], replicated
- m_vec: float32 [16, 768], replicated, may hold values from -1.5258789e-05 to 1.5258789e-05
- a_vec: float32 [16, 768], replicated
- w_qkv: float32 [2, 768, 3, 2, 384], P(None, 'dp', None, 'head'), may hold values from -0.21875 to 0.21875
- m_qkv: float32 [2, 768, 3, 2, 384], P(None, 'dp', None, 'head'), may hold values from -1.5258789e-05 to 1.5258789e-05
- a_qkv: float32 [2, 768, 3, 2, 384], P(None, 'dp', None, 'head'), may hold values from -0.21875 to 0.21875
- w_out: float32 [2, 2, 384, 768], P(None, 'head', 'dp'), may hold values from -0.875 to 0.875
- m_out: float32 [2, 2, 384, 768], P(None, 'head', 'dp'), may hold values from -1.5258789e-05 to 1.5258789e-05
- a_out: float32 [2, 2, 384, 768], P(None, 'head', 'dp'), may hold values from -0.875 to 0.875
- w_up: float32 [2, 768, 3072], P(None, ('dp', 'head')), may hold values from -0.21875 to 0.21875
- m_up: float32 [2, 768, 3072], P(None, ('dp', 'head')), may hold values from -1.5258789e-05 to 1.5258789e-05
- a_up: float32 [2, 768, 3072], P(None, ('dp', 'head')), may hold values from -0.21875 to 0.21875
- w_down: float32 [2, 3072, 768], P(None, ('dp', 'head')), may hold values from -0.109375 to 0.109375
- m_down: float32 [2, 3072, 768], P(None, ('dp', 'head')), may hold values from -1.5258789e-05 to 1.5258789e-05
- a_down: float32 [2, 3072, 768], P(None, ('dp', 'head')), may hold values from -0.109375 to 0.109375
- w_head: float32 [768, 512], replicated, may hold values from -0.4375 to 0.4375
- m_head: float32 [768, 512], replicated, may hold values from -1.5258789e-05 to 1.5258789e-05
- a_head: float32 [768, 512], replicated, may hold values from -0.4375 to 0.4375
Outputs:
- loss: float32 [], replicated
- grad_norm: float32 [], replicated
- new_w_emb: float32 [128, 768], replicated
- new_m_emb: float32 [128, 768], replicated
- new_a_emb: float32 [128, 768], replicated
- new_vectors: float32 [16, 768], replicated
- new_m_vec: float32 [16, 768], replicated
- new_a_vec: float32 [16, 768], replicated
- new_w_qkv: float32 [2, 768, 3, 2, 384], P(None, 'dp', None, 'head')
- new_m_qkv: float32 [2, 768, 3, 2, 384], P(None, 'dp', None, 'head')
- new_a_qkv: float32 [2, 768, 3, 2, 384], P(None, 'dp', None, 'head')
- new_w_out: float32 [2, 2, 384, 768], P(None, 'head', 'dp')
- new_m_out: float32 [2, 2, 384, 768], P(None, 'head', 'dp')
- new_a_out: float32 [2, 2, 384, 768], P(None, 'head', 'dp')
- new_w_up: float32 [2, 768, 3072], P(None, ('dp', 'head'))
- new_m_up: float32 [2, 768, 3072], P(None, ('dp', 'head'))
- new_a_up: float32 [2, 768, 3072], P(None, ('dp', 'head'))
- new_w_down: float32 [2, 3072, 768], P(None, ('dp', 'head'))
- new_m_down: float32 [2, 3072, 768], P(None, ('dp', 'head'))
- new_a_down: float32 [2, 3072, 768], P(None, ('dp', 'head'))
- new_w_head: float32 [768, 512], replicated
- new_m_head: float32 [768, 512], replicated
- new_a_head: float32 [768, 512], replicated
Inputs may be any that keep to these rules, and one draw needn't show every extreme that they name: Slots 0 to counts[t] - 1 of table t hold context; table 0 fills all 768, table 1 holds the least, 64. `query_mask`: the first query row of every table is true.
All inputs are finite; a program needn't handle non-finite values. No bound on the sum of `feat_mask` on one device may be relied on, other than what follows from the above.
Results may differ from a plain program's by a relative error of at most 0.012.
Values may be sent and summed in bfloat16 or wider, within the bound.
A program may use at most 256 MiB of HBM per device.

v0:
```python
import jax
import jax.numpy as jnp
from jax import lax
from jax.sharding import PartitionSpec as P

HD = 64
CTX = 768


eps_norm = 1e-05
clip_at = 0.01
rate = 3000.0
moment = 0.9
keep_avg = 0.9
decay_wd = 1e-05
low_type = jnp.bfloat16
wide_type = jnp.float32


def layer_norm(values, gain_row, shift_row):
    center = values - jnp.mean(values, -1, keepdims=True)
    spread = jnp.mean(center * center, -1, keepdims=True)
    return center * lax.rsqrt(spread + eps_norm) * gain_row + shift_row


def norm_back(values, gain_row, shift_row, upstream):
    _, pull = jax.vjp(layer_norm, values, gain_row, shift_row)
    return pull(upstream)


def gelu_back(values, upstream):
    _, pull = jax.vjp(jax.nn.gelu, values)
    return pull(upstream)[0]


def matmul(first_op, second_op):
    return jnp.dot(first_op, second_op, preferred_element_type=wide_type)


def matmul_tn(first_op, second_op):
    return lax.dot_general(
        first_op, second_op, (((0,), (0,)), ((), ())), preferred_element_type=wide_type
    )


def matmul_nt(first_op, second_op):
    return lax.dot_general(
        first_op, second_op, (((1,), (1,)), ((), ())), preferred_element_type=wide_type
    )


def block_scores(q_block, k_block, key_valid):
    raw_score = jnp.einsum("rhe,che->hrc", q_block, k_block, preferred_element_type=wide_type)
    raw_score = raw_score * q_block.shape[-1] ** (-0.5)
    return jnp.where(key_valid[None, None, :], raw_score, -1e30)


def block_layout(queries):
    tables, row_count, head_count, head_width = queries.shape
    block_rows = min(512, row_count)
    per_table = row_count // block_rows
    owners = jnp.arange(tables * per_table) // per_table
    return ((tables * per_table, block_rows, head_count, head_width), owners, per_table)


def attend(queries, key_rows, value_rows, key_valid):
    tables, row_count, head_count, head_width = queries.shape
    shape_blocks, owners, per_table = block_layout(queries)

    def one_block(block_item):
        q_block, block_owner = block_item
        score = block_scores(q_block, key_rows[block_owner], key_valid[block_owner])
        row_peak = jnp.max(score, -1, keepdims=True)
        lifted = jnp.exp(score - row_peak)
        row_total = jnp.sum(lifted, -1, keepdims=True)
        soft_prob = (lifted / row_total).astype(low_type)
        block_out = jnp.einsum(
            "hrc,che->rhe", soft_prob, value_rows[block_owner], preferred_element_type=wide_type
        )
        return (block_out.astype(low_type), (row_peak + jnp.log(row_total))[..., 0])

    mixed_rows, log_total = lax.map(one_block, (queries.reshape(shape_blocks), owners))
    return (mixed_rows.reshape((tables * row_count, head_count * head_width)), log_total)


def attend_back(queries, key_rows, value_rows, key_valid, log_total, grad_mixed):
    tables, row_count, head_count, head_width = queries.shape
    ctx_rows = key_rows.shape[1]
    shape_blocks, owners, per_table = block_layout(queries)
    score_scale = head_width ** (-0.5)

    def one_block(block_item):
        q_block, g_block, total_block, block_owner = block_item
        k_block = key_rows[block_owner]
        v_block = value_rows[block_owner]
        soft_prob = jnp.exp(
            block_scores(q_block, k_block, key_valid[block_owner]) - total_block[..., None]
        )
        grad_prob = jnp.einsum("rhe,che->hrc", g_block, v_block, preferred_element_type=wide_type)
        grad_value = jnp.einsum(
            "hrc,rhe->che", soft_prob.astype(low_type), g_block, preferred_element_type=wide_type
        )
        grad_score = soft_prob * (grad_prob - jnp.sum(soft_prob * grad_prob, -1, keepdims=True))
        grad_score = grad_score.astype(low_type)
        grad_query = (
            jnp.einsum("hrc,che->rhe", grad_score, k_block, preferred_element_type=wide_type)
            * score_scale
        )
        grad_key = (
            jnp.einsum("hrc,rhe->che", grad_score, q_block, preferred_element_type=wide_type)
            * score_scale
        )
        return (grad_query.astype(low_type), grad_key, grad_value)

    blocks_in = (queries.reshape(shape_blocks), grad_mixed.reshape(shape_blocks), log_total, owners)
    grad_q, grad_k, grad_v = lax.map(one_block, blocks_in)
    flat_width = head_count * head_width

    def key_side(blocked):
        summed = blocked.reshape((tables, per_table, ctx_rows, flat_width)).sum(1).astype(low_type)
        padding = jnp.zeros((tables, row_count - ctx_rows, flat_width), low_type)
        return jnp.concatenate([summed, padding], 1).reshape((tables * row_count, flat_width))

    return jnp.concatenate(
        [grad_q.reshape((tables * row_count, flat_width)), key_side(grad_k), key_side(grad_v)], 1
    )


def layer_forward(residual, vec_rows, w_joined, w_mix, w_grow, w_shrink, key_valid):
    normed_half = layer_norm(residual, vec_rows[0], vec_rows[1]).astype(low_type)
    normed = lax.all_gather(normed_half, "head", axis=0, tiled=True)
    tables = key_valid.shape[0]
    row_count = normed.shape[0] // tables
    width = w_joined.shape[1] // 3
    head_shape = (tables, row_count, width // HD, HD)
    joined = matmul(normed, w_joined).astype(low_type)
    queries = joined[:, :width].reshape(head_shape)
    key_rows = joined[:, width : 2 * width].reshape(head_shape)[:, :CTX]
    value_rows = joined[:, 2 * width :].reshape(head_shape)[:, :CTX]
    mixed_rows, log_total = attend(queries, key_rows, value_rows, key_valid)
    partial_out = matmul(mixed_rows, w_mix)
    middle = (
        residual
        + lax.psum_scatter(
            partial_out.astype(jnp.bfloat16), "head", scatter_dimension=0, tiled=True
        ).astype(jnp.float32)
        + vec_rows[4]
    )
    normed_mlp = layer_norm(middle, vec_rows[2], vec_rows[3]).astype(low_type)
    hidden = matmul(normed_mlp, w_grow)
    active = jax.nn.gelu(hidden).astype(low_type)
    output = middle + matmul(active, w_shrink) + vec_rows[5]
    kept = (
        residual,
        normed,
        queries,
        key_rows,
        value_rows,
        mixed_rows,
        log_total,
        middle,
        normed_mlp,
        hidden,
        active,
    )
    return (output, kept)


def layer_backward(upstream, kept, vec_rows, w_joined, w_mix, w_grow, w_shrink, key_valid):
    (
        norm_rows,
        normed,
        queries,
        key_rows,
        value_rows,
        mixed_rows,
        log_total,
        middle,
        normed_mlp,
        hidden,
        active,
    ) = kept
    down_low = upstream.astype(low_type)
    grad_shrink = matmul_tn(active, down_low)
    grad_hidden = gelu_back(hidden, matmul_nt(down_low, w_shrink)).astype(low_type)
    grad_grow = matmul_tn(normed_mlp, grad_hidden)
    grad_middle, gain_mlp, shift_mlp = norm_back(
        middle, vec_rows[2], vec_rows[3], matmul_nt(grad_hidden, w_grow)
    )
    grad_middle = grad_middle + upstream
    mix_low = lax.all_gather(grad_middle.astype(low_type), "head", axis=0, tiled=True)
    grad_mix = matmul_tn(mixed_rows, mix_low)
    grad_mixed = matmul_nt(mix_low, w_mix).astype(low_type)
    grad_joined = attend_back(queries, key_rows, value_rows, key_valid, log_total, grad_mixed)
    grad_wjoined = matmul_tn(normed, grad_joined)
    grad_normed = lax.psum_scatter(
        matmul_nt(grad_joined, w_joined).astype(jnp.bfloat16),
        "head",
        scatter_dimension=0,
        tiled=True,
    ).astype(jnp.float32)
    grad_input, gain_attn, shift_attn = norm_back(norm_rows, vec_rows[0], vec_rows[1], grad_normed)
    vec_grads = [
        gain_attn,
        shift_attn,
        gain_mlp,
        shift_mlp,
        jnp.sum(grad_middle, 0),
        jnp.sum(upstream, 0),
    ]
    return (grad_input + grad_middle, (grad_wjoined, grad_mix, grad_grow, grad_shrink), vec_grads)


def update(weight, moment_old, average, grad_in, scale):
    applied = grad_in * scale + decay_wd * weight
    moment_new = moment * moment_old + applied
    weight_new = weight - rate * (applied + moment * moment_new)
    return (weight_new, moment_new, keep_avg * average + (1.0 - keep_avg) * weight_new)


def shards(
    rows_in,
    feat_mask,
    counts,
    ctx_vals,
    targets,
    query_mask,
    w_emb,
    m_emb,
    a_emb,
    vectors,
    m_vec,
    a_vec,
    w_qkv,
    m_qkv,
    a_qkv,
    w_out,
    m_out,
    a_out,
    w_up,
    m_up,
    a_up,
    w_down,
    m_down,
    a_down,
    w_head,
    m_head,
    a_head,
):
    local_tables, row_count, feat_count = rows_in.shape
    layer_total = w_qkv.shape[0]
    width = w_emb.shape[1]
    group = local_tables * lax.axis_size("head")
    joined_all, mix_all = (
        lax.all_gather(w_qkv.astype(low_type), "dp", axis=1, tiled=True),
        lax.all_gather(w_out.astype(low_type), "dp", axis=2, tiled=True),
    )
    grow_all, shrink_all = (
        lax.all_gather(w_up.astype(low_type), ("dp", "head"), axis=1, tiled=True),
        lax.all_gather(w_down.astype(low_type), ("dp", "head"), axis=1, tiled=True),
    )
    head_share = mix_all.shape[2]
    joined_all = joined_all.reshape((layer_total, width, 3 * head_share))
    mix_all = mix_all.reshape((layer_total, head_share, width))
    query_weight = query_mask.astype(wide_type)
    pooled = lax.psum(jnp.sum(query_weight), ("dp", "head"))
    group_counts = lax.dynamic_slice_in_dim(counts, lax.axis_index("dp") * group, group, 0)
    key_valid = jnp.arange(CTX)[None, :] < group_counts[:, None]
    masked = (rows_in * feat_mask[:, None, :].astype(low_type)).reshape(
        (local_tables * row_count, feat_count)
    )
    leading = jnp.concatenate(
        [ctx_vals, jnp.zeros((local_tables, row_count - CTX), wide_type)], 1
    ).reshape((-1, 1))
    residual = matmul(masked, w_emb.astype(low_type)) + vectors[1] + leading * vectors[0]
    kept_all = []
    for layer_at in range(layer_total):
        vec_rows = vectors[2 + 6 * layer_at : 8 + 6 * layer_at]
        residual, kept = layer_forward(
            residual,
            vec_rows,
            joined_all[layer_at],
            mix_all[layer_at],
            grow_all[layer_at],
            shrink_all[layer_at],
            key_valid,
        )
        kept_all.append(kept)
    head_low = w_head.astype(low_type)
    final_in = residual.reshape((local_tables, row_count, width))[:, CTX:].reshape((-1, width))
    final_rows = layer_norm(final_in, vectors[-2], vectors[-1]).astype(low_type)
    logits = matmul(final_rows, head_low)
    row_peak = jnp.max(logits, -1, keepdims=True)
    log_total = row_peak[:, 0] + jnp.log(jnp.sum(jnp.exp(logits - row_peak), -1))
    target_hit = (jnp.arange(logits.shape[1])[None, :] == targets.reshape((-1, 1))).astype(
        wide_type
    )
    picked = jnp.sum(logits * target_hit, -1)
    row_weight = query_weight.reshape(-1)
    loss_part = jnp.sum((log_total - picked) * row_weight) / pooled
    grad_logits = (jnp.exp(logits - log_total[:, None]) - target_hit) * (row_weight / pooled)[
        :, None
    ]
    grad_logits = grad_logits.astype(low_type)
    grad_head = matmul_tn(final_rows, grad_logits)
    grad_final, gain_final, shift_final = norm_back(
        final_in, vectors[-2], vectors[-1], matmul_nt(grad_logits, head_low)
    )
    context_zero = jnp.zeros((local_tables, CTX, width), wide_type)
    upstream = jnp.concatenate(
        [context_zero, grad_final.reshape((local_tables, -1, width))], 1
    ).reshape((-1, width))
    big_grads = [None] * layer_total
    vec_grads = [None] * layer_total
    for layer_at in reversed(range(layer_total)):
        vec_rows = vectors[2 + 6 * layer_at : 8 + 6 * layer_at]
        upstream, big_grads[layer_at], vec_grads[layer_at] = layer_backward(
            upstream,
            kept_all[layer_at],
            vec_rows,
            joined_all[layer_at],
            mix_all[layer_at],
            grow_all[layer_at],
            shrink_all[layer_at],
            key_valid,
        )
    grad_emb = matmul_tn(masked, upstream.astype(low_type))
    vec_list = [jnp.sum(upstream * leading, 0), jnp.sum(upstream, 0)]
    for layer_at in range(layer_total):
        vec_list = vec_list + vec_grads[layer_at]
    grad_vec = jnp.stack(vec_list + [gain_final, shift_final])
    grad_joined = jnp.stack([grads_at[0] for grads_at in big_grads]).reshape(
        (layer_total, width, 3, 1, head_share)
    )
    grad_mix = jnp.stack([grads_at[1] for grads_at in big_grads]).reshape(
        (layer_total, 1, head_share, width)
    )
    grad_grow = jnp.stack([grads_at[2] for grads_at in big_grads])
    grad_shrink = jnp.stack([grads_at[3] for grads_at in big_grads])
    shard_joined, shard_mix = (
        lax.psum_scatter(grad_joined, "dp", scatter_dimension=1, tiled=True),
        lax.psum_scatter(grad_mix, "dp", scatter_dimension=2, tiled=True),
    )
    shard_grow, shard_shrink = (
        lax.psum_scatter(grad_grow, ("dp", "head"), scatter_dimension=1, tiled=True),
        lax.psum_scatter(grad_shrink, ("dp", "head"), scatter_dimension=1, tiled=True),
    )
    shard_square = jnp.sum(shard_joined * shard_joined) + jnp.sum(shard_mix * shard_mix)
    shard_square = (
        shard_square + jnp.sum(shard_grow * shard_grow) + jnp.sum(shard_shrink * shard_shrink)
    )
    grad_emb, grad_vec, grad_head, loss, shard_total = lax.psum(
        (grad_emb, grad_vec, grad_head, loss_part, shard_square), ("dp", "head")
    )
    total_sq = (
        shard_total
        + jnp.sum(grad_emb * grad_emb)
        + jnp.sum(grad_vec * grad_vec)
        + jnp.sum(grad_head * grad_head)
    )
    grad_norm = jnp.sqrt(total_sq)
    scale = jnp.minimum(1.0, clip_at / grad_norm)
    e_w, e_m, e_a = update(w_emb, m_emb, a_emb, grad_emb, scale)
    v_w, v_m, v_a = update(vectors, m_vec, a_vec, grad_vec, scale)
    q_w, q_m, q_a = update(w_qkv, m_qkv, a_qkv, shard_joined, scale)
    o_w, o_m, o_a = update(w_out, m_out, a_out, shard_mix, scale)
    u_w, u_m, u_a = update(w_up, m_up, a_up, shard_grow, scale)
    d_w, d_m, d_a = update(w_down, m_down, a_down, shard_shrink, scale)
    h_w, h_m, h_a = update(w_head, m_head, a_head, grad_head, scale)
    return (
        loss,
        grad_norm,
        e_w,
        e_m,
        e_a,
        v_w,
        v_m,
        v_a,
        q_w,
        q_m,
        q_a,
        o_w,
        o_m,
        o_a,
        u_w,
        u_m,
        u_a,
        d_w,
        d_m,
        d_a,
        h_w,
        h_m,
        h_a,
    )


def solution(mesh):
    return jax.shard_map(
        shards,
        mesh=mesh,
        in_specs=(
            P(("dp", "head"), None, None),
            P(("dp", "head"), None),
            P(),
            P(("dp", "head"), None),
            P(("dp", "head"), None),
            P(("dp", "head"), None),
            P(),
            P(),
            P(),
            P(),
            P(),
            P(),
            P(None, "dp", None, "head", None),
            P(None, "dp", None, "head", None),
            P(None, "dp", None, "head", None),
            P(None, "head", "dp", None),
            P(None, "head", "dp", None),
            P(None, "head", "dp", None),
            P(None, ("dp", "head"), None),
            P(None, ("dp", "head"), None),
            P(None, ("dp", "head"), None),
            P(None, ("dp", "head"), None),
            P(None, ("dp", "head"), None),
            P(None, ("dp", "head"), None),
            P(),
            P(),
            P(),
        ),
        out_specs=(
            P(),
            P(),
            P(),
            P(),
            P(),
            P(),
            P(),
            P(),
            P(None, "dp", None, "head", None),
            P(None, "dp", None, "head", None),
            P(None, "dp", None, "head", None),
            P(None, "head", "dp", None),
            P(None, "head", "dp", None),
            P(None, "head", "dp", None),
            P(None, ("dp", "head"), None),
            P(None, ("dp", "head"), None),
            P(None, ("dp", "head"), None),
            P(None, ("dp", "head"), None),
            P(None, ("dp", "head"), None),
            P(None, ("dp", "head"), None),
            P(),
            P(),
            P(),
        ),
        check_vma=False,
    )
```

profile of v0, /device:TPU:0, one launch (start us, length us, event | category | flops | bytes accessed | tf_op | source)
XLA Modules:
  0.0 1939.3 jit_solution(6010497869375767518)
XLA Ops:
  19.4 96.1 %all-gather.11.cloned.1.call-done = bf16[2,768,3,1,384]{4,3,2,1,0:T(2,128)(2,1)} async-done(((bf16[2,48,3,1,384]{4,3,2,1,0:T(2,128)(2,1)}), bf16[2,768,3,1,384]{4,3,2,1,0:T(2,128)(2,1)}) %all-gather.11.cloned.1.call-update) | async-done | bytes 3538960 | tf_op jit(solution)/shard_map/all_gather | solution.py:255
  115.5 25.1 %slice_reduce_fusion = (bf16[768,3,384]{2,1,0:T(4,128)(2,1)}, bf16[768,3,384]{2,1,0:T(4,128)(2,1)S(1)}) fusion(bf16[2,768,3,1,384]{4,3,2,1,0:T(2,128)(2,1)} %all-gather.11.cloned.1.call-done), kind=kLoop, calls=%fused_computation.186 | loop fusion | bytes 7077888 | tf_op jit(solution)/shard_map/slice | solution.py:282
  142.2 6.7 convolution_convert_fusion.1
  153.9 3.8 reshape.391
  162.8 3.8 reshape.392
  171.7 4.2 reshape_reshape.8
  180.1 44.6 %while.52 = (s32[]{:T(128)}, bf16[4,512,6,64]{1,3,2,0:T(8,128)(2,1)}, f32[4,6,512]{2,1,0:T(8,128)S(1)}, s32[4]{0:T(128)S(1)}, bf16[2,768,6,64]{1,3,2,0:T(8,128)(...) while((s32[]{:T(128)}, ...), condition=%wide.region_5.6_spmd, body=%wide.region_2.5_spmd.sunk | while | flops 632484864 | bytes 35120324 | solution.py:82
  187.7 3.6 fusion.262
  198.8 3.6 fusion.262
  209.9 3.6 fusion.262
  221.1 3.6 fusion.262
  228.9 5.0 convolution_convert_fusion.5
  237.8 5.8 reduce-scatter.8.cloned.1.call-done
  247.7 70.3 %all-gather.15.cloned.1.call-done = bf16[2,768,3072]{2,1,0:T(8,128)(2,1)} async-done(((bf16[2,24,3072]{2,1,0:T(8,128)(2,1)}), bf16[2,768,3072]{2,1,0:T(8,128)(2,1)}) %all-gather.15.cloned.1.call-update) | async-done | bytes 9437200 | tf_op jit(solution)/shard_map/all_gather | solution.py:259
  318.0 11.3 fusion.125
  329.3 72.0 %all-gather.17.cloned.1.call-done = bf16[2,3072,768]{2,1,0:T(8,128)(2,1)} async-done(((bf16[2,96,768]{2,1,0:T(8,128)(2,1)}), bf16[2,3072,768]{2,1,0:T(8,128)(2,1)}) %all-gather.17.cloned.1.call-update) | async-done | bytes 9437200 | tf_op jit(solution)/shard_map/all_gather | solution.py:260
  401.3 11.0 fusion.197
  418.0 7.6 all-gather.19.cloned.1.call-done
  425.6 6.7 convolution_convert_fusion
  437.4 3.8 reshape.394
  446.3 3.8 reshape.395
  455.2 3.9 reshape_reshape.9
  463.3 44.6 %while.53 = (s32[]{:T(128)}, bf16[4,512,6,64]{1,3,2,0:T(8,128)(2,1)}, f32[4,6,512]{2,1,0:T(8,128)S(1)}, s32[4]{0:T(128)S(1)}, bf16[2,768,6,64]{1,3,2,0:T(8,128)(...) while((s32[]{:T(128)}, ...), condition=%wide.region_14.15_spmd, body=%wide.region_11.14_spmd.sunk | while | flops 632484864 | bytes 35120324 | solution.py:82
  470.8 3.6 fusion.266
  481.9 3.6 fusion.266
  493.1 3.6 fusion.266
  504.2 3.6 fusion.266
  512.2 3.5 convolution_convert_fusion.4
  516.9 41.1 %psum.42 = f32[]{:T(128)} all-reduce(f32[]{:T(128)} %convert_reduce_fusion.2), channel_id=1, replica_groups=mesh['dp'=16,'head'=2] {'dp','head'}, use_global_device_ids=true, to_apply=%region_25.26 | all-reduce | flops 1 | bytes 8 | tf_op jit(solution)/shard_map/psum | solution.py:266
  560.7 11.0 fusion.129
  571.7 10.5 add_bitcast_fusion
  591.5 15.8 fusion.123
  607.3 7.3 fusion.200
  614.6 3.7 copy.267
  618.3 3.5 multiply_reduce_fusion.2
  626.2 12.2 all-gather.21.cloned.1.call-done
  638.4 3.7 convolution_convert_fusion.7
  652.7 70.6 %while.54 = (s32[]{:T(128)}, bf16[4,512,6,64]{1,3,2,0:T(8,128)(2,1)}, f32[4,768,6,64]{1,3,2,0:T(8,128)}, f32[4,768,6,64]{1,3,2,0:T(8,128)}, s32[4]{0:T(128)S(1)}...) while((s32[]{:T(128)}, ...), condition=%wide.region_33.34_spmd, body=%wide.region_31.33_spmd.sunk | while | flops 1546023936 | bytes 87985160 | solution.py:116
  739.1 5.6 convolution_convert_fusion.3
  744.9 12.2 reduce-scatter.12.cloned.1.call-done
  765.1 17.5 fusion.116
  782.6 9.0 fusion.199
  791.7 3.7 copy.279
  805.1 13.5 all-gather.23.cloned.1.call-done
  818.6 3.7 convolution_convert_fusion.6
  832.8 72.5 %while.55 = (s32[]{:T(128)}, bf16[4,512,6,64]{1,3,2,0:T(8,128)(2,1)}, f32[4,768,6,64]{1,3,2,0:T(8,128)}, f32[4,768,6,64]{1,3,2,0:T(8,128)}, s32[4]{0:T(128)S(1)}...) while((s32[]{:T(128)}, ...), condition=%wide.region_43.44_spmd, body=%wide.region_41.43_spmd.sunk | while | flops 1546023936 | bytes 87985160 | solution.py:116
  921.0 5.6 convolution_convert_fusion.2
  928.0 3.5 convolution_bitcast_fusion.4
  936.1 6.8 fusion.143
  942.9 3.9 fusion.142
  950.2 13.6 copy.292
  967.8 10.6 convolution_bitcast_fusion.2
  986.7 7.4 convolution_bitcast_fusion.3
  994.1 10.9 pad_maximum_fusion
  1006.1 11.1 convolution_bitcast_fusion
  1017.2 11.1 convolution_bitcast_fusion.1
  1028.3 6.9 pad_maximum_fusion.1
  1038.8 35.8 %reduce-scatter.14.cloned.1.call-done = f32[2,1,24,768]{3,2,0,1:T(8,128)} async-done(((f32[2,1,384,768]{3,2,0,1:T(8,128)}), f32[2,1,24,768]{3,2,0,1:T(8,128)}) %reduce-scatter.14.cloned.1.call-update) | async-done | bytes 147472 | tf_op jit(solution)/shard_map/reduce_scatter | solution.py:342
  1076.3 230.1 %all-reduce.12.cloned.1.call-done = f32[2,768,3,1,384]{4,0,3,2,1:T(2,128)} async-done(((f32[2,768,3,1,384]{4,0,3,2,1:T(2,128)}), f32[2,768,3,1,384]{4,0,3,2,1:T(2,128)}) %all-reduce.12.cloned.1.call-update) | async-done | bytes 7077904
  1310.4 135.8 %all-reduce.14.cloned.1.call-done = (f32[128,768]{1,0:T(8,128)}, f32[768,512]{1,0:T(8,128)}) async-done(((f32[128,768]{1,0:T(8,128)}, f32[768,512]{1,0:T(8,128)}), (f32[128,768]{1,0:T(8,128)}, f32[768,512]{1,0:T(8,128)})) %all-reduce.14.cloned.1.call-update) | async-done | bytes 1966096 | tf_op jit(solution)/shard_map/psum | solution.py:352
  1448.6 207.9 %reduce-scatter.16.cloned.1.call-done = f32[2,24,3072]{2,1,0:T(8,128)} async-done(((f32[2,768,3072]{2,1,0:T(8,128)}), f32[2,24,3072]{2,1,0:T(8,128)}) %reduce-scatter.16.cloned.1.call-update) | async-done | bytes 589840 | tf_op jit(solution)/shard_map/reduce_scatter | solution.py:345
  1659.0 208.0 %reduce-scatter.18.cloned.1.call-done = f32[2,96,768]{2,1,0:T(8,128)} async-done(((f32[2,3072,768]{2,1,0:T(8,128)}), f32[2,96,768]{2,1,0:T(8,128)}) %reduce-scatter.18.cloned.1.call-update) | async-done | bytes 589840 | tf_op jit(solution)/shard_map/reduce_scatter | solution.py:346
  1871.5 40.2 %all-reduce.7 = (f32[]{:T(128)}, f32[]{:T(128)}, f32[16,768]{1,0:T(8,128)S(1)}) all-reduce(f32[]{:T(128)S(6)} %div.161, f32[]{:T(128)S(6)} %add.466, f32[16,768]{1,0:T(8,128)S(1)} %stack.85), channel_id=1, replica_groups=mesh['dp'=16,'head'=2] {'dp','head'}, use_global_device_ids=true, to_apply=%region_26.27 | all-reduce | flops 12290 | bytes 98320 | tf_op jit(solution)/shard_map/psum | solution.py:352
  1920.5 4.4 multiply_add_fusion.1
  (683 shorter events, 380.3 us)
Async XLA Ops:
  8.0 107.4 %all-gather.11.cloned.1.call-start = ((), (), s32[]{:S(2)}) async-start(), calls=%async_computation.8 | async-start | bytes 7520256 | tf_op jit(solution)/shard_map/all_gather | solution.py:255
  10.2 132.0 %all-gather.9.cloned.1.call-start = ((), (), s32[]{:S(2)}) async-start(), calls=%async_computation.7 | async-start | bytes 4718592 | tf_op jit(solution)/shard_map/all_gather | solution.py:131
  12.9 305.0 %copy-start.96 = (f32[768]{0:T(1024)}, f32[768]{0:T(1024)S(1)}, u32[]{:S(2)}) copy-start(f32[768]{0:T(1024)S(1)} %get-tuple-element.572) | copy-start | bytes 9220
  12.9 305.0 %copy-start.140 = (f32[768]{0:T(1024)}, f32[768]{0:T(1024)S(1)}, u32[]{:S(2)}) copy-start(f32[768]{0:T(1024)S(1)} %get-tuple-element.571) | copy-start | bytes 9220
  12.9 399.8 %copy-start.87 = (f32[768]{0:T(1024)}, f32[768]{0:T(1024)S(1)}, u32[]{:S(2)}) copy-start(f32[768]{0:T(1024)S(1)} %get-tuple-element.569) | copy-start | bytes 9220
  15.4 228.3 %copy-start = (f32[1024,768]{0,1:T(8,128)}, f32[1024,768]{0,1:T(8,128)S(1)}, u32[]{:S(2)}) copy-start(f32[1024,768]{0,1:T(8,128)S(1)} %get-tuple-element.712) | copy-start | bytes 9437188
  18.4 210.5 %all-gather.13.cloned.1.call-start = ((), (), s32[]{:S(2)}) async-start(), calls=%async_computation.9 | async-start | bytes 1253376 | tf_op jit(solution)/shard_map/all_gather | solution.py:256
  19.2 224.5 %reduce-scatter.8.cloned.1.call-start = ((), (), s32[]{:S(2)}) async-start(), calls=%async_computation.10 | async-start | bytes 4718592 | tf_op jit(solution)/shard_map/reduce_scatter | solution.py:144
  234.0 83.9 %all-gather.15.cloned.1.call-start = ((), (), s32[]{:S(2)}) async-start(), calls=%async_computation.11 | async-start | bytes 9732096 | tf_op jit(solution)/shard_map/all_gather | solution.py:259
  235.9 165.4 %all-gather.17.cloned.1.call-start = ((), (), s32[]{:S(2)}) async-start(), calls=%async_computation.12 | async-start | bytes 9732096 | tf_op jit(solution)/shard_map/all_gather | solution.py:260
  237.8 187.8 %all-gather.19.cloned.1.call-start = ((), (), s32[]{:S(2)}) async-start(), calls=%async_computation.13 | async-start | bytes 4718592 | tf_op jit(solution)/shard_map/all_gather | solution.py:131
  245.6 83.7 %copy-start.89 = (f32[1024]{0:T(1024)}, f32[1024]{0:T(1024)S(1)}, u32[]{:S(2)}) copy-start(f32[1024]{0:T(1024)S(1)} %broadcast_multiply_fusion.2) | copy-start | bytes 12292
  247.6 81.6 %copy-start.112 = (f32[1024]{0:T(1024)}, f32[1024]{0:T(1024)S(1)}, u32[]{:S(2)}) copy-start(f32[1024]{0:T(1024)S(1)} %multiply_reduce_fusion.9) | copy-start | bytes 12292
  247.7 81.6 %copy-start.107 = (f32[1024]{0:T(1024)}, f32[1024]{0:T(1024)S(1)}, u32[]{:S(2)}) copy-start(f32[1024]{0:T(1024)S(1)} %fusion.175) | copy-start | bytes 12292
  412.3 145.7 %copy-start.2 = (f32[1024,768]{0,1:T(8,128)}, f32[1024,768]{0,1:T(8,128)S(1)}, u32[]{:S(2)}) copy-start(f32[1024,768]{0,1:T(8,128)S(1)} %get-tuple-element.714) | copy-start | bytes 9437188
  414.8 143.2 %reduce-scatter.10.cloned.1.call-start = ((), (), s32[]{:S(2)}) async-start(), calls=%async_computation.14 | async-start | bytes 4718592 | tf_op jit(solution)/shard_map/reduce_scatter | solution.py:144
  515.6 42.4 %copy-start.124 = (f32[768]{0:T(1024)S(1)}, f32[768]{0:T(1024)}, u32[]{:S(2)}) copy-start(f32[768]{0:T(1024)} %get-tuple-element.567) | copy-start | bytes 9220
  515.7 122.7 %all-gather.21.cloned.1.call-start = ((), (), s32[]{:S(2)}) async-start(), calls=%async_computation.15 | async-start | bytes 4718592 | tf_op jit(solution)/shard_map/all_gather | solution.py:191
  559.9 11.8 copy-start.9
  559.9 61.9 %copy-start.99 = (f32[1024]{0:T(1024)}, f32[1024]{0:T(1024)S(1)}, u32[]{:S(2)}) copy-start(f32[1024]{0:T(1024)S(1)} %broadcast_multiply_fusion) | copy-start | bytes 12292
  560.3 61.5 %copy-start.118 = (f32[1024]{0:T(1024)}, f32[1024]{0:T(1024)S(1)}, u32[]{:S(2)}) copy-start(f32[1024]{0:T(1024)S(1)} %fusion.177) | copy-start | bytes 12292
  560.7 11.0 copy-start.144
  571.7 10.9 copy-start.24
  571.7 10.9 copy-start.79
  571.7 10.9 copy-start.105
  582.4 7.7 copy-start.101
  582.6 7.5 copy-start.122
  586.4 20.9 %slice-start.4 = ((s8[9437184]{0:T(1024)(128)(4,1)}), s8[4194304]{0:T(1024)(128)(4,1)S(1)}, s32[]{:S(2)}) async-start(s8[9437184]{0:T(1024)(128)(4,1)} %bitcast.461), calls=%async_computation.28 | async-start | bytes 8388608
  591.4 15.8 copy-start.27
  591.4 15.8 slice-start.5
  591.5 15.8 slice-start.6
  607.3 7.3 copy-start.157
  624.5 13.9 copy-start.153
  626.1 130.9 %reduce-scatter.12.cloned.1.call-start = ((), (), s32[]{:S(2)}) async-start(), calls=%async_computation.16 | async-start | bytes 4718592 | tf_op jit(solution)/shard_map/reduce_scatter | solution.py:196
  739.1 18.0 copy-start.82
  739.1 18.0 copy-start.88
  744.8 12.3 copy-start.3
  744.8 15.4 copy-start.115
  744.8 15.4 copy-start.95
  744.8 73.8 %all-gather.23.cloned.1.call-start = ((), (), s32[]{:S(2)}) async-start(), calls=%async_computation.17 | async-start | bytes 4718592 | tf_op jit(solution)/shard_map/all_gather | solution.py:191
  762.4 20.2 %slice-start.7 = ((s8[9437184]{0:T(1024)(128)(4,1)}), s8[1048576]{0:T(1024)(128)(4,1)S(1)}, s32[]{:S(2)}) async-start(s8[9437184]{0:T(1024)(128)(4,1)} %bitcast.463), calls=%async_computation.31 | async-start | bytes 2097152
  765.1 17.5 copy-start.31
  765.1 17.5 slice-start.8
  765.1 17.5 slice-start.9
  803.6 14.9 copy-start.154
  805.0 173.5 %reduce-scatter.20.cloned.1.call-start = ((), (), s32[]{:S(2)}) async-start(), calls=%async_computation.21 | async-start | bytes 4718592 | tf_op jit(solution)/shard_map/reduce_scatter | solution.py:196
  926.6 148.0 %reduce-scatter.14.cloned.1.call-start = ((), (), s32[]{:S(2)}) async-start(), calls=%async_computation.18 | async-start | bytes 2506752 | tf_op jit(solution)/shard_map/reduce_scatter | solution.py:342
  934.7 371.7 %all-reduce.12.cloned.1.call-start = ((), (), s32[]{:S(2)}) async-start(), calls=%async_computation.22 | async-start | bytes 14155776
  936.1 6.8 copy-start.57
  936.1 6.8 copy-start.59
  936.1 6.8 copy-start.61
  936.1 6.8 copy-start.150
  964.0 482.3 %all-reduce.14.cloned.1.call-start = ((), (), s32[]{:S(2)}) async-start(), calls=%async_computation.23 | async-start | bytes 3932160 | tf_op jit(solution)/shard_map/psum | solution.py:352
  967.8 10.7 copy-start.1
  967.8 10.7 copy-start.78
  967.8 10.7 copy-start.86
  986.2 670.4 %reduce-scatter.16.cloned.1.call-start = ((), (), s32[]{:S(2)}) async-start(), calls=%async_computation.19 | async-start | bytes 19464192 | tf_op jit(solution)/shard_map/reduce_scatter | solution.py:345
  1005.0 862.0 %reduce-scatter.18.cloned.1.call-start = ((), (), s32[]{:S(2)}) async-start(), calls=%async_computation.20 | async-start | bytes 19464192 | tf_op jit(solution)/shard_map/reduce_scatter | solution.py:346
  1006.1 11.1 copy-start.33
  1868.8 51.6 %copy-start.25 = (f32[768,512]{1,0:T(8,128)S(1)}, f32[768,512]{1,0:T(8,128)}, u32[]{:S(2)}) copy-start(f32[768,512]{1,0:T(8,128)} %param.59) | copy-start | bytes 4718596
  1868.8 51.6 %copy-start.41 = (f32[768,512]{1,0:T(8,128)S(1)}, f32[768,512]{1,0:T(8,128)}, u32[]{:S(2)}) copy-start(f32[768,512]{1,0:T(8,128)} %get-tuple-element.658) | copy-start | bytes 4718596
  1915.0 5.4 copy-start.64
  1920.4 5.2 copy-start.62
  1920.4 5.2 copy-start.63
  (139 other events, 343.7 us)
Sparse Core Ops, SparseCore 0:
  12.1 103.3 all-gather.10
  117.6 10.4 all-gather.8
  131.4 57.1 all-gather.12
  234.1 9.4 reduce-scatter.7
  414.9 10.6 all-gather.18
  515.8 12.1 reduce-scatter.9
  626.3 12.0 all-gather.20
  744.9 12.1 reduce-scatter.11
  805.1 13.3 all-gather.22
  926.8 12.1 reduce-scatter.19
  943.8 130.7 reduce-scatter.13
  1080.7 225.5 all-reduce.11
  1313.1 133.0 all-reduce.13
  1452.5 203.9 reduce-scatter.15
  1662.8 204.1 reduce-scatter.17
Sparse Core Ops, SparseCore 1:
  238.0 79.9 all-gather.14
  321.3 79.9 all-gather.16
where the time goes:
time: 1950 us; the launch traced here: 1940 us
  waiting for transfers between devices  1110 us (57%)
  matrix products  347 us (18%)
  local copies, waits for them, and re-layouts  198 us (10%)
  other arithmetic  147 us (8%)
  blocking collectives  81.3 us (4%)
  loops' own time  31.7 us (2%)
  between operations  26.3 us (1%)
    unnamed x18, waiting for transfers between devices  230 us
    reduce_scatter x1, waiting for transfers between devices, shards(): lax.psum_scatter(grad_shrink, ('dp', 'head'), scatter_dimension=1, tiled=...  208 us
    reduce_scatter x1, waiting for transfers between devices, shards(): lax.psum_scatter(grad_grow, ('dp', 'head'), scatter_dimension=1, tiled=True)  208 us
    psum x1, waiting for transfers between devices, shards(): lax.psum((grad_emb, grad_vec, grad_head, loss_part, shard_square), ('dp',...  136 us
    all_gather x1, waiting for transfers between devices, shards(): lax.all_gather(w_qkv.astype(low_type), 'dp', axis=1, tiled=True)  96.1 us
    all_gather x1, waiting for transfers between devices, shards(): lax.all_gather(w_down.astype(low_type), ('dp', 'head'), axis=1, tiled=True)  72 us
    all_gather x1, waiting for transfers between devices, shards(): lax.all_gather(w_up.astype(low_type), ('dp', 'head'), axis=1, tiled=True)  70.3 us
    dot_general x9, matrix products, matmul_nt(): lax.dot_general(first_op, second_op, (((1,), (1,)), ((), ())), preferred_...  69.4 us
  transfers between devices with their start and end apart: 17, of which 13 were waited for; matrix products, arithmetic and copies ran while one was open for 13% of the time, Pallas kernels for 0%

commit v1 on v0

v1 whole, which is shorter than its diff:
```python
import functools
import jax
import jax.numpy as jnp
from jax import lax
from jax.sharding import PartitionSpec as P
from jax.experimental import pallas as pl
from jax.experimental.pallas import tpu as pltpu

MESH = pl.DeviceIdType.MESH
ORDERS = ("zxy", "xzy", "yzx")
PIECES = len(ORDERS)


class Place:
    def __init__(self):
        self.chip = lax.axis_index("dp")
        self.core = lax.axis_index("head")
        self.x = self.chip % 2
        self.y = (self.chip // 2) % 2
        self.z = self.chip // 4
        z = self.z
        self.z_from = (z, 1 + z % 2, (12 - 2 * z) % 5, 3 - 3 * (z // 2))

    def peer(self, way):
        step = {
            "x": 1 - 2 * self.x,
            "y": 2 - 4 * self.y,
            "u": 4,
            "d": -4,
            "c": 0,
        }[way]
        core = 1 - self.core if way == "c" else self.core
        return (self.chip + step, core)

    def block(self, k, ax, ay):
        sx = self.x if ax == 0 else 1 - self.x
        sy = self.y if ay == 0 else 1 - self.y
        return self.z_from[k] * 4 + sy * 2 + sx


def meet(place):
    barrier = pltpu.get_barrier_semaphore()
    for way in "xyc":
        pl.semaphore_signal(barrier, inc=1, device_id=place.peer(way), device_id_type=MESH)

    @pl.when(place.z < 3)
    def _():
        pl.semaphore_signal(barrier, inc=1, device_id=place.peer("u"), device_id_type=MESH)

    @pl.when(place.z > 0)
    def _():
        pl.semaphore_signal(barrier, inc=1, device_id=place.peer("d"), device_id_type=MESH)

    ends = place.z * (3 - place.z)
    pl.semaphore_wait(barrier, 4 + ends // 2)


def at_block(ref, chip, core, piece, by_core):
    return ref.at[core, chip, piece] if by_core else ref.at[chip, core, piece]


def gather_kernel(by_core, *refs):
    n = len(by_core)
    ins, outs = refs[:n], refs[n : 2 * n]
    local_sem, recv, core_recv, send, core_send = refs[2 * n :]
    place = Place()
    me = place.chip
    meet(place)

    def slot(a, c, chip, core=None):
        return at_block(outs[a], chip, place.core if core is None else core, c, by_core[a])

    def copy(a, c, chip, way, src, sems):
        return pltpu.make_async_remote_copy(
            src_ref=src, dst_ref=slot(a, c, chip), send_sem=sems[0], recv_sem=sems[1],
            device_id=place.peer(way), device_id_type=MESH)

    ways = {"x": 0, "y": 1, "u": 2, "d": 3}

    def forward(a, c, order, k, ax, ay):
        chip = place.block(k, ax, ay)
        rel = {"x": ax, "y": ay, "z": k}
        last = max([i for i in range(3) if rel[order[i]] != 0], default=-1)
        src = ins[a].at[c] if last < 0 else slot(a, c, chip)
        for i in range(max(last, 0), 3):
            dim = order[i]
            if dim == "z":
                sz = place.z_from[k]

                @pl.when((sz <= place.z) & (place.z < 3))
                def _():
                    copy(a, c, chip, "u", src, (send.at[a, c, 2], recv.at[a, c, chip])).start()

                @pl.when((sz >= place.z) & (place.z > 0))
                def _():
                    copy(a, c, chip, "d", src, (send.at[a, c, 3], recv.at[a, c, chip])).start()
            elif rel[dim] == 0:
                w = dim
                copy(a, c, chip, w, src, (send.at[a, c, ways[w]], recv.at[a, c, chip])).start()
        copy(a, c, chip, "c", src, (core_send.at[a], core_recv.at[a])).start()

    entries = sorted(
        [(k, ax, ay) for k in range(4) for ax in range(2) for ay in range(2)],
        key=lambda e: (e[0] * 1.0 + e[1] + e[2]))
    for k, ax, ay in entries:
        for a in range(n):
            for c, order in enumerate(ORDERS):
                chip = place.block(k, ax, ay)
                if (k, ax, ay) != (0, 0, 0):
                    copy(a, c, chip, "x", slot(a, c, chip), (send.at[a, c, 0], recv.at[a, c, chip])).wait_recv()
                forward(a, c, order, k, ax, ay)
    own = []
    for a in range(n):
        for c in range(PIECES):
            cp = pltpu.make_async_copy(ins[a].at[c], slot(a, c, me), local_sem.at[a, c])
            cp.start()
            own.append(cp)
    for cp in own:
        cp.wait()
    for a in range(n):
        whole = outs[a].at[0] if by_core[a] else outs[a].at[:, 0]
        pltpu.make_async_remote_copy(
            src_ref=whole, dst_ref=whole, send_sem=core_send.at[a], recv_sem=core_recv.at[a],
            device_id=place.peer("c"), device_id_type=MESH).wait()
        for c, order in enumerate(ORDERS):
            def drain(way, count):
                part = outs[a].at[0, pl.ds(0, count), c] if by_core[a] else outs[a].at[pl.ds(0, count), 0, c]
                pltpu.make_async_remote_copy(
                    src_ref=part, dst_ref=part, send_sem=send.at[a, c, ways[way]], recv_sem=recv.at[a, c, 0],
                    device_id=place.peer("c"), device_id_type=MESH).wait_send()
            size = {"x": 2, "y": 2, "z": 4}
            before = 1
            for dim in order:
                if dim == "z":
                    for zz in range(4):
                        @pl.when(place.z == zz)
                        def _(zz=zz, before=before):
                            if zz < 3:
                                drain("u", before * (zz + 1))
                            if zz > 0:
                                drain("d", before * (4 - zz))
                else:
                    drain(dim, before)
                before *= size[dim]


def all_gather_layer(arrays, by_core, collective_id):
    n = len(arrays)
    outs = tuple(
        jax.ShapeDtypeStruct(((2, 16) if bc else (16, 2)) + a.shape, a.dtype)
        for a, bc in zip(arrays, by_core))
    sent = sum(a.size * 2 for a in arrays) * 31
    return pl.pallas_call(
        functools.partial(gather_kernel, by_core),
        out_shape=outs,
        in_specs=[pl.BlockSpec(memory_space=pltpu.VMEM)] * n,
        out_specs=[pl.BlockSpec(memory_space=pl.ANY)] * n,
        scratch_shapes=[
            pltpu.SemaphoreType.DMA((n, PIECES)),
            pltpu.SemaphoreType.DMA((n, PIECES, 16)),
            pltpu.SemaphoreType.DMA((n,)),
            pltpu.SemaphoreType.DMA((n, PIECES, 4)),
            pltpu.SemaphoreType.DMA((n,)),
        ],
        compiler_params=pltpu.CompilerParams(
            collective_id=collective_id, has_side_effects=True),
        cost_estimate=pl.CostEstimate(flops=0, bytes_accessed=2 * sent, transcendentals=0),
    )(*arrays)


def reduce_kernel(by_core, *refs):
    n = len(by_core)
    ins, outs = refs[:n], refs[n : 2 * n]
    scr = refs[2 * n :]
    mine, other = scr[:n], scr[n : 2 * n]
    got = {"x": scr[2 * n : 3 * n], "y": scr[3 * n : 4 * n], "u": scr[4 * n : 5 * n], "d": scr[5 * n : 6 * n]}
    load_sem, core_recv, core_send, recv, send = scr[6 * n :]
    ways = {"x": 0, "y": 1, "u": 2, "d": 3}
    place = Place()
    meet(place)
    f32 = jnp.float32

    def chip_of(sx, sy, sz):
        return sz * 4 + sy * 2 + sx

    def load(a):
        src = ins[a].at[place.core] if by_core[a] else ins[a].at[:, place.core]
        return pltpu.make_async_copy(src, mine[a], load_sem.at[a])

    def to_core(a, c, chip):
        src = at_block(ins[a], chip, 1 - place.core, c, by_core[a])
        return pltpu.make_async_remote_copy(
            src_ref=src, dst_ref=other[a].at[chip, c], send_sem=core_send.at[a, c], recv_sem=core_recv.at[a, c, chip],
            device_id=place.peer("c"), device_id_type=MESH)

    def hop(a, c, chip, way):
        return pltpu.make_async_remote_copy(
            src_ref=mine[a].at[chip, c], dst_ref=got[way][a].at[chip, c],
            send_sem=send.at[a, c, ways[way]], recv_sem=recv.at[a, c, ways[way], chip],
            device_id=place.peer(way), device_id_type=MESH)

    def add(a, c, chip, extra):
        mine[a][chip, c] = (mine[a][chip, c].astype(f32) + extra[a][chip, c].astype(f32)).astype(jnp.bfloat16)

    for a in range(n):
        load(a).start()
    work = [(a, c, order) for a in range(n) for c, order in enumerate(ORDERS)]

    def split(order, i):
        dim = order[2]
        far = 1 - i // 8
        j = i % 8
        sz, w = j // 2, j % 2
        if dim == "x":
            sx = place.x + far * (1 - 2 * place.x)
            return chip_of(sx, w, sz)
        sy = place.y + far * (1 - 2 * place.y)
        return chip_of(w, sy, sz)

    for half in range(2):
        for a, c, order in work:
            def start_core(i, carry):
                to_core(a, c, split(order, i)).start()
                return carry
            lax.fori_loop(8 * half, 8 * half + 8, start_core, 0)
    for a in range(n):
        load(a).wait()
    for half in range(2):
        for a, c, order in work:
            def fold(i, carry):
                chip = split(order, i)
                to_core(a, c, chip).wait_recv()
                add(a, c, chip, other)
                if half == 0:
                    hop(a, c, chip, order[2]).start()
                return carry
            lax.fori_loop(8 * half, 8 * half + 8, fold, 0)

    def firsts_of(order):
        if order[0] == "z":
            return [(place.x, place.y)]
        if order[0] == "x":
            return [(1 - place.x, place.y), (place.x, place.y)]
        return [(place.x, 1 - place.y), (place.x, place.y)]

    for a, c, order in work:
        dim, nxt = order[2], order[1]
        for far in ((1, 0) if nxt != "z" else (None,)):
            def take(i, carry):
                if far is None:
                    w, sz = i % 2, i // 2
                else:
                    sz = i
                    m = place.x if nxt == "x" else place.y
                    w = m + far * (1 - 2 * m)
                chip = chip_of(place.x, w, sz) if dim == "x" else chip_of(w, place.y, sz)
                hop(a, c, chip, dim).wait_recv()
                add(a, c, chip, got[dim])
                if far == 1:
                    hop(a, c, chip, nxt).start()
                return carry
            lax.fori_loop(0, 8 if far is None else 4, take, 0)
    for a, c, order in work:
        if order[0] == "z":
            def take(i, carry):
                chip = chip_of(place.x, place.y, i)
                hop(a, c, chip, order[1]).wait_recv()
                add(a, c, chip, got[order[1]])
                return carry
            lax.fori_loop(0, 4, take, 0)
    for j in range(3):
        for way, target, active, inner in (
            ("u", 3 - j, place.z < 3 - j, place.z > 0),
            ("d", j, place.z > j, place.z < 3),
        ):
            @pl.when(active)
            def _():
                for a, c, order in work:
                    for sx, sy in firsts_of(order):
                        chip = chip_of(sx, sy, target)

                        @pl.when(inner)
                        def _():
                            hop(a, c, chip, way).wait_recv()
                            add(a, c, chip, got[way])
                        hop(a, c, chip, way).start()
    for a, c, order in work:
        for n_first, (sx, sy) in enumerate(firsts_of(order)):
            chip = chip_of(sx, sy, place.z)

            @pl.when(place.z > 0)
            def _():
                hop(a, c, chip, "u").wait_recv()
                add(a, c, chip, got["u"])

            @pl.when(place.z < 3)
            def _():
                hop(a, c, chip, "d").wait_recv()
                add(a, c, chip, got["d"])
            if order[0] != "z" and n_first == 0:
                hop(a, c, chip, order[0]).start()
    for a, c, order in work:
        if order[0] != "z":
            hop(a, c, place.chip, order[0]).wait_recv()
            add(a, c, place.chip, got[order[0]])
        outs[a][c] = mine[a][place.chip, c].astype(f32)
    for a, c, order in work:
        def drain(sem, count):
            part = other[a].at[pl.ds(0, count), c]
            pltpu.make_async_remote_copy(
                src_ref=part, dst_ref=part, send_sem=sem, recv_sem=recv.at[a, c, 0, 0],
                device_id=place.peer("c"), device_id_type=MESH).wait_send()
        drain(core_send.at[a, c], 16)
        left = 16
        for stage in (2, 1, 0):
            dim = order[stage]
            if dim == "z":
                q = left // 4
                for zz in range(4):
                    @pl.when(place.z == zz)
                    def _(zz=zz, q=q):
                        if zz < 3:
                            drain(send.at[a, c, 2], q * (3 - zz))
                        if zz > 0:
                            drain(send.at[a, c, 3], q * zz)
                left = q
            else:
                left //= 2
                drain(send.at[a, c, ways[dim]], left)


def reduce_scatter_layer(arrays, by_core, collective_id):
    n = len(arrays)
    shapes = [a.shape[2:] for a in arrays]
    full = [pltpu.VMEM((16,) + s, jnp.bfloat16) for s in shapes]
    sent = sum(a.size for a in arrays)
    return pl.pallas_call(
        functools.partial(reduce_kernel, by_core),
        out_shape=tuple(jax.ShapeDtypeStruct(s, jnp.float32) for s in shapes),
        in_specs=[pl.BlockSpec(memory_space=pl.ANY)] * n,
        out_specs=[pl.BlockSpec(memory_space=pltpu.VMEM)] * n,
        scratch_shapes=full * 6 + [
            pltpu.SemaphoreType.DMA((n,)),
            pltpu.SemaphoreType.DMA((n, PIECES, 16)),
            pltpu.SemaphoreType.DMA((n, PIECES)),
            pltpu.SemaphoreType.DMA((n, PIECES, 4, 16)),
            pltpu.SemaphoreType.DMA((n, PIECES, 4)),
        ],
        compiler_params=pltpu.CompilerParams(
            collective_id=collective_id, has_side_effects=True, vmem_limit_bytes=64 * 1024 * 1024 - 65536),
        cost_estimate=pl.CostEstimate(flops=sent, bytes_accessed=2 * sent, transcendentals=0),
    )(*arrays)


HD = 64
CTX = 768

eps_norm = 1e-05
clip_at = 0.01
rate = 3000.0
moment = 0.9
keep_avg = 0.9
decay_wd = 1e-05
low_type = jnp.bfloat16
wide_type = jnp.float32


def layer_norm(values, gain_row, shift_row):
    center = values - jnp.mean(values, -1, keepdims=True)
    spread = jnp.mean(center * center, -1, keepdims=True)
    return center * lax.rsqrt(spread + eps_norm) * gain_row + shift_row


def norm_back(values, gain_row, shift_row, upstream):
    _, pull = jax.vjp(layer_norm, values, gain_row, shift_row)
    return pull(upstream)


def gelu_back(values, upstream):
    _, pull = jax.vjp(jax.nn.gelu, values)
    return pull(upstream)[0]


def matmul(first_op, second_op):
    return jnp.dot(first_op, second_op, preferred_element_type=wide_type)


def contract(first_op, second_op, first_dim, second_dim):
    return lax.dot_general(
        first_op, second_op, (((first_dim,), (second_dim,)), ((), ())), preferred_element_type=wide_type
    )


def matmul_tn(first_op, second_op):
    return contract(first_op, second_op, 0, 0)


def matmul_nt(first_op, second_op):
    return contract(first_op, second_op, 1, 1)


def head_lanes(shape, head):
    lane = lax.broadcasted_iota(jnp.int32, shape, 1)
    mine = (lane < HD) if head == 0 else (lane >= HD)
    return mine, lane == (HD if head == 0 else 0)


def attend_kernel(q_ref, k_ref, v_ref, bias_ref, out_ref, lse_ref):
    q_block = q_ref[0] * jnp.asarray(HD ** -0.5, low_type)
    k_block, v_block, bias = k_ref[0], v_ref[0], bias_ref[...]
    v_turned = v_block.T
    parts = []
    for head in range(2):
        q_mine, q_one = head_lanes(q_block.shape, head)
        k_mine, _ = head_lanes(k_block.shape, head)
        one = jnp.where(q_one, jnp.ones_like(q_block), jnp.zeros_like(q_block))
        score = matmul_nt(jnp.where(k_mine, k_block, bias), jnp.where(q_mine, q_block, one))
        peak = jnp.max(score, 0, keepdims=True)
        lifted = jnp.exp(score - peak)
        total = jnp.sum(lifted, 0, keepdims=True)
        mixed = matmul(v_turned[head * HD : (head + 1) * HD], lifted.astype(low_type))
        parts.append(mixed / total)
        lse_ref[0, head : head + 1, :] = peak + jnp.log(total)
    out_ref[...] = jnp.concatenate(parts, 0).T.astype(low_type)


def attend(queries, keys_values, bias):
    groups, rows, width = queries.shape
    pairs = width // 128
    block = min(256, rows)
    grid = (groups * pairs, rows // block)
    return pl.pallas_call(
        attend_kernel,
        grid=grid,
        in_specs=[
            pl.BlockSpec((1, block, 128), lambda p, i: (p // pairs, i, p % pairs)),
            pl.BlockSpec((1, CTX, 128), lambda p, i: (p // pairs, 0, p % pairs)),
            pl.BlockSpec((1, CTX, 128), lambda p, i: (p // pairs, 0, pairs + p % pairs)),
            pl.BlockSpec((CTX, 128), lambda p, i: (0, 0)),
        ],
        out_specs=[
            pl.BlockSpec((block, 128), lambda p, i: (i, p)),
            pl.BlockSpec((1, 2, block), lambda p, i: (p, 0, i)),
        ],
        out_shape=(
            jax.ShapeDtypeStruct((rows, groups * width), low_type),
            jax.ShapeDtypeStruct((groups * pairs, 2, rows), wide_type),
        ),
        cost_estimate=pl.CostEstimate(
            flops=4 * rows * CTX * groups * width, bytes_accessed=8 * rows * groups * width,
            transcendentals=rows * CTX * groups * width // HD),
    )(queries, keys_values, keys_values, bias)


def attend_back_kernel(q_ref, k_ref, v_ref, bias_ref, g_ref, o_ref, lse_ref, gq_ref, gk_ref, gv_ref, k_sum, v_sum):
    step = pl.program_id(1)

    @pl.when(step == 0)
    def _():
        k_sum[...] = jnp.zeros_like(k_sum)
        v_sum[...] = jnp.zeros_like(v_sum)

    scale = HD ** -0.5
    q_block = q_ref[0] * jnp.asarray(scale, low_type)
    k_block, v_block, bias = k_ref[0], v_ref[0], bias_ref[...]
    g_block = g_ref[...]
    k_turned = k_block.T
    both = (g_block.astype(wide_type) * o_ref[...].astype(wide_type)).T
    parts = []
    for head in range(2):
        q_mine, q_one = head_lanes(q_block.shape, head)
        k_mine, _ = head_lanes(k_block.shape, head)
        nothing = jnp.zeros_like(q_block)
        one = jnp.where(q_one, jnp.ones_like(q_block), nothing)
        score = matmul_nt(jnp.where(k_mine, k_block, bias), jnp.where(q_mine, q_block, one))
        prob = jnp.exp(score - lse_ref[0, head : head + 1, :])
        g_mine = jnp.where(q_mine, g_block, nothing)
        grad_prob = matmul_nt(v_block, g_mine)
        inner = jnp.sum(both[head * HD : (head + 1) * HD], 0, keepdims=True)
        grad_score = (prob * (grad_prob - inner)).astype(low_type)
        v_sum[...] += matmul(prob.astype(low_type), g_mine)
        k_sum[...] += matmul(grad_score, jnp.where(q_mine, q_block, nothing))
        parts.append(matmul(k_turned[head * HD : (head + 1) * HD], grad_score) * scale)
    gq_ref[0] = jnp.concatenate(parts, 0).T.astype(low_type)

    @pl.when(step == pl.num_programs(1) - 1)
    def _():
        gk_ref[0] = k_sum[...].astype(low_type)
        gv_ref[0] = v_sum[...].astype(low_type)


def attend_back(queries, keys_values, bias, grad_mixed, mixed, lse):
    groups, rows, width = queries.shape
    pairs = width // 128
    block = min(256, rows)
    grid = (groups * pairs, rows // block)
    row_spec = pl.BlockSpec((block, 128), lambda p, i: (i, p))
    key_out = pl.BlockSpec((1, CTX, 128), lambda p, i: (p // pairs, 0, p % pairs))
    return pl.pallas_call(
        attend_back_kernel,
        grid=grid,
        in_specs=[
            pl.BlockSpec((1, block, 128), lambda p, i: (p // pairs, i, p % pairs)),
            pl.BlockSpec((1, CTX, 128), lambda p, i: (p // pairs, 0, p % pairs)),
            pl.BlockSpec((1, CTX, 128), lambda p, i: (p // pairs, 0, pairs + p % pairs)),
            pl.BlockSpec((CTX, 128), lambda p, i: (0, 0)),
            row_spec,
            row_spec,
            pl.BlockSpec((1, 2, block), lambda p, i: (p, 0, i)),
        ],
        out_specs=[
            pl.BlockSpec((1, block, 128), lambda p, i: (p // pairs, i, p % pairs)),
            key_out,
            key_out,
        ],
        out_shape=(
            jax.ShapeDtypeStruct(queries.shape, low_type),
            jax.ShapeDtypeStruct((groups, CTX, width), low_type),
            jax.ShapeDtypeStruct((groups, CTX, width), low_type),
        ),
        scratch_shapes=[pltpu.VMEM((CTX, 128), wide_type)] * 2,
        cost_estimate=pl.CostEstimate(
            flops=10 * rows * CTX * groups * width, bytes_accessed=16 * rows * groups * width,
            transcendentals=rows * CTX * groups * width // HD),
    )(queries, keys_values, keys_values, bias, grad_mixed, mixed, lse)


def grouped(rows, weight):
    return jnp.einsum("rd,gdc->grc", rows, weight, preferred_element_type=wide_type)


def layer_forward(residual, first, vec_rows, weights, bias):
    w_joined, w_mix, w_grow, w_shrink = weights
    width = w_joined.shape[2] // 3
    normed = layer_norm(residual, vec_rows[0], vec_rows[1]).astype(low_type)
    queries = grouped(normed[first:], w_joined[:, :, :width]).astype(low_type)
    keys_values = grouped(normed[:CTX], w_joined[:, :, width:]).astype(low_type)
    mixed, lse = attend(queries, keys_values, bias)
    middle = residual[first:] + matmul(mixed, w_mix) + vec_rows[4]
    normed_mlp = layer_norm(middle, vec_rows[2], vec_rows[3]).astype(low_type)
    hidden = matmul(normed_mlp, w_grow)
    active = jax.nn.gelu(hidden).astype(low_type)
    output = middle + matmul(active, w_shrink) + vec_rows[5]
    return output, (residual, normed, queries, keys_values, mixed, lse, middle, normed_mlp, hidden, active)


def layer_backward(upstream, kept, first, vec_rows, weights, bias):
    w_joined, w_mix, w_grow, w_shrink = weights
    width = w_joined.shape[2] // 3
    residual, normed, queries, keys_values, mixed, lse, middle, normed_mlp, hidden, active = kept
    down_low = upstream.astype(low_type)
    grad_shrink = matmul_tn(active, down_low).astype(low_type)
    grad_hidden = gelu_back(hidden, matmul_nt(down_low, w_shrink)).astype(low_type)
    grad_grow = matmul_tn(normed_mlp, grad_hidden).astype(low_type)
    grad_middle, gain_mlp, shift_mlp = norm_back(
        middle, vec_rows[2], vec_rows[3], matmul_nt(grad_hidden, w_grow))
    grad_middle = grad_middle + upstream
    mix_low = grad_middle.astype(low_type)
    grad_mix = matmul_tn(mixed, mix_low).astype(low_type)
    grad_mixed = matmul_nt(mix_low, w_mix).astype(low_type)
    grad_q, grad_k, grad_v = attend_back(queries, keys_values, bias, grad_mixed, mixed, lse)

    def weight_grad(rows, grads):
        return jnp.einsum("rd,grc->gdc", rows, grads, preferred_element_type=wide_type).astype(low_type)

    def row_grad(grads, part):
        return jnp.einsum(
            "grc,gdc->rd", grads, w_joined[:, :, part * width : (part + 1) * width], preferred_element_type=wide_type)

    grad_joined = jnp.concatenate(
        [weight_grad(normed[first:], grad_q), weight_grad(normed[:CTX], grad_k), weight_grad(normed[:CTX], grad_v)], 2)
    from_q = row_grad(grad_q, 0)
    from_kv = row_grad(grad_k, 1) + row_grad(grad_v, 2)
    rows = residual.shape[0]
    below = jnp.zeros((first, from_q.shape[1]), wide_type)
    tail = jnp.zeros((rows - CTX, from_q.shape[1]), wide_type)
    grad_normed = jnp.concatenate([below, from_q], 0) + jnp.concatenate([from_kv, tail], 0)
    grad_input, gain_attn, shift_attn = norm_back(residual, vec_rows[0], vec_rows[1], grad_normed)
    vec_grads = [gain_attn, shift_attn, gain_mlp, shift_mlp, jnp.sum(grad_middle, 0), jnp.sum(upstream, 0)]
    grad_out = grad_input + jnp.concatenate([below, grad_middle], 0)
    return grad_out, (grad_joined, grad_mix, grad_grow, grad_shrink), vec_grads


def update(weight, moment_old, average, grad_in, scale):
    applied = grad_in * scale + decay_wd * weight
    moment_new = moment * moment_old + applied
    weight_new = weight - rate * (applied + moment * moment_new)
    return (weight_new, moment_new, keep_avg * average + (1.0 - keep_avg) * weight_new)


BY_CORE = (True, True, False, False)


def gather_weights(shard_list, direct, number):
    if direct:
        pieces = [s.reshape((PIECES, s.shape[0] // PIECES, s.shape[1])) for s in shard_list]
        return all_gather_layer(pieces, BY_CORE, number)
    out = []
    for shard, by_core in zip(shard_list, BY_CORE):
        whole = lax.all_gather(shard, "dp", axis=0)
        out.append(lax.all_gather(whole, "head", axis=0 if by_core else 1))
    return out


def scatter_grads(grads, by_core_list, rows_list, direct, number):
    chips, cores = lax.axis_size("dp"), lax.axis_size("head")
    if direct:
        pieces = []
        for grad, by_core, rows in zip(grads, by_core_list, rows_list):
            lead = (cores, chips) if by_core else (chips, cores)
            pieces.append(grad.reshape(lead + (PIECES, rows // PIECES, -1)))
        outs = reduce_scatter_layer(pieces, by_core_list, number)
        return [o.reshape((rows, -1)) for o, rows in zip(outs, rows_list)]
    outs = []
    for grad, by_core, rows in zip(grads, by_core_list, rows_list):
        lead = (cores, chips) if by_core else (chips, cores)
        grad = grad.reshape(lead + (rows, -1)).astype(wide_type)
        half = lax.psum_scatter(grad, "head", scatter_dimension=0 if by_core else 1)
        outs.append(lax.psum_scatter(half, "dp", scatter_dimension=0))
    return outs


def gather_small(arrays, direct, number):
    if direct:
        return all_gather_layer(arrays, (False,) * len(arrays), number)
    return [lax.all_gather(lax.all_gather(a, "dp", axis=0), "head", axis=1) for a in arrays]


def shards(
    rows_in, feat_mask, counts, ctx_vals, targets, query_mask,
    w_emb, m_emb, a_emb, vectors, m_vec, a_vec,
    w_qkv, m_qkv, a_qkv, w_out, m_out, a_out, w_up, m_up, a_up, w_down, m_down, a_down,
    w_head, m_head, a_head,
):
    chips, cores = lax.axis_size("dp"), lax.axis_size("head")
    direct = (chips, cores) == (16, 2)
    _, row_count, feat_count = rows_in.shape
    layer_total = w_qkv.shape[0]
    width = w_emb.shape[1]
    joined_rows = w_qkv.shape[1]
    kinds = w_qkv.shape[2] * w_qkv.shape[4]

    weights = []
    for at in range(layer_total):
        own = [
            w_qkv[at].reshape((joined_rows, kinds)).astype(low_type),
            w_out[at, 0].astype(low_type),
            w_up[at].astype(low_type),
            w_down[at].astype(low_type),
        ]
        qkv, out, up, down = gather_weights(own, direct, 1 + at)
        weights.append((
            qkv.reshape((cores, width, kinds)),
            out.reshape((width, width)),
            up.reshape((width, -1)),
            down.reshape((-1, width)),
        ))

    table = lax.axis_index("dp") * cores + lax.axis_index("head")
    count = lax.dynamic_slice_in_dim(counts, table, 1, 0)
    bias = jnp.where(jnp.arange(CTX) < count, 0.0, -1e30).astype(low_type)
    bias = jnp.broadcast_to(bias[:, None], (CTX, 128))
    masked = rows_in[0] * feat_mask[0][None, :].astype(low_type)
    leading = jnp.concatenate([ctx_vals[0], jnp.zeros((row_count - CTX,), wide_type)])[:, None]
    residual = matmul(masked, w_emb.astype(low_type)) + vectors[1] + leading * vectors[0]
    kept_all = []
    for at in range(layer_total):
        first = CTX if at == layer_total - 1 else 0
        residual, kept = layer_forward(residual, first, vectors[2 + 6 * at : 8 + 6 * at], weights[at], bias)
        kept_all.append(kept)

    head_low = w_head.astype(low_type)
    final_rows = layer_norm(residual, vectors[-2], vectors[-1]).astype(low_type)
    logits = matmul(final_rows, head_low)
    row_peak = jnp.max(logits, -1, keepdims=True)
    log_total = row_peak[:, 0] + jnp.log(jnp.sum(jnp.exp(logits - row_peak), -1))
    target_hit = (jnp.arange(logits.shape[1])[None, :] == targets[0][:, None]).astype(wide_type)
    picked = jnp.sum(logits * target_hit, -1)
    row_weight = query_mask[0].astype(wide_type)
    loss_part = jnp.sum((log_total - picked) * row_weight)
    grad_logits = ((jnp.exp(logits - log_total[:, None]) - target_hit) * row_weight[:, None]).astype(low_type)
    grad_head = matmul_tn(final_rows, grad_logits).astype(low_type)
    upstream, gain_final, shift_final = norm_back(
        residual, vectors[-2], vectors[-1], matmul_nt(grad_logits, head_low))

    rows_list = [joined_rows, w_out.shape[2], w_up.shape[1], w_down.shape[1]]
    parts = [None] * layer_total
    vec_grads = [None] * layer_total
    for at in reversed(range(layer_total)):
        first = CTX if at == layer_total - 1 else 0
        upstream, big, vec_grads[at] = layer_backward(
            upstream, kept_all[at], first, vectors[2 + 6 * at : 8 + 6 * at], weights[at], bias)
        if at > 0:
            parts[at] = scatter_grads(big, BY_CORE, rows_list, direct, 11 + at)
    grad_emb = matmul_tn(masked, upstream.astype(low_type))
    vec_list = [jnp.sum(upstream * leading, 0), jnp.sum(upstream, 0)]
    for at in range(layer_total):
        vec_list = vec_list + vec_grads[at]
    grad_vec = jnp.stack(vec_list + [gain_final, shift_final])

    devices = chips * cores
    n_emb = feat_count * width // (devices * 128)
    n_vec = -(-grad_vec.size // (devices * 128))
    emb_part = grad_emb.reshape((devices, n_emb, 128))
    vec_flat = jnp.pad(grad_vec.reshape(-1), (0, n_vec * devices * 128 - grad_vec.size))
    vec_part = vec_flat.reshape((devices, n_vec, 128))
    n_all = 48 if direct else n_emb + n_vec
    small = jnp.concatenate([emb_part, vec_part, jnp.zeros((devices, n_all - n_emb - n_vec, 128), wide_type)], 1)
    head_rows = width // devices
    sums = scatter_grads(
        list(big) + [grad_head, small.astype(low_type)], BY_CORE + (False, False),
        rows_list + [head_rows, n_all], direct, 11)
    parts[0] = sums[:4]
    head_sum, small_sum = sums[4], sums[5].reshape((n_all, 128))

    square = sum(jnp.sum(p * p) for ps in parts for p in ps)
    square = square + jnp.sum(head_sum * head_sum) + jnp.sum(small_sum * small_sum)
    scalars = jnp.stack([square, loss_part, jnp.sum(row_weight)])
    scalars = jnp.broadcast_to(scalars[:, None, None], (3, 8, 128))
    split = PIECES if direct else 1
    head_all, small_all, scalar_all = gather_small(
        [head_sum.reshape((split, head_rows // split, -1)), small_sum.reshape((split, n_all // split, 128)), scalars],
        direct, 10)
    totals = jnp.sum(scalar_all[..., 0, 0], (0, 1))
    pooled = totals[2]
    loss = totals[1] / pooled
    grad_norm = jnp.sqrt(totals[0]) / pooled
    scale = jnp.minimum(1.0, clip_at / grad_norm) / pooled
    grad_head = head_all.reshape(w_head.shape)
    small_all = small_all.reshape((devices, n_all, 128))
    grad_emb = small_all[:, :n_emb].reshape(w_emb.shape)
    grad_vec = small_all[:, n_emb : n_emb + n_vec].reshape(-1)[: vectors.size].reshape(vectors.shape)

    def big_update(weight, moment_old, average, kind):
        grad = jnp.stack([parts[at][kind].reshape(weight.shape[1:]) for at in range(layer_total)])
        return update(weight, moment_old, average, grad, scale)

    e_w, e_m, e_a = update(w_emb, m_emb, a_emb, grad_emb, scale)
    v_w, v_m, v_a = update(vectors, m_vec, a_vec, grad_vec, scale)
    q_w, q_m, q_a = big_update(w_qkv, m_qkv, a_qkv, 0)
    o_w, o_m, o_a = big_update(w_out, m_out, a_out, 1)
    u_w, u_m, u_a = big_update(w_up, m_up, a_up, 2)
    d_w, d_m, d_a = big_update(w_down, m_down, a_down, 3)
    h_w, h_m, h_a = update(w_head, m_head, a_head, grad_head, scale)
    return (
        loss, grad_norm, e_w, e_m, e_a, v_w, v_m, v_a, q_w, q_m, q_a, o_w, o_m, o_a,
        u_w, u_m, u_a, d_w, d_m, d_a, h_w, h_m, h_a,
    )


def solution(mesh):
    tables = [P(("dp", "head"), None, None)] + [P(("dp", "head"), None)] + [P()] + [P(("dp", "head"), None)] * 3
    joined = P(None, "dp", None, "head", None)
    mixed = P(None, "head", "dp", None)
    wide = P(None, ("dp", "head"), None)
    state = [P()] * 6 + [joined] * 3 + [mixed] * 3 + [wide] * 6 + [P()] * 3
    return jax.shard_map(
        shards, mesh=mesh, in_specs=tuple(tables + state), out_specs=tuple([P(), P()] + state), check_vma=False)
```

time: 1950 us -> 804 us (0.41)
  waiting for transfers between devices: 1110 us -> 0 us
  Pallas kernels: 0 us -> 512 us
  matrix products: 347 us -> 149 us
  local copies, waits for them, and re-layouts: 198 us -> 50.9 us
  blocking collectives: 81.3 us -> 0 us
  other arithmetic: 147 us -> 68.2 us
  loops' own time: 31.7 us -> 0 us
    pallas_call x0 -> x9, Pallas kernels: none -> 512 us  [the longest x2 246 us: reduce_scatter_layer(): pl.pallas_call(functools.partial(reduce_kernel, by_core), out_shape=tuple...]
    reduce_scatter x7 -> x0, waiting for transfers between devices: 470 us -> none  [the longest x1 208 us: shards(): lax.psum_scatter(grad_shrink, ('dp', 'head'), scatter_dimension=1, tiled=...]
    all_gather x8 -> x0, waiting for transfers between devices: 272 us -> none  [the longest x1 96.1 us: shards(): lax.all_gather(w_qkv.astype(low_type), 'dp', axis=1, tiled=True)]
    unnamed x18 -> x0, waiting for transfers between devices: 230 us -> none
    dot_general x75 -> x31, matrix products: 278 us -> 114 us  [the longest x15 77 us: contract(): lax.dot_general(first_op, second_op, (((first_dim,), (second_dim,)), ((),...]
    psum x1 -> x0, waiting for transfers between devices: 136 us -> none  [shards(): lax.psum((grad_emb, grad_vec, grad_head, loss_part, shard_square), ('dp',...]
    psum x2 -> x0, blocking collectives: 81.3 us -> none  [the longest x1 41.1 us: shards(): pooled = lax.psum(jnp.sum(query_weight), ('dp', 'head'))]
    slice x18 -> x4, local copies, waits for them, and re-layouts: 52.6 us -> 4.53 us  [the longest x1 1.99 us: shards(): final_rows = layer_norm(residual, vectors[-2], vectors[-1]).astype(low_type)]
  transfers between devices with their start and end apart: 17 -> 0, of which waited for: 13 -> 0; matrix products, arithmetic and copies ran while one was open for 13% -> 0% of each run, Pallas kernels for 0% -> 0%
where the time goes in v1:
time: 804 us; the launch traced here: 795 us
  Pallas kernels  512 us (64%)
  matrix products  149 us (19%)
  other arithmetic  68.2 us (8%)
  local copies, waits for them, and re-layouts  50.9 us (6%)
  between operations  15.4 us (2%)
    pallas_call x2, Pallas kernels, reduce_scatter_layer(): pl.pallas_call(functools.partial(reduce_kernel, by_core), out_shape=tuple...  246 us
    pallas_call x3, Pallas kernels, all_gather_layer(): pl.pallas_call(functools.partial(gather_kernel, by_core), out_shape=outs,...  177 us
    dot_general x15, matrix products, contract(): lax.dot_general(first_op, second_op, (((first_dim,), (second_dim,)), ((),...  77 us
    pallas_call x2, Pallas kernels, attend(): pl.pallas_call(attend_kernel, grid=grid, in_specs=[pl.BlockSpec((1, block...  45 us
    pallas_call x2, Pallas kernels, attend_back(): pl.pallas_call(attend_back_kernel, grid=grid, in_specs=[pl.BlockSpec((1,...  43.6 us
    dot_general x8, matrix products, matmul(): return jnp.dot(first_op, second_op, preferred_element_type=wide_type)  35.3 us

profile of v1, /device:TPU:0, one launch (start us, length us, event | category | flops | bytes accessed | tf_op | source)
XLA Modules:
  0.0 795.0 jit_solution(5644313796686720005)
XLA Ops:
  8.2 2.0 slice_reduce_fusion.4
  19.3 1.7 fusion.98
  21.5 1.7 add_convert_fusion.2
  23.2 69.0 %shard_map.434 = (bf16[2,16,3,16,1152]{4,3,2,1,0:T(8,128)(2,1)}, bf16[2,16,3,8,768]{4,3,2,1,0:T(8,128)(2,1)}, bf16[16,2,3,8,3072]{4,3,2,1,0:T(8,128)(2,1)}, bf16[16,2,3,32,768]{4,3,2,1,0:T(8,128)(2,1)}) custom-call(bf16[3,16,1152]{2,1,0:T(8,128)(2,1)} %convert_element_type.202.refs_0_, bf16[3,8,768]{2,1,0:T(8,128)(2,1)} %get-tuple-element.205.refs_1_, ...), custom_call_target="tpu_custom_call" | custom-call | bytes 27426816 | tf_op jit(solution)/shard_map/pallas_call | solution.py:153
  92.2 4.5 fusion.30.q_ref
  96.7 3.5 convert_bitcast_fusion.1.k_ref.v_ref
  100.2 34.6 %shard_map.436 = (bf16[1024,768]{1,0:T(8,128)(2,1)}, f32[6,2,1024]{2,1,0:T(2,128)}) custom-call(bf16[2,1024,384]{2,1,0:T(8,128)(2,1)} %fusion.30.q_ref, bf16[2,768,768]{2,1,0:T(8,128)(2,1)} %convert_bitcast_fusion.1.k_ref.v_ref, bf16[2,768,768]{2,1,0:T(8,128)(2,1)} %convert_bitcast_fusion.1.k_ref.v_ref, bf16[768,128]{1,0:T(8,128)(2,1)} %broadcast_in_dim.36.bias_ref), custom_call_target="tpu_custom_call" | custom-call | flops 2415919104 | bytes 6291456 | tf_op jit(solution)/shard_map/pallas_call | solution.py:432
  134.8 3.5 fusion.99
  138.8 8.7 %fusion.89 = f32[1024,3072]{1,0:T(8,128)} fusion(bf16[768,3072]{1,0:T(8,128)(2,1)S(1)} %bitcast.167, f32[1024,768]{0,1:T(8,128)S(1)} %get-tuple-element.212, f32[768]{0:T(1024)S(1)} %get-tuple-element.159, f32[768]{0:T(1024)S(1)} %get-tuple-element.160, f32[1024]{0:T(1024)S(1)} %fusion.79, f32[1024]{0:T(1024)S(1)} %broadcast_multiply_fusion.2), kind=kOutput, calls=%fused_computation.243 | convolution fusion | flops 4835770368 | bytes 20461568 | tf_op jit(solution)/shard_map/dot_general | solution.py:385
  147.5 11.8 %fusion.100 = (f32[1024]{0:T(1024)S(1)}, f32[1024,768]{0,1:T(8,128)S(1)}) fusion(f32[768]{0:T(1024)S(1)} %copy-done.103, f32[1024,768]{0,1:T(8,128)S(1)} %get-tuple-element.212, bf16[3072,768]{1,0:T(8,128)(2,1)S(1)} %bitcast.205, f32[1024,3072]{1,0:T(8,128)} %fusion.89), kind=kOutput, calls=%fused_computation.254 | convolution fusion | flops 4862508032 | bytes 23600128 | tf_op jit(solution)/shard_map/dot_general | solution.py:385
  160.0 1.7 add_convert_fusion
  161.7 68.9 %shard_map.435 = (bf16[2,16,3,16,1152]{4,3,2,1,0:T(8,128)(2,1)}, bf16[2,16,3,8,768]{4,3,2,1,0:T(8,128)(2,1)}, bf16[16,2,3,8,3072]{4,3,2,1,0:T(8,128)(2,1)}, bf16[16,2,3,32,768]{4,3,2,1,0:T(8,128)(2,1)}) custom-call(bf16[3,16,1152]{2,1,0:T(8,128)(2,1)} %convert_element_type.214.refs_0_, bf16[3,8,768]{2,1,0:T(8,128)(2,1)} %get-tuple-element.204.refs_1_, ...), custom_call_target="tpu_custom_call" | custom-call | bytes 27426816 | tf_op jit(solution)/shard_map/pallas_call | solution.py:153
  230.6 2.6 fusion.46.q_ref
  233.3 5.5 convert_bitcast_fusion.k_ref.v_ref
  238.8 10.4 %shard_map.437 = (bf16[256,768]{1,0:T(8,128)(2,1)}, f32[6,2,256]{2,1,0:T(2,128)}) custom-call(bf16[2,256,384]{2,1,0:T(8,128)(2,1)} %fusion.46.q_ref, bf16[2,768,768]{2,1,0:T(8,128)(2,1)} %convert_bitcast_fusion.k_ref.v_ref, bf16[2,768,768]{2,1,0:T(8,128)(2,1)} %convert_bitcast_fusion.k_ref.v_ref, bf16[768,128]{1,0:T(8,128)(2,1)} %broadcast_in_dim.36.bias_ref), custom_call_target="tpu_custom_call" | custom-call | flops 603979776 | bytes 1572864 | tf_op jit(solution)/shard_map/pallas_call | solution.py:432
  249.2 2.1 fusion.101
  251.5 4.3 fusion.88
  255.9 2.5 fusion.102
  263.9 2.3 copy.157
  266.2 1.9 multiply_reduce_fusion.10
  268.0 1.8 fusion.95
  269.8 5.6 fusion.13
  275.5 2.3 fusion.105
  279.0 2.3 copy.158
  281.3 1.7 multiply_reduce_fusion.12
  283.0 1.9 multiply_reduce_fusion.11
  285.5 1.6 fusion.92
  289.4 9.5 %shard_map.438 = (bf16[2,256,384]{2,1,0:T(8,128)(2,1)}, bf16[2,768,384]{2,1,0:T(8,128)(2,1)}, bf16[2,768,384]{2,1,0:T(8,128)(2,1)}) custom-call(bf16[2,256,384]{2,1,0:T(8,128)(2,1)} %fusion.46.q_ref, bf16[2,768,768]{2,1,0:T(8,128)(2,1)} %convert_bitcast_fusion.k_ref.v_ref, bf16[2,768,768]{2,1,0:T(8,128)(2,1)} %convert_bitcast_fusion.k_ref.v_ref, ...), custom_call_target="tpu_custom_call" | custom-call | flops 1509949440 | bytes 3145728 | tf_op jit(solution)/shard_map/pallas_call | solution.py:499
  300.1 6.7 convolution_convert_fusion.2
  306.7 2.8 convolution_bitcast_fusion
  314.1 1.9 pad_maximum_fusion.1
  316.0 5.8 copy.184
  321.8 2.8 fusion.51
  324.7 2.5 bitcast_add_fusion.2
  331.0 16.1 %fusion.6 = bf16[1024,3072]{1,0:T(8,128)(2,1)} fusion(f32[1024,3072]{1,0:T(8,128)} %fusion.89, bf16[3072,768]{1,0:T(8,128)(2,1)} %bitcast.202, f32[256,768]{0,1:T(8,128)S(1)} %copy-done.20, f32[1024,768]{0,1:T(8,128)S(1)} %get-tuple-element.194, f32[1024]{0:T(1024)S(1)} %negate_multiply_fusion.2), kind=kOutput, calls=%fused_computation.8 | convolution fusion | flops 4897112064 | bytes 27529216 | tf_op jit(solution)/shard_map/dot_general | solution.py:389
  347.1 13.1 %convolution_convert_fusion = bf16[3072,768]{1,0:T(8,128)(2,1)} fusion(f32[256,768]{0,1:T(8,128)S(1)} %copy-done.20, f32[1024,768]{0,1:T(8,128)S(1)} %get-tuple-element.194, f32[1024]{0:T(1024)S(1)} %negate_multiply_fusion.2, f32[1024,3072]{1,0:T(8,128)} %fusion.89), kind=kOutput, calls=%fused_computation.10 | convolution fusion | flops 4864868352 | bytes 21237760 | tf_op jit(solution)/shard_map/dot_general | solution.py:389
  360.2 9.2 %fusion.104 = (bf16[768]{0:T(1024)(128)(2,1)S(1)}, f32[1024,768]{1,0:T(8,128)}) fusion(bf16[1024,3072]{1,0:T(8,128)(2,1)S(1)} %copy-done.110, bf16[768,3072]{1,0:T(8,128)(2,1)} %bitcast.164), kind=kOutput, calls=%fused_computation.258 | convolution fusion | flops 4832623616 | bytes 14157312 | tf_op jit(solution)/shard_map/dot_general | solution.py:389
  369.4 7.6 convolution_convert_fusion.1
  377.5 3.6 convolution_convert_fusion.3
  381.2 115.0 %shard_map.441 = (f32[3,16,1152]{2,1,0:T(8,128)}, f32[3,8,768]{2,1,0:T(8,128)}, f32[3,8,3072]{2,1,0:T(8,128)}, f32[3,32,768]{2,1,0:T(8,128)}) custom-call(bf16[2,16,3,16,1152]{4,3,2,1,0:T(8,128)(2,1)} %bitcast.157, bf16[2,16,3,8,768]{4,3,2,1,0:T(8,128)(2,1)} %bitcast.163, bf16[16,2,3,8,3072]{4,3,2,1,0:T(8,128)(2,1)} %bitcast.156, ...), custom_call_target="tpu_custom_call" | custom-call | flops 7077888 | bytes 14155776 | tf_op jit(solution)/shard_map/pallas_call | solution.py:337
  496.2 1.7 multiply_reduce_fusion.16
  497.8 1.6 multiply_reduce_fusion.17
  501.0 1.6 multiply_reduce_fusion.20
  504.3 3.9 copy.163
  508.2 2.5 multiply_reduce_fusion.5
  513.2 1.8 fusion.93
  515.0 1.6 copy-done.15
  516.6 2.6 convolution_convert_fusion.4.g_ref
  519.2 34.1 %shard_map.439 = (bf16[2,1024,384]{2,1,0:T(8,128)(2,1)}, bf16[2,768,384]{2,1,0:T(8,128)(2,1)}, bf16[2,768,384]{2,1,0:T(8,128)(2,1)}) custom-call(bf16[2,1024,384]{2,1,0:T(8,128)(2,1)} %fusion.30.q_ref, bf16[2,768,768]{2,1,0:T(8,128)(2,1)} %convert_bitcast_fusion.1.k_ref.v_ref, bf16[2,768,768]{2,1,0:T(8,128)(2,1)} %convert_bitcast_fusion.1.k_ref.v_ref, ...), custom_call_target="tpu_custom_call" | custom-call | flops 6039797760 | bytes 12582912 | tf_op jit(solution)/shard_map/pallas_call | solution.py:499
  553.3 4.0 convolution_convert_fusion.10
  561.5 4.0 copy.170
  565.6 2.9 fusion.48
  571.0 1.7 fusion.90
  574.8 1.6 fusion.91
  578.4 131.0 %shard_map.440 = (f32[3,16,1152]{2,1,0:T(8,128)}, f32[3,8,768]{2,1,0:T(8,128)}, f32[3,8,3072]{2,1,0:T(8,128)}, f32[3,32,768]{2,1,0:T(8,128)}, f32[3,8,512]{2,1,0:T(8,128)}, /*index=5*/f32[3,16,128]{2,1,0:T(8,128)}) custom-call(bf16[2,16,3,16,1152]{4,3,2,1,0:T(8,128)(2,1)} %bitcast.158, bf16[2,16,3,8,768]{4,3,2,1,0:T(8,128)(2,1)} %bitcast.189, ...), custom_call_target="tpu_custom_call" | custom-call | flops 7667712 | bytes 15335424 | tf_op jit(solution)/shard_map/pallas_call | solution.py:337
  709.4 1.6 multiply_reduce_fusion.18
  711.1 1.6 multiply_reduce_fusion.19
  714.2 1.6 multiply_reduce_fusion.21
  728.7 39.0 %shard_map.442 = (f32[16,2,3,8,512]{4,3,2,1,0:T(8,128)}, f32[16,2,3,16,128]{4,3,2,1,0:T(8,128)}, f32[16,2,3,8,128]{4,3,2,1,0:T(8,128)}) custom-call(f32[3,8,512]{2,1,0:T(8,128)} %get-tuple-element.72.refs_0_, f32[3,16,128]{2,1,0:T(8,128)} %get-tuple-element.73.refs_1_, f32[3,8,128]{2,1,0:T(8,128)} %broadcast_in_dim.48.refs_2_), custom_call_target="tpu_custom_call" | custom-call | bytes 2666496 | tf_op jit(solution)/shard_map/pallas_call | solution.py:153
  773.6 1.7 broadcast_multiply_fusion
  776.1 1.6 multiply_add_fusion.12
  777.7 1.9 multiply_add_fusion.10
  779.6 2.2 multiply_add_fusion.7
  789.5 2.8 multiply_add_fusion.1
  (348 shorter events, 71.8 us)
Async XLA Ops:
  0.7 15.6 %copy-start.31 = (f32[2,48,3,1,384]{4,3,2,1,0:T(1,128)S(1)}, f32[2,48,3,1,384]{4,3,2,1,0:T(1,128)}, u32[]{:S(2)}) copy-start(f32[2,48,3,1,384]{4,3,2,1,0:T(1,128)} %param.39) | copy-start | bytes 1327108
  0.7 18.7 %copy-start.39 = (f32[128,768]{1,0:T(8,128)S(1)}, f32[128,768]{1,0:T(8,128)}, u32[]{:S(2)}) copy-start(f32[128,768]{1,0:T(8,128)} %param.33) | copy-start | bytes 1179652
  10.2 359.1 %copy-start.63 = (f32[768]{0:T(1024)}, f32[768]{0:T(1024)S(1)}, u32[]{:S(2)}) copy-start(f32[768]{0:T(1024)S(1)} %get-tuple-element.160) | copy-start | bytes 9220
  21.0 113.7 %copy-start = (f32[1024,768]{0,1:T(8,128)}, f32[1024,768]{0,1:T(8,128)S(1)}, u32[]{:S(2)}) copy-start(f32[1024,768]{0,1:T(8,128)S(1)} %get-tuple-element.210) | copy-start | bytes 9437188
  21.4 75.3 %copy-start.81 = (f32[1024]{0:T(1024)}, f32[1024]{0:T(1024)S(1)}, u32[]{:S(2)}) copy-start(f32[1024]{0:T(1024)S(1)} %multiply_reduce_fusion.9) | copy-start | bytes 12292
  21.5 75.2 %copy-start.77 = (f32[1024]{0:T(1024)}, f32[1024]{0:T(1024)S(1)}, u32[]{:S(2)}) copy-start(f32[1024]{0:T(1024)S(1)} %fusion.78) | copy-start | bytes 12292
  92.2 4.5 copy-start.33
  92.2 4.5 copy-start.37
  100.2 34.6 %copy-start.104 = (f32[768]{0:T(1024)S(1)}, f32[768]{0:T(1024)}, u32[]{:S(2)}) copy-start(f32[768]{0:T(1024)} %get-tuple-element.161) | copy-start | bytes 9220
  134.8 4.0 slice-start.2
  134.8 4.0 slice-start.3
  138.3 9.2 %copy-start.2 = (f32[1024,768]{0,1:T(8,128)}, f32[1024,768]{0,1:T(8,128)S(1)}, u32[]{:S(2)}) copy-start(f32[1024,768]{0,1:T(8,128)S(1)} %get-tuple-element.212) | copy-start | bytes 9437188
  138.3 231.1 %copy-start.57 = (f32[1024]{0:T(1024)}, f32[1024]{0:T(1024)S(1)}, u32[]{:S(2)}) copy-start(f32[1024]{0:T(1024)S(1)} %broadcast_multiply_fusion.2) | copy-start | bytes 12292
  138.3 9.1 %slice-start.4 = ((s8[4718592]{0:T(1024)(128)(4,1)}), s8[4194304]{0:T(1024)(128)(4,1)S(1)}, s32[]{:S(2)}) async-start(s8[4718592]{0:T(1024)(128)(4,1)} %bitcast.203), calls=%async_computation.4 | async-start | bytes 8388608
  138.7 8.7 %copy-start.83 = (f32[1024]{0:T(1024)}, f32[1024]{0:T(1024)S(1)}, u32[]{:S(2)}) copy-start(f32[1024]{0:T(1024)S(1)} %multiply_reduce_fusion.8) | copy-start | bytes 12292
  138.8 230.6 %copy-start.65 = (f32[1024]{0:T(1024)}, f32[1024]{0:T(1024)S(1)}, u32[]{:S(2)}) copy-start(f32[1024]{0:T(1024)S(1)} %fusion.79) | copy-start | bytes 12292
  138.8 8.7 %copy-start.103 = (f32[768]{0:T(1024)S(1)}, f32[768]{0:T(1024)}, u32[]{:S(2)}) copy-start(f32[768]{0:T(1024)} %get-tuple-element.158) | copy-start | bytes 9220
  138.8 8.7 %slice-start.5 = ((s8[4718592]{0:T(1024)(128)(4,1)}), s8[524288]{0:T(1024)(128)(4,1)S(1)}, s32[]{:S(2)}) async-start(s8[4718592]{0:T(1024)(128)(4,1)} %bitcast.203), calls=%async_computation.5 | async-start | bytes 1048576
  238.8 10.5 %copy-start.86 = (f32[768]{0:T(1024)S(1)}, f32[768]{0:T(1024)}, u32[]{:S(2)}) copy-start(f32[768]{0:T(1024)} %get-tuple-element.155) | copy-start | bytes 9220
  251.3 4.5 copy-start.6
  251.3 4.5 slice-start.6
  251.5 4.3 copy-start.102
  251.5 4.3 slice-start.7
  266.2 3.7 copy-start.26
  268.0 7.4 slice-start
  269.8 5.6 copy-start.27
  269.8 5.6 slice-start.1
  281.3 4.2 copy-start.7
  281.3 4.3 copy-start.12
  281.3 6.8 copy-start.23
  300.0 6.7 copy-start.41
  300.0 9.5 %copy-start.28 = (bf16[1024,768]{0,1:T(8,128)(2,1)S(1)}, bf16[1024,768]{0,1:T(8,128)(2,1)}, u32[]{:S(2)}) copy-start(bf16[1024,768]{0,1:T(8,128)(2,1)} %add_convert_fusion) | copy-start | bytes 4718596
  306.7 4.9 copy-start.108
  329.3 17.7 %copy-start.13 = (f32[1024,768]{0,1:T(8,128)}, f32[1024,768]{0,1:T(8,128)S(1)}, u32[]{:S(2)}) copy-start(f32[1024,768]{0,1:T(8,128)S(1)} %get-tuple-element.194) | copy-start | bytes 9437188
  329.4 17.7 %copy-start.89 = (f32[1024]{0:T(1024)}, f32[1024]{0:T(1024)S(1)}, u32[]{:S(2)}) copy-start(f32[1024]{0:T(1024)S(1)} %negate_multiply_fusion.2) | copy-start | bytes 12292
  347.1 13.1 %copy-start.110 = (bf16[1024,3072]{1,0:T(8,128)(2,1)S(1)}, bf16[1024,3072]{1,0:T(8,128)(2,1)}, u32[]{:S(2)}) copy-start(bf16[1024,3072]{1,0:T(8,128)(2,1)} %fusion.6) | copy-start | bytes 18874372
  360.2 9.2 %copy-start.3 = (f32[1024,768]{0,1:T(8,128)S(1)}, f32[1024,768]{0,1:T(8,128)}, u32[]{:S(2)}) copy-start(f32[1024,768]{0,1:T(8,128)} %copy-done.2) | copy-start | bytes 9437188
  369.4 8.2 %copy-start.8 = (f32[256,768]{0,1:T(8,128)S(1)}, f32[256,768]{0,1:T(8,128)}, u32[]{:S(2)}) copy-start(f32[256,768]{0,1:T(8,128)} %copy-done.6) | copy-start | bytes 2359300
  369.4 8.2 %copy-start.45 = (bf16[256,3072]{1,0:T(8,128)(2,1)S(1)}, bf16[256,3072]{1,0:T(8,128)(2,1)}, u32[]{:S(2)}) copy-start(bf16[256,3072]{1,0:T(8,128)(2,1)} %copy-done.44) | copy-start | bytes 4718596
  504.3 3.9 copy-start.4
  504.3 3.9 copy-start.58
  504.3 3.9 copy-start.64
  519.2 34.1 %copy-start.16 = (f32[1024,768]{0,1:T(8,128)S(1)}, f32[1024,768]{0,1:T(8,128)}, u32[]{:S(2)}) copy-start(f32[1024,768]{0,1:T(8,128)} %copy-done.15) | copy-start | bytes 9437188
  553.3 4.0 copy-start.35
  553.3 4.0 copy-start.38
  715.8 60.3 %copy-start.71 = (f32[16,768]{1,0:T(8,128)S(1)}, f32[16,768]{1,0:T(8,128)}, u32[]{:S(2)}) copy-start(f32[16,768]{1,0:T(8,128)} %param.36) | copy-start | bytes 147460
  726.9 50.8 %copy-start.69 = (f32[3,8,768]{2,1,0:T(8,128)S(1)}, f32[3,8,768]{2,1,0:T(8,128)}, u32[]{:S(2)}) copy-start(f32[3,8,768]{2,1,0:T(8,128)} %get-tuple-element.79) | copy-start | bytes 221188
  773.5 6.1 copy-start.40
  775.3 6.6 copy-start.32
  775.3 6.6 copy-start.55
  776.1 5.8 copy-start.56
  776.1 5.8 copy-start.67
  776.1 5.8 copy-start.68
  781.9 4.0 copy-start.29
  781.9 4.0 copy-start.47
  781.9 4.0 copy-start.49
  781.9 4.0 copy-start.59
  781.9 4.0 copy-start.60
  783.4 3.9 copy-start.30
  783.4 3.9 copy-start.46
  783.4 3.9 copy-start.48
  783.4 3.9 copy-start.61
  783.4 3.9 copy-start.62
  785.9 3.6 copy-start.43
  (55 other events, 117.9 us)

commit v2 on v1

v2 whole, which is shorter than its diff:
```python
import functools
import jax
import jax.numpy as jnp
from jax import lax
from jax.sharding import PartitionSpec as P
from jax.experimental import pallas as pl
from jax.experimental.pallas import tpu as pltpu

MESH = pl.DeviceIdType.MESH


class Place:
    def __init__(self):
        self.chip = lax.axis_index("dp")
        self.core = lax.axis_index("head")
        self.x = self.chip % 2
        self.y = (self.chip // 2) % 2
        self.z = self.chip // 4
        z = self.z
        self.z_from = (z, 1 + z % 2, (12 - 2 * z) % 5, 3 - 3 * (z // 2))

    def peer(self, way):
        step = {
            "x": 1 - 2 * self.x,
            "y": 2 - 4 * self.y,
            "u": 4,
            "d": -4,
            "c": 0,
        }[way]
        core = 1 - self.core if way == "c" else self.core
        return (self.chip + step, core)

    def block(self, k, ax, ay):
        sx = self.x if ax == 0 else 1 - self.x
        sy = self.y if ay == 0 else 1 - self.y
        return self.z_from[k] * 4 + sy * 2 + sx


def meet(place):
    barrier = pltpu.get_barrier_semaphore()
    for way in "xyc":
        pl.semaphore_signal(barrier, inc=1, device_id=place.peer(way), device_id_type=MESH)

    @pl.when(place.z < 3)
    def _():
        pl.semaphore_signal(barrier, inc=1, device_id=place.peer("u"), device_id_type=MESH)

    @pl.when(place.z > 0)
    def _():
        pl.semaphore_signal(barrier, inc=1, device_id=place.peer("d"), device_id_type=MESH)

    ends = place.z * (3 - place.z)
    pl.semaphore_wait(barrier, 4 + ends // 2)


def at_block(ref, chip, core, piece, by_core):
    return ref.at[core, chip, piece] if by_core else ref.at[chip, core, piece]


class Gather:
    def __init__(self, by_core, orders, shapes, dtype):
        self.by_core, self.orders, self.shapes, self.dtype = by_core, orders, shapes, dtype
        self.n, self.pieces = len(by_core), max(map(len, orders))

    def in_specs(self):
        return [pl.BlockSpec(memory_space=pl.ANY)] * self.n

    def out_specs(self):
        return [pl.BlockSpec(memory_space=pl.ANY)] * self.n

    def out_shape(self):
        return [
            jax.ShapeDtypeStruct(((2, 16) if bc else (16, 2)) + s, self.dtype)
            for s, bc in zip(self.shapes, self.by_core)]

    def scratch(self):
        n, pieces = self.n, self.pieces
        return [
            pltpu.SemaphoreType.DMA((n, pieces)),
            pltpu.SemaphoreType.DMA((n, pieces, 16)),
            pltpu.SemaphoreType.DMA((n,)),
            pltpu.SemaphoreType.DMA((n, pieces, 4)),
            pltpu.SemaphoreType.DMA((n,)),
        ]

    def steps(self, ins, outs, scratch):
        n, orders = self.n, self.orders
        local_sem, recv, core_recv, send, core_send = scratch
        place = Place()
        me = place.chip
        ways = {"x": 0, "y": 1, "u": 2, "d": 3}

        def slot(a, c, chip):
            return at_block(outs[a], chip, place.core, c, self.by_core[a])

        def copy(a, c, chip, way, src, sems):
            return pltpu.make_async_remote_copy(
                src_ref=src, dst_ref=slot(a, c, chip), send_sem=sems[0], recv_sem=sems[1],
                device_id=place.peer(way), device_id_type=MESH)

        def forward(a, c, order, k, ax, ay):
            chip = place.block(k, ax, ay)
            rel = {"x": ax, "y": ay, "z": k}
            last = max([i for i in range(3) if rel[order[i]] != 0], default=-1)
            src = ins[a].at[c] if last < 0 else slot(a, c, chip)
            for i in range(max(last, 0), 3):
                dim = order[i]
                if dim == "z":
                    sz = place.z_from[k]

                    @pl.when((sz <= place.z) & (place.z < 3))
                    def _():
                        copy(a, c, chip, "u", src, (send.at[a, c, 2], recv.at[a, c, chip])).start()

                    @pl.when((sz >= place.z) & (place.z > 0))
                    def _():
                        copy(a, c, chip, "d", src, (send.at[a, c, 3], recv.at[a, c, chip])).start()
                elif rel[dim] == 0:
                    copy(a, c, chip, dim, src, (send.at[a, c, ways[dim]], recv.at[a, c, chip])).start()
            copy(a, c, chip, "c", src, (core_send.at[a], core_recv.at[a])).start()

        def own(a, c):
            return pltpu.make_async_copy(ins[a].at[c], slot(a, c, me), local_sem.at[a, c])

        def entry(k, ax, ay):
            if (k, ax, ay) == (0, 0, 0):
                meet(place)
            for a in range(n):
                for c, order in enumerate(orders[a]):
                    chip = place.block(k, ax, ay)
                    if (k, ax, ay) != (0, 0, 0):
                        copy(a, c, chip, "x", slot(a, c, chip), (send.at[a, c, 0], recv.at[a, c, chip])).wait_recv()
                    forward(a, c, order, k, ax, ay)
                    if (k, ax, ay) == (0, 0, 0):
                        own(a, c).start()

        def finish():
            for a in range(n):
                for c in range(len(orders[a])):
                    own(a, c).wait()
            for a in range(n):
                whole = outs[a].at[0] if self.by_core[a] else outs[a].at[:, 0]
                pltpu.make_async_remote_copy(
                    src_ref=whole, dst_ref=whole, send_sem=core_send.at[a], recv_sem=core_recv.at[a],
                    device_id=place.peer("c"), device_id_type=MESH).wait()
                for c, order in enumerate(orders[a]):
                    def drain(way, count):
                        lead = outs[a].at[0] if self.by_core[a] else outs[a].at[:, 0]
                        part = lead.at[pl.ds(0, count), c]
                        pltpu.make_async_remote_copy(
                            src_ref=part, dst_ref=part, send_sem=send.at[a, c, ways[way]],
                            recv_sem=recv.at[a, c, 0],
                            device_id=place.peer("c"), device_id_type=MESH).wait_send()
                    before = 1
                    for dim in order:
                        if dim == "z":
                            for zz in range(4):
                                @pl.when(place.z == zz)
                                def _(zz=zz, before=before):
                                    if zz < 3:
                                        drain("u", before * (zz + 1))
                                    if zz > 0:
                                        drain("d", before * (4 - zz))
                            before *= 4
                        else:
                            drain(dim, before)
                            before *= 2

        entries = sorted(
            [(k, ax, ay) for k in range(4) for ax in range(2) for ay in range(2)], key=lambda e: e[0] + e[1] + e[2])
        return [functools.partial(entry, *e) for e in entries] + [finish]


class Reduce:
    def __init__(self, by_core, orders, shapes):
        self.by_core, self.orders, self.shapes = by_core, orders, shapes
        self.n, self.pieces = len(by_core), max(map(len, orders))

    def in_specs(self):
        return [pl.BlockSpec(memory_space=pl.ANY)] * self.n

    def out_specs(self):
        return [pl.BlockSpec(memory_space=pltpu.VMEM)] * self.n

    def out_shape(self):
        return [jax.ShapeDtypeStruct(s, jnp.float32) for s in self.shapes]

    def room(self, a, way):
        most = 1
        for order in self.orders[a]:
            if way in "ud":
                most = max(most, 4 if order[0] == "z" else 8)
            else:
                most = max(most, {2: 8, 1: 4, 0: 1}[order.index(way)])
        return most

    def scratch(self):
        n, pieces = self.n, self.pieces
        buffers = []
        for sizes in ([16] * n, [16] * n, *[[self.room(a, w) for a in range(n)] for w in "xyud"]):
            buffers += [pltpu.VMEM((k,) + s, jnp.bfloat16) for k, s in zip(sizes, self.shapes)]
        return buffers + [
            pltpu.SemaphoreType.DMA((n,)),
            pltpu.SemaphoreType.DMA((n, pieces, 16)),
            pltpu.SemaphoreType.DMA((n, pieces)),
            pltpu.SemaphoreType.DMA((n, pieces, 4, 8)),
            pltpu.SemaphoreType.DMA((n, pieces, 4)),
        ]

    def steps(self, ins, outs, scratch):
        n, orders, by_core = self.n, self.orders, self.by_core
        mine, other = scratch[:n], scratch[n : 2 * n]
        got = {w: scratch[(2 + i) * n : (3 + i) * n] for i, w in enumerate("xyud")}
        load_sem, core_recv, core_send, recv, send = scratch[6 * n :]
        ways = {"x": 0, "y": 1, "u": 2, "d": 3}
        place = Place()

        def number(at):
            sx, sy, sz = at
            return sz * 4 + sy * 2 + sx

        def load(a):
            src = ins[a].at[place.core] if by_core[a] else ins[a].at[:, place.core]
            return pltpu.make_async_copy(src, mine[a], load_sem.at[a])

        def to_core(a, c, at):
            chip = number(at)
            return pltpu.make_async_remote_copy(
                src_ref=at_block(ins[a], chip, 1 - place.core, c, by_core[a]), dst_ref=other[a].at[chip, c],
                send_sem=core_send.at[a, c], recv_sem=core_recv.at[a, c, chip],
                device_id=place.peer("c"), device_id_type=MESH)

        def landing(order, at, way):
            sx, sy, sz = at
            if way in "ud":
                return sz if order[0] == "z" else sz * 2 + (sx if order[0] == "x" else sy)
            turn = order.index(way)
            return (0, sz, sz * 2 + (sx if way == "y" else sy))[turn]

        def hop(a, c, order, at, way):
            spot = landing(order, at, way)
            return pltpu.make_async_remote_copy(
                src_ref=mine[a].at[number(at), c], dst_ref=got[way][a].at[spot, c],
                send_sem=send.at[a, c, ways[way]], recv_sem=recv.at[a, c, ways[way], spot],
                device_id=place.peer(way), device_id_type=MESH)

        def take(a, c, order, at, way):
            hop(a, c, order, at, way).wait_recv()
            mine[a][number(at), c] = mine[a][number(at), c] + got[way][a][landing(order, at, way), c]

        def fold(a, c, at):
            to_core(a, c, at).wait_recv()
            chip = number(at)
            mine[a][chip, c] = mine[a][chip, c] + other[a][chip, c]

        items = [(a, c, order) for a in range(n) for c, order in enumerate(orders[a])]
        lined = [it for it in items if it[2][1] == "z"]
        flat = [it for it in items if it[2][0] == "z"]
        items = lined + flat

        def side(dim, far):
            m = place.x if dim == "x" else place.y
            return 1 - m if far else m

        def spot(order, wave, i, far):
            sz = wave + (3 - 2 * wave) * (i // 2)
            if order[2] == "y":
                return (i % 2, side("y", far), sz)
            return (side("x", far), i % 2, sz)

        def loop(count, body):
            def run(i, carry):
                body(i)
                return carry
            lax.fori_loop(0, count, run, 0)

        def start(wave, far):
            for a, c, order in items:
                loop(4, lambda i: to_core(a, c, spot(order, wave, i, far)).start())

        def begin():
            meet(place)
            for a in range(n):
                load(a).start()
            for wave, far in ((0, True), (0, False), (1, True), (1, False)):
                start(wave, far)
            for a in range(n):
                load(a).wait()

        def far(wave):
            for a, c, order in items:
                def one(i):
                    at = spot(order, wave, i, True)
                    fold(a, c, at)
                    hop(a, c, order, at, order[2]).start()
                loop(4, one)

        def near(wave):
            for a, c, order in items:
                loop(4, lambda i: fold(a, c, spot(order, wave, i, False)))

        def second(it, wave):
            a, c, order = it
            if order[1] == "z":
                loop(4, lambda i: take(a, c, order, spot(order, wave, i, False), order[2]))
                return
            for away in (True, False):
                def one(i):
                    sz = wave + (3 - 2 * wave) * i
                    at = (side("x", away and order[1] == "x"), side("y", away and order[1] == "y"), sz)
                    take(a, c, order, at, order[2])
                    if away:
                        hop(a, c, order, at, order[1]).start()
                loop(2, one)

        def third(it, wave):
            a, c, order = it
            loop(2, lambda i: take(a, c, order, (place.x, place.y, wave + (3 - 2 * wave) * i), order[1]))

        def here(order):
            if order[0] == "z":
                return [(place.x, place.y)]
            return [(side("x", order[0] == "x"), side("y", order[0] == "y")), (place.x, place.y)]

        def line(it, j):
            a, c, order = it
            for way, target, active, inner in (
                ("u", 3 - j, place.z < 3 - j, place.z > 0),
                ("d", j, place.z > j, place.z < 3),
            ):
                @pl.when(active)
                def _():
                    for sx, sy in here(order):
                        at = (sx, sy, target)

                        @pl.when(inner)
                        def _():
                            take(a, c, order, at, way)
                        hop(a, c, order, at, way).start()

        def owned(it):
            a, c, order = it
            for first, (sx, sy) in enumerate(here(order)):
                at = (sx, sy, place.z)

                @pl.when(place.z > 0)
                def _():
                    take(a, c, order, at, "u")

                @pl.when(place.z < 3)
                def _():
                    take(a, c, order, at, "d")
                if order[0] != "z" and first == 0:
                    hop(a, c, order, at, order[0]).start()

        def last(it):
            a, c, order = it
            if order[0] != "z":
                take(a, c, order, (place.x, place.y, place.z), order[0])
            outs[a][c] = mine[a][place.chip, c].astype(jnp.float32)

        def drain(a, c, sem, count):
            part = other[a].at[pl.ds(0, count), c]
            pltpu.make_async_remote_copy(
                src_ref=part, dst_ref=part, send_sem=sem, recv_sem=recv.at[a, c, 0, 0],
                device_id=place.peer("c"), device_id_type=MESH).wait_send()

        def finish():
            for it in lined:
                last(it)
            for a, c, order in items:
                drain(a, c, core_send.at[a, c], 16)
                left = 16
                for turn in (2, 1, 0):
                    dim = order[turn]
                    if dim == "z":
                        left //= 4
                        for zz in range(4):
                            @pl.when(place.z == zz)
                            def _(zz=zz, left=left):
                                if zz < 3:
                                    drain(a, c, send.at[a, c, 2], left * (3 - zz))
                                if zz > 0:
                                    drain(a, c, send.at[a, c, 3], left * zz)
                    else:
                        left //= 2
                        drain(a, c, send.at[a, c, ways[dim]], left)

        part = functools.partial
        out = [begin, part(far, 0), part(near, 0), part(far, 1)]
        for it in lined:
            out += [part(second, it, 0), part(line, it, 0)]
        out += [part(second, it, 0) for it in flat]
        out += [part(near, 1)]
        for i, it in enumerate(lined):
            out += [part(second, it, 1), part(line, it, 1), part(line, it, 2)]
            if i == 0:
                for fl in flat:
                    out += [part(third, fl, 0), part(line, fl, 0)]
        if not lined:
            for fl in flat:
                out += [part(third, fl, 0), part(line, fl, 0)]
        out += [part(second, it, 1) for it in flat]
        out += [part(owned, it) for it in lined]
        for it in flat:
            out += [part(third, it, 1), part(line, it, 1), part(line, it, 2), part(owned, it), part(last, it)]
        return out + [finish]


VMEM_ALL = 64 * 1024 * 1024 - 65536


class Aside:
    def __init__(self, plan, arrays, collective_id):
        self.plan, self.arrays, self.collective_id = plan, arrays, collective_id


def with_aside(body, aside, *, grid, in_specs, out_specs, out_shape, scratch_shapes=(), cost, operands):
    if aside is None:
        out = pl.pallas_call(
            body, grid=grid, in_specs=in_specs, out_specs=out_specs, out_shape=tuple(out_shape),
            scratch_shapes=scratch_shapes, cost_estimate=cost,
            compiler_params=pltpu.CompilerParams(vmem_limit_bytes=VMEM_ALL))(*operands)
        return out, None
    plan = aside.plan
    n_in, n_out, n_scr, n = len(in_specs), len(out_specs), len(scratch_shapes), plan.n
    cells = 1
    for extent in grid:
        cells *= extent

    def kernel(*refs):
        refs = list(refs)
        ins, refs = refs[:n_in], refs[n_in:]
        plan_ins, refs = refs[:n], refs[n:]
        outs, refs = refs[:n_out], refs[n_out:]
        plan_outs, refs = refs[:n], refs[n:]
        scratch, plan_scratch = refs[:n_scr], refs[n_scr:]
        steps = plan.steps(plan_ins, plan_outs, plan_scratch)
        cell = 0
        for axis, extent in enumerate(grid):
            cell = cell * extent + pl.program_id(axis)
        by_cell = {}
        for i, step in enumerate(steps):
            by_cell.setdefault(i * (cells - 1) // (len(steps) - 1), []).append(step)
        for index in sorted(by_cell):
            if index < cells - 1:
                @pl.when(cell == index)
                def _():
                    for step in by_cell[index]:
                        step()
        body(*ins, *outs, *scratch)

        @pl.when(cell == cells - 1)
        def _():
            for step in by_cell[cells - 1]:
                step()

    out = pl.pallas_call(
        kernel, grid=grid,
        in_specs=list(in_specs) + plan.in_specs(), out_specs=list(out_specs) + plan.out_specs(),
        out_shape=tuple(out_shape) + tuple(plan.out_shape()),
        scratch_shapes=list(scratch_shapes) + plan.scratch(), cost_estimate=cost,
        compiler_params=pltpu.CompilerParams(
            collective_id=aside.collective_id, has_side_effects=True, vmem_limit_bytes=VMEM_ALL),
    )(*operands, *aside.arrays)
    return out[:n_out], out[n_out:]


def exchange(plan, arrays, collective_id):
    n = plan.n

    def kernel(*refs):
        for step in plan.steps(refs[:n], refs[n : 2 * n], refs[2 * n :]):
            step()

    moved = sum(a.size for a in arrays) * 2
    return pl.pallas_call(
        kernel,
        out_shape=tuple(plan.out_shape()),
        in_specs=plan.in_specs(),
        out_specs=plan.out_specs(),
        scratch_shapes=plan.scratch(),
        compiler_params=pltpu.CompilerParams(
            collective_id=collective_id, has_side_effects=True, vmem_limit_bytes=VMEM_ALL),
        cost_estimate=pl.CostEstimate(flops=0, bytes_accessed=32 * moved, transcendentals=0),
    )(*arrays)


def gather_plan(arrays, by_core, orders):
    return Gather(by_core, orders, [a.shape for a in arrays], arrays[0].dtype)


def reduce_plan(arrays, by_core, orders):
    return Reduce(by_core, orders, [a.shape[2:] for a in arrays])


def all_gather_layer(arrays, by_core, orders, collective_id):
    return exchange(gather_plan(arrays, by_core, orders), arrays, collective_id)


def reduce_scatter_layer(arrays, by_core, orders, collective_id):
    return exchange(reduce_plan(arrays, by_core, orders), arrays, collective_id)


HD = 64
CTX = 768

eps_norm = 1e-05
clip_at = 0.01
rate = 3000.0
moment = 0.9
keep_avg = 0.9
decay_wd = 1e-05
low_type = jnp.bfloat16
wide_type = jnp.float32


def layer_norm(values, gain_row, shift_row):
    center = values - jnp.mean(values, -1, keepdims=True)
    spread = jnp.mean(center * center, -1, keepdims=True)
    return center * lax.rsqrt(spread + eps_norm) * gain_row + shift_row


def norm_back(values, gain_row, shift_row, upstream):
    _, pull = jax.vjp(layer_norm, values, gain_row, shift_row)
    return pull(upstream)


def gelu_back(values, upstream):
    _, pull = jax.vjp(jax.nn.gelu, values)
    return pull(upstream)[0]


def matmul(first_op, second_op):
    return jnp.dot(first_op, second_op, preferred_element_type=wide_type)


def contract(first_op, second_op, first_dim, second_dim):
    return lax.dot_general(
        first_op, second_op, (((first_dim,), (second_dim,)), ((), ())), preferred_element_type=wide_type
    )


def matmul_tn(first_op, second_op):
    return contract(first_op, second_op, 0, 0)


def matmul_nt(first_op, second_op):
    return contract(first_op, second_op, 1, 1)


def head_lanes(shape, head):
    lane = lax.broadcasted_iota(jnp.int32, shape, 1)
    mine = (lane < HD) if head == 0 else (lane >= HD)
    return mine, lane == (HD if head == 0 else 0)


def attend_kernel(q_ref, k_ref, v_ref, bias_ref, out_ref, lse_ref):
    q_block = q_ref[0] * jnp.asarray(HD ** -0.5, low_type)
    k_block, v_block, bias = k_ref[0], v_ref[0], bias_ref[...]
    v_turned = v_block.T
    parts = []
    for head in range(2):
        q_mine, q_one = head_lanes(q_block.shape, head)
        k_mine, _ = head_lanes(k_block.shape, head)
        one = jnp.where(q_one, jnp.ones_like(q_block), jnp.zeros_like(q_block))
        score = matmul_nt(jnp.where(k_mine, k_block, bias), jnp.where(q_mine, q_block, one))
        peak = jnp.max(score, 0, keepdims=True)
        lifted = jnp.exp(score - peak)
        total = jnp.sum(lifted, 0, keepdims=True)
        mixed = matmul(v_turned[head * HD : (head + 1) * HD], lifted.astype(low_type))
        parts.append(mixed / total)
        lse_ref[0, head : head + 1, :] = peak + jnp.log(total)
    out_ref[...] = jnp.concatenate(parts, 0).T.astype(low_type)


def attend(queries, keys_values, bias, aside):
    groups, rows, width = queries.shape
    pairs = width // 128
    block = min(256, rows)
    grid = (groups * pairs, rows // block)
    (mixed, lse), extra = with_aside(
        attend_kernel,
        aside,
        grid=grid,
        in_specs=[
            pl.BlockSpec((1, block, 128), lambda p, i: (p // pairs, i, p % pairs)),
            pl.BlockSpec((1, CTX, 128), lambda p, i: (p // pairs, 0, p % pairs)),
            pl.BlockSpec((1, CTX, 128), lambda p, i: (p // pairs, 0, pairs + p % pairs)),
            pl.BlockSpec((CTX, 128), lambda p, i: (0, 0)),
        ],
        out_specs=[
            pl.BlockSpec((block, 128), lambda p, i: (i, p)),
            pl.BlockSpec((1, 2, block), lambda p, i: (p, 0, i)),
        ],
        out_shape=(
            jax.ShapeDtypeStruct((rows, groups * width), low_type),
            jax.ShapeDtypeStruct((groups * pairs, 2, rows), wide_type),
        ),
        cost=pl.CostEstimate(
            flops=4 * rows * CTX * groups * width, bytes_accessed=8 * rows * groups * width,
            transcendentals=rows * CTX * groups * width // HD),
        operands=(queries, keys_values, keys_values, bias),
    )
    return mixed, lse, extra


def attend_back_kernel(q_ref, k_ref, v_ref, bias_ref, g_ref, o_ref, lse_ref, gq_ref, gk_ref, gv_ref, k_sum, v_sum):
    step = pl.program_id(1)

    @pl.when(step == 0)
    def _():
        k_sum[...] = jnp.zeros_like(k_sum)
        v_sum[...] = jnp.zeros_like(v_sum)

    scale = HD ** -0.5
    q_block = q_ref[0] * jnp.asarray(scale, low_type)
    k_block, v_block, bias = k_ref[0], v_ref[0], bias_ref[...]
    g_block = g_ref[...]
    k_turned = k_block.T
    both = (g_block.astype(wide_type) * o_ref[...].astype(wide_type)).T
    parts = []
    for head in range(2):
        q_mine, q_one = head_lanes(q_block.shape, head)
        k_mine, _ = head_lanes(k_block.shape, head)
        nothing = jnp.zeros_like(q_block)
        one = jnp.where(q_one, jnp.ones_like(q_block), nothing)
        score = matmul_nt(jnp.where(k_mine, k_block, bias), jnp.where(q_mine, q_block, one))
        prob = jnp.exp(score - lse_ref[0, head : head + 1, :])
        g_mine = jnp.where(q_mine, g_block, nothing)
        grad_prob = matmul_nt(v_block, g_mine)
        inner = jnp.sum(both[head * HD : (head + 1) * HD], 0, keepdims=True)
        grad_score = (prob * (grad_prob - inner)).astype(low_type)
        v_sum[...] += matmul(prob.astype(low_type), g_mine)
        k_sum[...] += matmul(grad_score, jnp.where(q_mine, q_block, nothing))
        parts.append(matmul(k_turned[head * HD : (head + 1) * HD], grad_score) * scale)
    gq_ref[0] = jnp.concatenate(parts, 0).T.astype(low_type)

    @pl.when(step == pl.num_programs(1) - 1)
    def _():
        gk_ref[0] = k_sum[...].astype(low_type)
        gv_ref[0] = v_sum[...].astype(low_type)


def attend_back(queries, keys_values, bias, grad_mixed, mixed, lse, aside):
    groups, rows, width = queries.shape
    pairs = width // 128
    block = min(256, rows)
    grid = (groups * pairs, rows // block)
    row_spec = pl.BlockSpec((block, 128), lambda p, i: (i, p))
    key_out = pl.BlockSpec((1, CTX, 128), lambda p, i: (p // pairs, 0, p % pairs))
    grads, extra = with_aside(
        attend_back_kernel,
        aside,
        grid=grid,
        in_specs=[
            pl.BlockSpec((1, block, 128), lambda p, i: (p // pairs, i, p % pairs)),
            pl.BlockSpec((1, CTX, 128), lambda p, i: (p // pairs, 0, p % pairs)),
            pl.BlockSpec((1, CTX, 128), lambda p, i: (p // pairs, 0, pairs + p % pairs)),
            pl.BlockSpec((CTX, 128), lambda p, i: (0, 0)),
            row_spec,
            row_spec,
            pl.BlockSpec((1, 2, block), lambda p, i: (p, 0, i)),
        ],
        out_specs=[
            pl.BlockSpec((1, block, 128), lambda p, i: (p // pairs, i, p % pairs)),
            key_out,
            key_out,
        ],
        out_shape=(
            jax.ShapeDtypeStruct(queries.shape, low_type),
            jax.ShapeDtypeStruct((groups, CTX, width), low_type),
            jax.ShapeDtypeStruct((groups, CTX, width), low_type),
        ),
        scratch_shapes=[pltpu.VMEM((CTX, 128), wide_type)] * 2,
        cost=pl.CostEstimate(
            flops=10 * rows * CTX * groups * width, bytes_accessed=16 * rows * groups * width,
            transcendentals=rows * CTX * groups * width // HD),
        operands=(queries, keys_values, keys_values, bias, grad_mixed, mixed, lse),
    )
    return tuple(grads) + (extra,)


def grouped(rows, weight):
    return jnp.einsum("rd,gdc->grc", rows, weight, preferred_element_type=wide_type)


def layer_forward(residual, first, vec_rows, weights, bias, aside):
    w_joined, w_mix, w_grow, w_shrink = weights
    width = w_joined.shape[2] // 3
    normed = layer_norm(residual, vec_rows[0], vec_rows[1]).astype(low_type)
    queries = grouped(normed[first:], w_joined[:, :, :width]).astype(low_type)
    keys_values = grouped(normed[:CTX], w_joined[:, :, width:]).astype(low_type)
    mixed, lse, extra = attend(queries, keys_values, bias, aside)
    middle = residual[first:] + matmul(mixed, w_mix) + vec_rows[4]
    normed_mlp = layer_norm(middle, vec_rows[2], vec_rows[3]).astype(low_type)
    hidden = matmul(normed_mlp, w_grow)
    active = jax.nn.gelu(hidden).astype(low_type)
    output = middle + matmul(active, w_shrink) + vec_rows[5]
    return output, extra, (residual, normed, queries, keys_values, mixed, lse, middle, normed_mlp, hidden, active)


def layer_backward(upstream, kept, first, vec_rows, weights, bias, aside):
    w_joined, w_mix, w_grow, w_shrink = weights
    width = w_joined.shape[2] // 3
    residual, normed, queries, keys_values, mixed, lse, middle, normed_mlp, hidden, active = kept
    down_low = upstream.astype(low_type)
    grad_shrink = matmul_tn(active, down_low).astype(low_type)
    grad_hidden = gelu_back(hidden, matmul_nt(down_low, w_shrink)).astype(low_type)
    grad_grow = matmul_tn(normed_mlp, grad_hidden).astype(low_type)
    grad_middle, gain_mlp, shift_mlp = norm_back(
        middle, vec_rows[2], vec_rows[3], matmul_nt(grad_hidden, w_grow))
    grad_middle = grad_middle + upstream
    mix_low = grad_middle.astype(low_type)
    grad_mix = matmul_tn(mixed, mix_low).astype(low_type)
    grad_mixed = matmul_nt(mix_low, w_mix).astype(low_type)
    grad_q, grad_k, grad_v, extra = attend_back(queries, keys_values, bias, grad_mixed, mixed, lse, aside)

    def weight_grad(rows, grads):
        return jnp.einsum("rd,grc->gdc", rows, grads, preferred_element_type=wide_type).astype(low_type)

    def row_grad(grads, part):
        return jnp.einsum(
            "grc,gdc->rd", grads, w_joined[:, :, part * width : (part + 1) * width], preferred_element_type=wide_type)

    grad_joined = jnp.concatenate(
        [weight_grad(normed[first:], grad_q), weight_grad(normed[:CTX], grad_k), weight_grad(normed[:CTX], grad_v)], 2)
    from_q = row_grad(grad_q, 0)
    from_kv = row_grad(grad_k, 1) + row_grad(grad_v, 2)
    rows = residual.shape[0]
    below = jnp.zeros((first, from_q.shape[1]), wide_type)
    tail = jnp.zeros((rows - CTX, from_q.shape[1]), wide_type)
    grad_normed = jnp.concatenate([below, from_q], 0) + jnp.concatenate([from_kv, tail], 0)
    grad_input, gain_attn, shift_attn = norm_back(residual, vec_rows[0], vec_rows[1], grad_normed)
    vec_grads = [gain_attn, shift_attn, gain_mlp, shift_mlp, jnp.sum(grad_middle, 0), jnp.sum(upstream, 0)]
    grad_out = grad_input + jnp.concatenate([below, grad_middle], 0)
    return grad_out, extra, (grad_joined, grad_mix, grad_grow, grad_shrink), vec_grads


def update(weight, moment_old, average, grad_in, scale):
    applied = grad_in * scale + decay_wd * weight
    moment_new = moment * moment_old + applied
    weight_new = weight - rate * (applied + moment * moment_new)
    return (weight_new, moment_new, keep_avg * average + (1.0 - keep_avg) * weight_new)


BY_CORE = (True, True, False, False)
ROUTES = (("zxy",), ("zxy",), ("xzy",), ("yzx",))
HALVES = (("zxy", "zyx"),)


def whole_gather(shard_list, by_core):
    return [
        lax.all_gather(lax.all_gather(shard, "dp", axis=0), "head", axis=0 if bc else 1)
        for shard, bc in zip(shard_list, by_core)]


def as_blocks(grads, by_core, rows_list, routes):
    chips, cores = lax.axis_size("dp"), lax.axis_size("head")
    return [
        grad.reshape(((cores, chips) if bc else (chips, cores)) + (len(route), rows // len(route), -1))
        for grad, bc, rows, route in zip(grads, by_core, rows_list, routes)]


def whole_scatter(grads, by_core, rows_list):
    outs = []
    for grad, bc in zip(as_blocks(grads, by_core, rows_list, ROUTES + (("zyx",),)), by_core):
        half = lax.psum_scatter(grad.astype(wide_type), "head", scatter_dimension=0 if bc else 1)
        outs.append(lax.psum_scatter(half, "dp", scatter_dimension=0))
    return outs


def shards(
    rows_in, feat_mask, counts, ctx_vals, targets, query_mask,
    w_emb, m_emb, a_emb, vectors, m_vec, a_vec,
    w_qkv, m_qkv, a_qkv, w_out, m_out, a_out, w_up, m_up, a_up, w_down, m_down, a_down,
    w_head, m_head, a_head,
):
    chips, cores = lax.axis_size("dp"), lax.axis_size("head")
    direct = (chips, cores) == (16, 2)
    _, row_count, feat_count = rows_in.shape
    layer_total = w_qkv.shape[0]
    width = w_emb.shape[1]
    joined_rows = w_qkv.shape[1]
    kinds = w_qkv.shape[2] * w_qkv.shape[4]

    def own_weights(at):
        return [
            w_qkv[at].reshape((joined_rows, kinds)).astype(low_type)[None],
            w_out[at, 0].astype(low_type)[None],
            w_up[at].astype(low_type)[None],
            w_down[at].astype(low_type)[None],
        ]

    def as_weights(gathered):
        qkv, out, up, down = gathered
        return (
            qkv.reshape((cores, width, kinds)),
            out.reshape((width, width)),
            up.reshape((width, -1)),
            down.reshape((-1, width)),
        )

    own = [own_weights(at) for at in range(layer_total)]
    forward_aside = [None] * layer_total
    if direct:
        got = all_gather_layer(own[0] + own[1][:2], BY_CORE + BY_CORE[:2], ROUTES + (("zyx",), ("zyx",)), 1)
        gathered = [list(got[:4]), list(got[4:])]
        last_two = own[1][2:]
        forward_aside[0] = Aside(gather_plan(last_two, BY_CORE[2:], (("zxy",), ("zyx",))), last_two, 2)
    else:
        gathered = [whole_gather(o, BY_CORE) for o in own]

    table = lax.axis_index("dp") * cores + lax.axis_index("head")
    count = lax.dynamic_slice_in_dim(counts, table, 1, 0)
    bias = jnp.where(jnp.arange(CTX) < count, 0.0, -1e30).astype(low_type)
    bias = jnp.broadcast_to(bias[:, None], (CTX, 128))
    masked = rows_in[0] * feat_mask[0][None, :].astype(low_type)
    leading = jnp.concatenate([ctx_vals[0], jnp.zeros((row_count - CTX,), wide_type)])[:, None]
    residual = matmul(masked, w_emb.astype(low_type)) + vectors[1] + leading * vectors[0]
    kept_all = []
    weights = []
    for at in range(layer_total):
        first = CTX if at == layer_total - 1 else 0
        weights.append(as_weights(gathered[at]))
        residual, extra, kept = layer_forward(
            residual, first, vectors[2 + 6 * at : 8 + 6 * at], weights[at], bias, forward_aside[at])
        if extra is not None:
            gathered[at + 1] += list(extra)
        kept_all.append(kept)

    head_low = w_head.astype(low_type)
    final_rows = layer_norm(residual, vectors[-2], vectors[-1]).astype(low_type)
    logits = matmul(final_rows, head_low)
    row_peak = jnp.max(logits, -1, keepdims=True)
    log_total = row_peak[:, 0] + jnp.log(jnp.sum(jnp.exp(logits - row_peak), -1))
    target_hit = (jnp.arange(logits.shape[1])[None, :] == targets[0][:, None]).astype(wide_type)
    picked = jnp.sum(logits * target_hit, -1)
    row_weight = query_mask[0].astype(wide_type)
    loss_part = jnp.sum((log_total - picked) * row_weight)
    grad_logits = ((jnp.exp(logits - log_total[:, None]) - target_hit) * row_weight[:, None]).astype(low_type)
    grad_head = matmul_tn(final_rows, grad_logits).astype(low_type)
    upstream, gain_final, shift_final = norm_back(
        residual, vectors[-2], vectors[-1], matmul_nt(grad_logits, head_low))

    rows_list = [joined_rows, w_out.shape[2], w_up.shape[1], w_down.shape[1]]
    sums = [None] * layer_total
    vec_grads = [None] * layer_total
    aside = None
    for at in reversed(range(layer_total)):
        first = CTX if at == layer_total - 1 else 0
        upstream, extra, big, vec_grads[at] = layer_backward(
            upstream, kept_all[at], first, vectors[2 + 6 * at : 8 + 6 * at], weights[at], bias, aside)
        if extra is not None:
            sums[at + 1] = extra
        if at > 0 and direct:
            blocks = as_blocks(big, BY_CORE, rows_list, ROUTES)
            aside = Aside(reduce_plan(blocks, BY_CORE, ROUTES), blocks, 3)
        elif at > 0:
            sums[at] = whole_scatter(big, BY_CORE, rows_list)
    grad_emb = matmul_tn(masked, upstream.astype(low_type))
    vec_list = [jnp.sum(upstream * leading, 0), jnp.sum(upstream, 0)]
    for at in range(layer_total):
        vec_list = vec_list + vec_grads[at]
    grad_vec = jnp.stack(vec_list + [gain_final, shift_final])

    devices = chips * cores
    n_head, n_emb = w_head.size // (devices * 128), w_emb.size // (devices * 128)
    n_vec = -(-vectors.size // (devices * 128))
    vec_flat = jnp.pad(grad_vec.astype(low_type).reshape(-1), (0, n_vec * devices * 128 - vectors.size))
    used = n_head + n_emb + n_vec
    n_all = -(-(used + 1) // 32) * 32
    small = jnp.concatenate([
        grad_head.reshape((devices, n_head, 128)),
        grad_emb.astype(low_type).reshape((devices, n_emb, 128)),
        vec_flat.reshape((devices, n_vec, 128)),
        jnp.zeros((devices, n_all - used, 128), low_type)], 1)
    last_grads, last_rows, last_core = list(big) + [small], rows_list + [n_all], BY_CORE + (False,)
    if direct:
        routes = ROUTES + (("zyx",),)
        blocks = as_blocks(last_grads, last_core, last_rows, routes)
        *sums[0], small_sum = reduce_scatter_layer(blocks, last_core, routes, 4)
    else:
        *sums[0], small_sum = whole_scatter(last_grads, last_core, last_rows)
    small_sum = small_sum.reshape((n_all, 128))

    square = sum(jnp.sum(p * p) for ps in sums for p in ps) + jnp.sum(small_sum * small_sum)
    scalars = jnp.pad(jnp.stack([square, loss_part, jnp.sum(row_weight)]), (0, 125))
    small_sum = jnp.concatenate([small_sum[: n_all - 1], scalars[None]], 0)
    if direct:
        small_all = all_gather_layer([small_sum.reshape((2, n_all // 2, 128))], (False,), HALVES, 5)[0]
    else:
        small_all = whole_gather([small_sum], (False,))[0]
    small_all = small_all.reshape((devices, n_all, 128))
    totals = jnp.sum(small_all[:, n_all - 1, :3], 0)
    pooled = totals[2]
    loss = totals[1] / pooled
    grad_norm = jnp.sqrt(totals[0]) / pooled
    scale = jnp.minimum(1.0, clip_at / grad_norm) / pooled
    grad_head = small_all[:, :n_head].reshape(w_head.shape)
    grad_emb = small_all[:, n_head : n_head + n_emb].reshape(w_emb.shape)
    grad_vec = small_all[:, n_head + n_emb : used].reshape(-1)[: vectors.size].reshape(vectors.shape)

    def big_update(weight, moment_old, average, kind):
        grad = jnp.stack([sums[at][kind].reshape(weight.shape[1:]) for at in range(layer_total)])
        return update(weight, moment_old, average, grad, scale)

    e_w, e_m, e_a = update(w_emb, m_emb, a_emb, grad_emb, scale)
    v_w, v_m, v_a = update(vectors, m_vec, a_vec, grad_vec, scale)
    q_w, q_m, q_a = big_update(w_qkv, m_qkv, a_qkv, 0)
    o_w, o_m, o_a = big_update(w_out, m_out, a_out, 1)
    u_w, u_m, u_a = big_update(w_up, m_up, a_up, 2)
    d_w, d_m, d_a = big_update(w_down, m_down, a_down, 3)
    h_w, h_m, h_a = update(w_head, m_head, a_head, grad_head, scale)
    return (
        loss, grad_norm, e_w, e_m, e_a, v_w, v_m, v_a, q_w, q_m, q_a, o_w, o_m, o_a,
        u_w, u_m, u_a, d_w, d_m, d_a, h_w, h_m, h_a,
    )


def solution(mesh):
    tables = [P(("dp", "head"), None, None)] + [P(("dp", "head"), None)] + [P()] + [P(("dp", "head"), None)] * 3
    joined = P(None, "dp", None, "head", None)
    mixed = P(None, "head", "dp", None)
    wide = P(None, ("dp", "head"), None)
    state = [P()] * 6 + [joined] * 3 + [mixed] * 3 + [wide] * 6 + [P()] * 3
    return jax.shard_map(
        shards, mesh=mesh, in_specs=tuple(tables + state), out_specs=tuple([P(), P()] + state), check_vma=False)
```

time: 804 us -> 713 us (0.89)
  Pallas kernels: 512 us -> 400 us
  matrix products: 149 us -> 159 us
    pallas_call x9 -> x7, Pallas kernels: 512 us -> 400 us  [the longest x3 222 us: exchange(): pl.pallas_call(kernel, out_shape=tuple(plan.out_shape()), in_specs=plan.i...]
    dot_general x15, matrix products: 77 us -> 88.6 us  [contract(): lax.dot_general(first_op, second_op, (((first_dim,), (second_dim,)), ((),...]
    reduce_sum x11 -> x10, other arithmetic: 16.7 us -> 11.5 us  [the longest x8 9 us: shards(): jnp.sum(p * p)]
where the time goes in v2:
time: 713 us; the launch traced here: 705 us
  Pallas kernels  400 us (56%)
  matrix products  159 us (22%)
  other arithmetic  73.9 us (10%)
  local copies, waits for them, and re-layouts  56.5 us (8%)
  between operations  15 us (2%)
    pallas_call x3, Pallas kernels, exchange(): pl.pallas_call(kernel, out_shape=tuple(plan.out_shape()), in_specs=plan.i...  222 us
    pallas_call x2, Pallas kernels, with_aside(): pl.pallas_call(kernel, grid=grid, in_specs=list(in_specs) + plan.in_specs...  158 us
    dot_general x15, matrix products, contract(): lax.dot_general(first_op, second_op, (((first_dim,), (second_dim,)), ((),...  88.6 us
    dot_general x8, matrix products, matmul(): return jnp.dot(first_op, second_op, preferred_element_type=wide_type)  35.4 us
    pallas_call x2, Pallas kernels, with_aside(): pl.pallas_call(body, grid=grid, in_specs=in_specs, out_specs=out_specs, o...  19.9 us
    dot_general x6, matrix products, row_grad(): jnp.einsum('grc,gdc->rd', grads, w_joined[:, :, part * width:(part + 1) *...  15.6 us

profile of v2, /device:TPU:0, one launch (start us, length us, event | category | flops | bytes accessed | tf_op | source)
XLA Modules:
  0.0 704.6 jit_solution(8890056317964250566)
XLA Ops:
  7.3 2.1 slice_reduce_fusion.4
  21.4 1.6 add_convert_fusion.2
  23.1 79.8 %shard_map.434 = (bf16[2,16,1,48,1152]{4,3,2,1,0:T(8,128)(2,1)}, bf16[2,16,1,24,768]{4,3,2,1,0:T(8,128)(2,1)}, bf16[16,2,1,24,3072]{4,3,2,1,0:T(8,128)(2,1)}, bf...) custom-call(bf16[1,48,1152]{2,1,0:T(8,128)(2,1)} %convert_element_typ, ...), custom_call_target="tpu_custom_call" | custom-call | bytes 18874368 | tf_op jit(solution)/shard_map/pallas_call | solution.py:477
  102.9 4.5 fusion.30.refs_0_
  107.4 3.5 convert_bitcast_fusion.1.refs_1_.refs_2_
  111.0 66.7 %shard_map.435 = (bf16[1024,768]{1,0:T(8,128)(2,1)}, f32[6,2,1024]{2,1,0:T(2,128)}, bf16[16,2,1,24,3072]{4,3,2,1,0:T(8,128)(2,1)}, bf16[16,2,1,96,768]{4,3,2,1,0:T(8,128)(2,1)}) custom-call(bf16[2,1024,384]{2,1,0:T(8,128)(2,1)} %fusion.30.refs_0_, bf16[2,768,768]{2,1,0:T(8,128)(2,1)} %convert_bitcast_fusion.1.refs_1_.refs_2_, ...), custom_call_target="tpu_custom_call" | custom-call | flops 2415919104 | bytes 6291456 | tf_op jit(solution)/shard_map/pallas_call | solution.py:458
  177.7 4.5 fusion.101
  183.9 8.6 %fusion.90 = f32[1024,3072]{1,0:T(8,128)} fusion(bf16[768,3072]{1,0:T(8,128)(2,1)S(1)} %bitcast.188, f32[1024,768]{0,1:T(8,128)S(1)} %get-tuple-element.204, f32[768]{0:T(1024)S(1)} %copy-done.69, f32[768]{0:T(1024)S(1)} %copy-done.63, f32[1024]{0:T(1024)S(1)} %fusion.79, f32[1024]{0:T(1024)S(1)} %broadcast_multiply_fusion.1), kind=kOutput, calls=%fused_computation.261 | convolution fusion | flops 4835770368 | bytes 20461568 | tf_op jit(solution)/shard_map/dot_general | solution.py:535
  192.6 11.8 %fusion.102 = (f32[1024]{0:T(1024)S(1)}, f32[1024,768]{0,1:T(8,128)S(1)}) fusion(f32[768]{0:T(1024)S(1)} %copy-done.118, f32[1024,768]{0,1:T(8,128)S(1)} %get-tuple-element.204, bf16[3072,768]{1,0:T(8,128)(2,1)S(1)} %bitcast.217, f32[1024,3072]{1,0:T(8,128)} %fusion.90), kind=kOutput, calls=%fused_computation.273 | convolution fusion | flops 4862508032 | bytes 23600128 | tf_op jit(solution)/shard_map/dot_general | solution.py:535
  206.0 1.5 copy-done.32
  208.8 3.5 convert_bitcast_fusion.k_ref.v_ref
  212.3 10.4 %shard_map.436 = (bf16[256,768]{1,0:T(8,128)(2,1)}, f32[6,2,256]{2,1,0:T(2,128)}) custom-call(bf16[2,256,384]{2,1,0:T(8,128)(2,1)} %fusion.46.q_ref, bf16[2,768,768]{2,1,0:T(8,128)(2,1)} %convert_bitcast_fusion.k_ref.v_ref, bf16[2,768,768]{2,1,0:T(8,128)(2,1)} %convert_bitcast_fusion.k_ref.v_ref, bf16[768,128]{1,0:T(8,128)(2,1)} %broadcast_in_dim.36.refs_3_.bias_ref), custom_call_target="tpu_custom_call" | custom-call | flops 603979776 | bytes 1572864 | tf_op jit(solution)/shard_map/pallas_call | solution.py:420
  222.7 2.4 fusion.103
  226.0 4.0 fusion.89
  230.0 2.5 fusion.104
  234.6 1.4 convolution_convert_fusion.13
  236.0 2.3 concatenate.62
  238.3 2.4 fusion.108
  241.3 1.4 copy.173
  244.8 7.4 %fusion.13 = bf16[256,3072]{1,0:T(8,128)(2,1)S(1)} fusion(f32[256,3072]{1,0:T(8,128)} %copy-done.20, bf16[3072,768]{1,0:T(8,128)(2,1)} %bitcast.220, f32[256,768]{0,1:T(8,128)S(1)} %get-tuple-element.186, f32[256]{0:T(256)S(1)} %negate_multiply_fusion.4), kind=kOutput, calls=%fused_computation.27 | convolution fusion | flops 1224081408 | bytes 10224640 | tf_op jit(solution)/shard_map/dot_general | solution.py:539
  252.2 2.4 fusion.107
  255.2 1.4 copy.174
  260.6 1.7 fusion.93
  264.5 9.5 %shard_map.437 = (bf16[2,256,384]{2,1,0:T(8,128)(2,1)}, bf16[2,768,384]{2,1,0:T(8,128)(2,1)}, bf16[2,768,384]{2,1,0:T(8,128)(2,1)}) custom-call(bf16[2,256,384]{2,1,0:T(8,128)(2,1)} %fusion.46.q_ref, bf16[2,768,768]{2,1,0:T(8,128)(2,1)} %convert_bitcast_fusion.k_ref.v_ref, bf16[2,768,768]{2,1,0:T(8,128)(2,1)} %convert_bitcast_fusion.k_ref.v_ref, ...), custom_call_target="tpu_custom_call" | custom-call | flops 1509949440 | bytes 3145728 | tf_op jit(solution)/shard_map/pallas_call | solution.py:420
  276.5 6.7 convolution_convert_fusion.2
  283.3 2.8 convolution_bitcast_fusion
  286.6 1.5 convolution_convert_fusion.9
  290.9 4.0 copy.186
  294.9 2.8 fusion.51
  297.8 2.6 bitcast_add_fusion.2
  302.4 4.3 fusion.95
  307.3 18.5 %fusion.6 = bf16[1024,3072]{1,0:T(8,128)(2,1)} fusion(f32[1024,3072]{1,0:T(8,128)} %fusion.90, bf16[3072,768]{1,0:T(8,128)(2,1)} %bitcast.214, f32[256,768]{0,1:T(8,128)} %copy-done.12, f32[1024,768]{0,1:T(8,128)} %get-tuple-element.184, f32[1024]{0:T(1024)S(1)} %negate_multiply_fusion.2), kind=kOutput, calls=%fused_computation.8 | convolution fusion | flops 4897112064 | bytes 27529216 | tf_op jit(solution)/shard_map/dot_general | solution.py:539
  325.8 13.5 %convolution_convert_fusion = bf16[3072,768]{1,0:T(8,128)(2,1)} fusion(f32[256,768]{0,1:T(8,128)S(1)} %copy-done.14, f32[1024,768]{0,1:T(8,128)S(1)} %copy-done.11, f32[1024]{0:T(1024)S(1)} %negate_multiply_fusion.2, f32[1024,3072]{1,0:T(8,128)} %fusion.90), kind=kOutput, calls=%fused_computation.10 | convolution fusion | flops 4864868352 | bytes 21237760 | tf_op jit(solution)/shard_map/dot_general | solution.py:539
  339.3 9.2 %fusion.106 = (bf16[768]{0:T(1024)(128)(2,1)S(1)}, f32[1024,768]{1,0:T(8,128)}) fusion(bf16[1024,3072]{1,0:T(8,128)(2,1)S(1)} %copy-done.124, bf16[768,3072]{1,0:T(8,128)(2,1)} %bitcast.185), kind=kOutput, calls=%fused_computation.277 | convolution fusion | flops 4832623616 | bytes 14157312 | tf_op jit(solution)/shard_map/dot_general | solution.py:539
  348.6 7.1 %convolution_convert_fusion.1 = bf16[768,3072]{1,0:T(8,128)(2,1)} fusion(bf16[1024,3072]{1,0:T(8,128)(2,1)S(1)} %copy-done.124, f32[1024,768]{0,1:T(8,128)S(1)} %copy-done.3, f32[768]{0:T(1024)S(1)} %copy-done.70, f32[768]{0:T(1024)S(1)} %copy-done.64, f32[1024]{0:T(1024)S(1)} %copy-done.66, f32[1024]{0:T(1024)S(1)} %copy-done.56), kind=kOutput, calls=%fused_computation.11 | convolution fusion | flops 4838129664 | bytes 14170112 | tf_op jit(solution)/shard_map/dot_general | solution.py:539
  356.3 5.3 convolution_convert_fusion.3
  361.7 3.8 copy.179
  365.5 2.5 multiply_reduce_fusion.5
  370.1 5.0 fusion.94
  376.3 4.8 convolution_convert_fusion.4.refs_4_
  381.1 91.7 %shard_map.438 = (bf16[2,1024,384]{2,1,0:T(8,128)(2,1)}, bf16[2,768,384]{2,1,0:T(8,128)(2,1)}, bf16[2,768,384]{2,1,0:T(8,128)(2,1)}, f32[1,48,1152]{2,1,0:T(8,12...) custom-call(bf16[2,1024,384]{2,1,0:T(8,128)(2,1)} %fusion.30.refs_0_, ...), custom_call_target="tpu_custom_call" | custom-call | flops 6039797760 | bytes 12582912 | tf_op jit(solution)/shard_map/pallas_call | solution.py:458
  472.9 5.0 convolution_convert_fusion.6
  482.2 1.4 fusion.34
  486.4 4.1 copy.193
  490.5 2.9 fusion.48
  495.9 3.4 fusion.91
  499.3 3.1 multiply_reduce_fusion.2
  502.6 5.4 fusion.92
  508.4 2.1 fusion.53
  510.7 2.5 maximum_maximum_fusion.refs_4_
  513.1 103.9 %shard_map.439 = (f32[1,48,1152]{2,1,0:T(8,128)}, f32[1,24,768]{2,1,0:T(8,128)}, f32[1,24,3072]{2,1,0:T(8,128)}, f32[1,96,768]{2,1,0:T(8,128)}, f32[1,128,128]{2,1,0:T(8,128)}) custom-call(bf16[2,16,1,48,1152]{4,3,2,1,0:T(8,128)(2,1)} %bitcast.175, bf16[2,16,1,24,768]{4,3,2,1,0:T(8,128)(2,1)} %bitcast.204, bf16[16,2,1,24,3072]{4,3,2,1,0:T(8,128)(2,1)} %bitcast.193, ...), custom_call_target="tpu_custom_call" | custom-call | bytes 486539264 | tf_op jit(solution)/shard_map/pallas_call | solution.py:477
  617.1 1.6 multiply_reduce_fusion.18
  618.7 1.6 multiply_reduce_fusion.19
  620.4 1.5 multiply_reduce_fusion.23
  621.9 1.6 multiply_reduce_fusion.21
  628.7 1.5 multiply_reduce_fusion.24
  635.4 38.2 %shard_map.440 = f32[16,2,2,64,128]{4,3,2,1,0:T(8,128)} custom-call(f32[2,64,128]{2,1,0:T(8,128)} %bitcast.207), custom_call_target="tpu_custom_call" | custom-call | bytes 1048576 | tf_op jit(solution)/shard_map/pallas_call | solution.py:477
  680.3 1.5 multiply_add_fusion.13
  681.8 1.9 multiply_add_fusion.11
  686.1 1.8 mul.913
  687.9 2.2 multiply_add_fusion.8
  690.2 1.6 fusion.65
  695.5 1.4 multiply_add_fusion.6
  699.1 2.8 multiply_add_fusion.1
  (390 shorter events, 73.0 us)
Async XLA Ops:
  0.7 14.8 %copy-start.26 = (f32[2,48,3,1,384]{4,3,2,1,0:T(1,128)S(1)}, f32[2,48,3,1,384]{4,3,2,1,0:T(1,128)}, u32[]{:S(2)}) copy-start(f32[2,48,3,1,384]{4,3,2,1,0:T(1,128)} %param.39) | copy-start | bytes 1327108
  0.7 17.8 %copy-start.35 = (f32[128,768]{1,0:T(8,128)S(1)}, f32[128,768]{1,0:T(8,128)}, u32[]{:S(2)}) copy-start(f32[128,768]{1,0:T(8,128)} %param.33) | copy-start | bytes 1179652
  0.7 17.8 %copy-start.51 = (bf16[1,1024,128]{2,1,0:T(8,128)(2,1)S(1)}, bf16[1,1024,128]{2,1,0:T(8,128)(2,1)}, u32[]{:S(2)}) copy-start(bf16[1,1024,128]{2,1,0:T(8,128)(2,1)} %param.27) | copy-start | bytes 786436
  4.0 15.2 %copy-start.119 = (bf16[128]{0:T(256)(128)(2,1)}, bf16[128]{0:T(256)(128)(2,1)S(1)}, u32[]{:S(2)}) copy-start(bf16[128]{0:T(256)(128)(2,1)S(1)} %convert_bitcast_fusion.2) | copy-start | bytes 772
  7.3 11.9 %copy-start.97 = (f32[1024]{0:T(1024)}, f32[1024]{0:T(1024)S(1)}, u32[]{:S(2)}) copy-start(f32[1024]{0:T(1024)S(1)} %concatenate.56) | copy-start | bytes 12292
  9.3 11.1 %copy-start.74 = (f32[768]{0:T(1024)}, f32[768]{0:T(1024)S(1)}, u32[]{:S(2)}) copy-start(f32[768]{0:T(1024)S(1)} %get-tuple-element.155) | copy-start | bytes 9220
  177.7 6.2 slice-start.2
  177.7 6.2 slice-start.3
  182.2 10.3 %copy-start.2 = (f32[1024,768]{0,1:T(8,128)}, f32[1024,768]{0,1:T(8,128)S(1)}, u32[]{:S(2)}) copy-start(f32[1024,768]{0,1:T(8,128)S(1)} %get-tuple-element.204) | copy-start | bytes 9437188
  182.3 10.3 %slice-start.4 = ((s8[4718592]{0:T(1024)(128)(4,1)}), s8[4194304]{0:T(1024)(128)(4,1)S(1)}, s32[]{:S(2)}) async-start(s8[4718592]{0:T(1024)(128)(4,1)} %bitcast.215), calls=%async_computation.4 | async-start | bytes 8388608
  183.9 8.6 %copy-start.118 = (f32[768]{0:T(1024)S(1)}, f32[768]{0:T(1024)}, u32[]{:S(2)}) copy-start(f32[768]{0:T(1024)} %get-tuple-element.150) | copy-start | bytes 9220
  183.9 8.6 %slice-start.5 = ((s8[4718592]{0:T(1024)(128)(4,1)}), s8[524288]{0:T(1024)(128)(4,1)S(1)}, s32[]{:S(2)}) async-start(s8[4718592]{0:T(1024)(128)(4,1)} %bitcast.215), calls=%async_computation.5 | async-start | bytes 1048576
  222.7 7.2 %slice-start.6 = ((s8[4718592]{0:T(1024)(128)(4,1)}), s8[4194304]{0:T(1024)(128)(4,1)S(1)}, s32[]{:S(2)}) async-start(s8[4718592]{0:T(1024)(128)(4,1)} %bitcast.221), calls=%async_computation.6 | async-start | bytes 8388608
  225.1 35.4 %copy-start.7 = (f32[256,768]{0,1:T(8,128)}, f32[256,768]{0,1:T(8,128)S(1)}, u32[]{:S(2)}) copy-start(f32[256,768]{0,1:T(8,128)S(1)} %get-tuple-element.208) | copy-start | bytes 2359300
  225.2 35.4 %copy-start.79 = (f32[256]{0:T(256)}, f32[256]{0:T(256)S(1)}, u32[]{:S(2)}) copy-start(f32[256]{0:T(256)S(1)} %broadcast_multiply_fusion.4) | copy-start | bytes 3076
  226.0 34.6 %copy-start.87 = (f32[256]{0:T(256)}, f32[256]{0:T(256)S(1)}, u32[]{:S(2)}) copy-start(f32[256]{0:T(256)S(1)} %fusion.81) | copy-start | bytes 3076
  232.6 10.1 %copy-start.96 = (f32[256]{0:T(256)}, f32[256]{0:T(256)S(1)}, u32[]{:S(2)}) copy-start(f32[256]{0:T(256)S(1)} %broadcast_multiply_fusion.3) | copy-start | bytes 3076
  232.8 9.9 %copy-start.99 = (f32[256]{0:T(256)}, f32[256]{0:T(256)S(1)}, u32[]{:S(2)}) copy-start(f32[256]{0:T(256)S(1)} %fusion.82) | copy-start | bytes 3076
  243.7 8.5 %slice-start = ((s8[4718592]{0:T(1024)(128)(4,1)}), s8[4194304]{0:T(1024)(128)(4,1)S(1)}, s32[]{:S(2)}) async-start(s8[4718592]{0:T(1024)(128)(4,1)} %bitcast.177), calls=%async_computation | async-start | bytes 8388608
  244.8 15.8 %copy-start.21 = (f32[256,768]{0,1:T(8,128)}, f32[256,768]{0,1:T(8,128)S(1)}, u32[]{:S(2)}) copy-start(f32[256,768]{0,1:T(8,128)S(1)} %get-tuple-element.186) | copy-start | bytes 2359300
  244.8 7.4 %copy-start.116 = (f32[256]{0:T(256)}, f32[256]{0:T(256)S(1)}, u32[]{:S(2)}) copy-start(f32[256]{0:T(256)S(1)} %negate_multiply_fusion.4) | copy-start | bytes 3076
  244.8 7.4 %slice-start.1 = ((s8[4718592]{0:T(1024)(128)(4,1)}), s8[524288]{0:T(1024)(128)(4,1)S(1)}, s32[]{:S(2)}) async-start(s8[4718592]{0:T(1024)(128)(4,1)} %bitcast.177), calls=%async_computation.1 | async-start | bytes 1048576
  256.6 6.6 copy-start.18
  276.5 6.7 copy-start.37
  276.5 9.5 %copy-start.23 = (bf16[1024,768]{0,1:T(8,128)(2,1)S(1)}, bf16[1024,768]{0,1:T(8,128)(2,1)}, u32[]{:S(2)}) copy-start(bf16[1024,768]{0,1:T(8,128)(2,1)} %copy-done.22) | copy-start | bytes 4718596
  307.3 18.5 %copy-start.11 = (f32[1024,768]{0,1:T(8,128)S(1)}, f32[1024,768]{0,1:T(8,128)}, u32[]{:S(2)}) copy-start(f32[1024,768]{0,1:T(8,128)} %get-tuple-element.184) | copy-start | bytes 9437188
  307.3 18.5 %copy-start.14 = (f32[256,768]{0,1:T(8,128)S(1)}, f32[256,768]{0,1:T(8,128)}, u32[]{:S(2)}) copy-start(f32[256,768]{0,1:T(8,128)} %copy-done.12) | copy-start | bytes 2359300
  325.8 13.6 %copy-start.124 = (bf16[1024,3072]{1,0:T(8,128)(2,1)S(1)}, bf16[1024,3072]{1,0:T(8,128)(2,1)}, u32[]{:S(2)}) copy-start(bf16[1024,3072]{1,0:T(8,128)(2,1)} %fusion.6) | copy-start | bytes 18874372
  339.3 9.3 %copy-start.3 = (f32[1024,768]{0,1:T(8,128)S(1)}, f32[1024,768]{0,1:T(8,128)}, u32[]{:S(2)}) copy-start(f32[1024,768]{0,1:T(8,128)} %copy-done.2) | copy-start | bytes 9437188
  339.3 9.3 %copy-start.56 = (f32[1024]{0:T(1024)S(1)}, f32[1024]{0:T(1024)}, u32[]{:S(2)}) copy-start(f32[1024]{0:T(1024)} %copy-done.55) | copy-start | bytes 12292
  339.3 9.3 %copy-start.64 = (f32[768]{0:T(1024)S(1)}, f32[768]{0:T(1024)}, u32[]{:S(2)}) copy-start(f32[768]{0:T(1024)} %get-tuple-element.152) | copy-start | bytes 9220
  339.3 9.3 %copy-start.66 = (f32[1024]{0:T(1024)S(1)}, f32[1024]{0:T(1024)}, u32[]{:S(2)}) copy-start(f32[1024]{0:T(1024)} %copy-done.65) | copy-start | bytes 12292
  339.3 9.3 %copy-start.70 = (f32[768]{0:T(1024)S(1)}, f32[768]{0:T(1024)}, u32[]{:S(2)}) copy-start(f32[768]{0:T(1024)} %get-tuple-element.151) | copy-start | bytes 9220
  348.6 7.7 %copy-start.58 = (f32[768]{0:T(1024)S(1)}, f32[768]{0:T(1024)}, u32[]{:S(2)}) copy-start(f32[768]{0:T(1024)} %get-tuple-element.146) | copy-start | bytes 9220
  348.6 7.7 %copy-start.68 = (f32[768]{0:T(1024)S(1)}, f32[768]{0:T(1024)}, u32[]{:S(2)}) copy-start(f32[768]{0:T(1024)} %get-tuple-element.145) | copy-start | bytes 9220
  348.6 7.7 %copy-start.80 = (f32[256]{0:T(256)S(1)}, f32[256]{0:T(256)}, u32[]{:S(2)}) copy-start(f32[256]{0:T(256)} %copy-done.79) | copy-start | bytes 3076
  348.6 7.7 %copy-start.88 = (f32[256]{0:T(256)S(1)}, f32[256]{0:T(256)}, u32[]{:S(2)}) copy-start(f32[256]{0:T(256)} %copy-done.87) | copy-start | bytes 3076
  472.9 5.0 copy-start.41
  472.9 5.7 copy-start.43
  472.9 6.4 copy-start.71
  472.9 7.0 copy-start.54
  472.9 9.3 %copy-start.30 = (bf16[2,1024,384]{2,1,0:T(8,128)(2,1)S(1)}, bf16[2,1024,384]{2,1,0:T(8,128)(2,1)}, u32[]{:S(2)}) copy-start(bf16[2,1024,384]{2,1,0:T(8,128)(2,1)} %get-tuple-element.65) | copy-start | bytes 4718596
  472.9 9.3 %copy-start.34 = (bf16[1024,768]{0,1:T(8,128)(2,1)S(1)}, bf16[1024,768]{0,1:T(8,128)(2,1)}, u32[]{:S(2)}) copy-start(bf16[1024,768]{0,1:T(8,128)(2,1)} %add_convert_fusion.2) | copy-start | bytes 4718596
  502.4 5.7 copy-start.113
  502.4 5.7 copy-start.112
  502.5 5.7 copy-start.115
  502.5 5.7 copy-start.114
  502.5 5.7 copy-start.110
  502.5 5.7 copy-start.111
  502.5 5.7 copy-start.107
  502.5 5.7 copy-start.106
  502.5 5.7 copy-start.109
  502.5 5.8 copy-start.108
  502.6 5.8 copy-start.105
  502.6 5.8 copy-start.104
  502.6 5.8 copy-start.52
  502.6 5.8 copy-start.120
  502.6 8.1 %copy-start.121 = (bf16[128]{0:T(256)(128)(2,1)S(1)}, bf16[128]{0:T(256)(128)(2,1)}, u32[]{:S(2)}) copy-start(bf16[128]{0:T(256)(128)(2,1)} %pad.26.clone) | copy-start | bytes 772
  673.6 11.2 %copy-start.16 = (f32[16,2,2,64,128]{4,3,2,1,0:T(8,128)S(1)}, f32[16,2,2,64,128]{4,3,2,1,0:T(8,128)}, u32[]{:S(2)}) copy-start(f32[16,2,2,64,128]{4,3,2,1,0:T(8,128)} %shard_map.440) | copy-start | bytes 6291460
  690.2 5.3 copy-start.24
  690.2 5.3 copy-start.44
  690.2 5.3 copy-start.46
  690.2 5.3 copy-start.59
  690.2 5.3 copy-start.60
  (69 other events, 168.0 us)

commit v3 on v2

--- a/solution.py
+++ b/solution.py
@@ -685,36 +685,187 @@
     return jnp.einsum("rd,gdc->grc", rows, weight, preferred_element_type=wide_type)
 
 
-def layer_forward(residual, first, vec_rows, weights, bias, aside):
-    w_joined, w_mix, w_grow, w_shrink = weights
+GELU_K = 0.7978845608028654
+GELU_C = 0.044715
+
+
+def center_scale(values):
+    center = values - jnp.mean(values, -1, keepdims=True)
+    return center, lax.rsqrt(jnp.mean(center * center, -1, keepdims=True) + eps_norm)
+
+
+def mlp_kernel(res_ref, mixed_ref, mix_ref, up_ref, down_ref, vec_ref, out_ref, middle_ref, hidden_ref, normed, total):
+    step, last = pl.program_id(1), pl.num_programs(1) - 1
+    size = hidden_ref.shape[1]
+
+    @pl.when(step == 0)
+    def _():
+        middle = res_ref[...] + matmul(mixed_ref[...], mix_ref[...]) + vec_ref[4:5]
+        middle_ref[...] = middle
+        center, spread = center_scale(middle)
+        normed[...] = (center * spread * vec_ref[2:3] + vec_ref[3:4]).astype(low_type)
+        total[...] = middle + vec_ref[5:6]
+
+    part = pl.ds(pl.multiple_of(step * size, size), size)
+    hidden = matmul(normed[...], up_ref[:, part])
+    hidden_ref[...] = hidden.astype(low_type)
+    inner = jnp.tanh(GELU_K * (hidden + GELU_C * hidden * hidden * hidden))
+    active = (0.5 * hidden * (1.0 + inner)).astype(low_type)
+    total[...] += matmul(active, down_ref[part, :])
+
+    @pl.when(step == last)
+    def _():
+        out_ref[...] = total[...]
+
+
+def mlp_forward(residual, first, mixed, weights, vec_rows, aside):
+    _, w_mix, w_grow, w_shrink = weights
+    rows, width = mixed.shape
+    wide = w_grow.shape[1]
+    block, chunk = 256, 512
+    skip = first // block
+
+    def whole(a):
+        return pl.BlockSpec(a.shape, lambda i, j: (0, 0), pipeline_mode=pl.Buffered(1))
+
+    row_spec = pl.BlockSpec((block, width), lambda i, j: (i, 0))
+    outs, extra = with_aside(
+        mlp_kernel,
+        aside,
+        grid=(rows // block, wide // chunk),
+        in_specs=[
+            pl.BlockSpec((block, width), lambda i, j: (i + skip, 0)), row_spec,
+            whole(w_mix), whole(w_grow), whole(w_shrink), whole(vec_rows),
+        ],
+        out_specs=[row_spec, row_spec, pl.BlockSpec((block, chunk), lambda i, j: (i, j))],
+        out_shape=(
+            jax.ShapeDtypeStruct((rows, width), wide_type),
+            jax.ShapeDtypeStruct((rows, width), wide_type),
+            jax.ShapeDtypeStruct((rows, wide), low_type),
+        ),
+        scratch_shapes=[pltpu.VMEM((block, width), low_type), pltpu.VMEM((block, width), wide_type)],
+        cost=pl.CostEstimate(
+            flops=2 * rows * width * (2 * wide + width), bytes_accessed=rows * width * 24, transcendentals=rows * wide),
+        operands=(residual, mixed, w_mix, w_grow, w_shrink, vec_rows),
+    )
+    return outs, extra
+
+
+def mlp_back_kernel(
+    u_ref, middle_ref, mixed_ref, mix_ref, up_ref, down_ref, vec_ref, hidden_ref,
+    up_grad_ref, down_grad_ref, mix_grad_ref, mixed_grad_ref, mid_grad_ref, vec_grad_ref,
+    u_low, normed_turned, normed_grad,
+):
+    step, last = pl.program_id(0), pl.num_programs(0) - 1
+    rows, width = u_ref.shape
+    block = 256
+
+    @pl.when(step == 0)
+    def _():
+        @pl.loop(0, rows // block)
+        def _(i):
+            part = pl.ds(pl.multiple_of(i * block, block), block)
+            center, spread = center_scale(middle_ref[part, :])
+            normed = (center * spread * vec_ref[2:3] + vec_ref[3:4]).astype(low_type)
+            normed_turned[:, part] = normed.T
+            u_low[part, :] = u_ref[part, :].astype(low_type)
+            normed_grad[part, :] = jnp.zeros((block, width), wide_type)
+
+    hidden = hidden_ref[...].astype(wide_type)
+    square = hidden * hidden
+    inner = jnp.tanh(GELU_K * hidden * (1.0 + GELU_C * square))
+    half = 0.5 * (1.0 + inner)
+    active = (hidden * half).astype(low_type)
+    slope = half + 0.5 * hidden * (1.0 - inner * inner) * (GELU_K * (1.0 + 3.0 * GELU_C * square))
+    grad = (matmul_nt(u_low[...], down_ref[...]) * slope).astype(low_type)
+    down_grad_ref[...] = matmul(active.T, u_low[...]).astype(low_type)
+    up_grad_ref[...] = matmul(normed_turned[...], grad).astype(low_type)
+    normed_grad[...] += matmul_nt(grad, up_ref[...])
+
+    @pl.when(step == last)
+    def _():
+        vec_grad_ref[...] = jnp.zeros_like(vec_grad_ref)
+
+        @pl.loop(0, rows // block)
+        def _(i):
+            part = pl.ds(pl.multiple_of(i * block, block), block)
+            center, spread = center_scale(middle_ref[part, :])
+            shape = center * spread
+            grads = normed_grad[part, :]
+            scaled = grads * vec_ref[2:3]
+            from_norm = spread * (
+                scaled - jnp.mean(scaled, -1, keepdims=True) - shape * jnp.mean(scaled * shape, -1, keepdims=True))
+            u_part = u_ref[part, :]
+            total = from_norm + u_part
+            mid_grad_ref[part, :] = total
+            vec_grad_ref[0:1] += jnp.sum(grads * shape, 0, keepdims=True)
+            vec_grad_ref[1:2] += jnp.sum(grads, 0, keepdims=True)
+            vec_grad_ref[2:3] += jnp.sum(total, 0, keepdims=True)
+            vec_grad_ref[3:4] += jnp.sum(u_part, 0, keepdims=True)
+            low = total.astype(low_type)
+            u_low[part, :] = low
+            mixed_grad_ref[part, :] = matmul_nt(low, mix_ref[...]).astype(low_type)
+            normed_turned[:, part] = mixed_ref[part, :].T
+        mix_grad_ref[...] = matmul(normed_turned[...], u_low[...]).astype(low_type)
+
+
+def mlp_backward(upstream, middle, mixed, weights, vec_rows, hidden, aside):
+    _, w_mix, w_grow, w_shrink = weights
+    rows, width = upstream.shape
+    wide = hidden.shape[1]
+    chunk = 256
+
+    def whole(shape):
+        return pl.BlockSpec(shape, lambda j: (0, 0), pipeline_mode=pl.Buffered(1))
+
+    square, row_shape = (width, width), (rows, width)
+    up_spec = pl.BlockSpec((width, chunk), lambda j: (0, j))
+    down_spec = pl.BlockSpec((chunk, width), lambda j: (j, 0))
+    return with_aside(
+        mlp_back_kernel,
+        aside,
+        grid=(wide // chunk,),
+        in_specs=[
+            whole(row_shape), whole(row_shape), whole(row_shape), whole(square), up_spec, down_spec,
+            whole(vec_rows.shape), pl.BlockSpec((rows, chunk), lambda j: (0, j)),
+        ],
+        out_specs=[up_spec, down_spec] + [
+            pl.BlockSpec(s, lambda j: (0, 0)) for s in (square, row_shape, row_shape, (8, width))],
+        out_shape=(
+            jax.ShapeDtypeStruct((width, wide), low_type),
+            jax.ShapeDtypeStruct((wide, width), low_type),
+            jax.ShapeDtypeStruct(square, low_type),
+            jax.ShapeDtypeStruct(row_shape, low_type),
+            jax.ShapeDtypeStruct(row_shape, wide_type),
+            jax.ShapeDtypeStruct((8, width), wide_type),
+        ),
+        scratch_shapes=[
+            pltpu.VMEM(row_shape, low_type), pltpu.VMEM((width, rows), low_type), pltpu.VMEM(row_shape, wide_type)],
+        cost=pl.CostEstimate(
+            flops=4 * rows * width * (2 * wide + width), bytes_accessed=rows * width * 40, transcendentals=rows * wide),
+        operands=(upstream, middle, mixed, w_mix, w_grow, w_shrink, vec_rows, hidden),
+    )
+
+
+def layer_forward(residual, first, vec_rows, weights, bias, asides):
+    w_joined = weights[0]
     width = w_joined.shape[2] // 3
     normed = layer_norm(residual, vec_rows[0], vec_rows[1]).astype(low_type)
     queries = grouped(normed[first:], w_joined[:, :, :width]).astype(low_type)
     keys_values = grouped(normed[:CTX], w_joined[:, :, width:]).astype(low_type)
-    mixed, lse, extra = attend(queries, keys_values, bias, aside)
-    middle = residual[first:] + matmul(mixed, w_mix) + vec_rows[4]
-    normed_mlp = layer_norm(middle, vec_rows[2], vec_rows[3]).astype(low_type)
-    hidden = matmul(normed_mlp, w_grow)
-    active = jax.nn.gelu(hidden).astype(low_type)
-    output = middle + matmul(active, w_shrink) + vec_rows[5]
-    return output, extra, (residual, normed, queries, keys_values, mixed, lse, middle, normed_mlp, hidden, active)
-
-
-def layer_backward(upstream, kept, first, vec_rows, weights, bias, aside):
-    w_joined, w_mix, w_grow, w_shrink = weights
+    mixed, lse, extra = attend(queries, keys_values, bias, asides[0])
+    (output, middle, hidden), more = mlp_forward(residual, first, mixed, weights, vec_rows, asides[1])
+    return output, (extra, more), (residual, normed, queries, keys_values, mixed, lse, middle, hidden)
+
+
+def layer_backward(upstream, kept, first, vec_rows, weights, bias, make_asides):
+    w_joined = weights[0]
     width = w_joined.shape[2] // 3
-    residual, normed, queries, keys_values, mixed, lse, middle, normed_mlp, hidden, active = kept
-    down_low = upstream.astype(low_type)
-    grad_shrink = matmul_tn(active, down_low).astype(low_type)
-    grad_hidden = gelu_back(hidden, matmul_nt(down_low, w_shrink)).astype(low_type)
-    grad_grow = matmul_tn(normed_mlp, grad_hidden).astype(low_type)
-    grad_middle, gain_mlp, shift_mlp = norm_back(
-        middle, vec_rows[2], vec_rows[3], matmul_nt(grad_hidden, w_grow))
-    grad_middle = grad_middle + upstream
-    mix_low = grad_middle.astype(low_type)
-    grad_mix = matmul_tn(mixed, mix_low).astype(low_type)
-    grad_mixed = matmul_nt(mix_low, w_mix).astype(low_type)
-    grad_q, grad_k, grad_v, extra = attend_back(queries, keys_values, bias, grad_mixed, mixed, lse, aside)
+    residual, normed, queries, keys_values, mixed, lse, middle, hidden = kept
+    outs, extra = mlp_backward(upstream, middle, mixed, weights, vec_rows, hidden, make_asides(0, None))
+    grad_grow, grad_shrink, grad_mix, grad_mixed, grad_middle, mlp_vec = outs
+    grad_q, grad_k, grad_v, more = attend_back(
+        queries, keys_values, bias, grad_mixed, mixed, lse, make_asides(1, (grad_grow, grad_shrink)))
 
     def weight_grad(rows, grads):
         return jnp.einsum("rd,grc->gdc", rows, grads, preferred_element_type=wide_type).astype(low_type)
@@ -732,9 +883,9 @@
     tail = jnp.zeros((rows - CTX, from_q.shape[1]), wide_type)
     grad_normed = jnp.concatenate([below, from_q], 0) + jnp.concatenate([from_kv, tail], 0)
     grad_input, gain_attn, shift_attn = norm_back(residual, vec_rows[0], vec_rows[1], grad_normed)
-    vec_grads = [gain_attn, shift_attn, gain_mlp, shift_mlp, jnp.sum(grad_middle, 0), jnp.sum(upstream, 0)]
+    vec_grads = [gain_attn, shift_attn, mlp_vec[0], mlp_vec[1], mlp_vec[2], mlp_vec[3]]
     grad_out = grad_input + jnp.concatenate([below, grad_middle], 0)
-    return grad_out, extra, (grad_joined, grad_mix, grad_grow, grad_shrink), vec_grads
+    return grad_out, (extra, more), (grad_joined, grad_mix, grad_grow, grad_shrink), vec_grads
 
 
 def update(weight, moment_old, average, grad_in, scale):
@@ -764,7 +915,7 @@
 
 def whole_scatter(grads, by_core, rows_list):
     outs = []
-    for grad, bc in zip(as_blocks(grads, by_core, rows_list, ROUTES + (("zyx",),)), by_core):
+    for grad, bc in zip(as_blocks(grads, by_core, rows_list, ROUTES), by_core):
         half = lax.psum_scatter(grad.astype(wide_type), "head", scatter_dimension=0 if bc else 1)
         outs.append(lax.psum_scatter(half, "dp", scatter_dimension=0))
     return outs
@@ -802,12 +953,14 @@
         )
 
     own = [own_weights(at) for at in range(layer_total)]
-    forward_aside = [None] * layer_total
+    forward_asides = [[None, None] for _ in own]
     if direct:
-        got = all_gather_layer(own[0] + own[1][:2], BY_CORE + BY_CORE[:2], ROUTES + (("zyx",), ("zyx",)), 1)
-        gathered = [list(got[:4]), list(got[4:])]
-        last_two = own[1][2:]
-        forward_aside[0] = Aside(gather_plan(last_two, BY_CORE[2:], (("zxy",), ("zyx",))), last_two, 2)
+        gathered = [all_gather_layer(own[0], BY_CORE, ROUTES, 1)]
+        first_two, last_two = own[1][:2], own[1][2:]
+        forward_asides[0] = [
+            Aside(gather_plan(last_two, BY_CORE[2:], (("zxy",), ("zyx",))), last_two, 2),
+            Aside(gather_plan(first_two, BY_CORE[:2], (("zxy",), ("zyx",))), first_two, 6),
+        ]
     else:
         gathered = [whole_gather(o, BY_CORE) for o in own]
 
@@ -824,9 +977,9 @@
         first = CTX if at == layer_total - 1 else 0
         weights.append(as_weights(gathered[at]))
         residual, extra, kept = layer_forward(
-            residual, first, vectors[2 + 6 * at : 8 + 6 * at], weights[at], bias, forward_aside[at])
-        if extra is not None:
-            gathered[at + 1] += list(extra)
+            residual, first, vectors[2 + 6 * at : 8 + 6 * at], weights[at], bias, forward_asides[at])
+        if extra[0] is not None:
+            gathered.append(list(extra[1]) + list(extra[0]))
         kept_all.append(kept)
 
     head_low = w_head.astype(low_type)
@@ -846,18 +999,27 @@
     rows_list = [joined_rows, w_out.shape[2], w_up.shape[1], w_down.shape[1]]
     sums = [None] * layer_total
     vec_grads = [None] * layer_total
-    aside = None
+    big = None
     for at in reversed(range(layer_total)):
         first = CTX if at == layer_total - 1 else 0
+        above = big
+
+        def make_asides(turn, ready):
+            if not direct or above is None:
+                return None
+            if turn == 0:
+                blocks = as_blocks(above[2:], BY_CORE[2:], rows_list[2:], ROUTES[2:])
+                return Aside(reduce_plan(blocks, BY_CORE[2:], ROUTES[2:]), blocks, 3)
+            blocks = as_blocks(list(above[:2]) + list(ready), BY_CORE, rows_list, ROUTES)
+            return Aside(reduce_plan(blocks, BY_CORE, ROUTES), blocks, 7)
+
         upstream, extra, big, vec_grads[at] = layer_backward(
-            upstream, kept_all[at], first, vectors[2 + 6 * at : 8 + 6 * at], weights[at], bias, aside)
-        if extra is not None:
-            sums[at + 1] = extra
-        if at > 0 and direct:
-            blocks = as_blocks(big, BY_CORE, rows_list, ROUTES)
-            aside = Aside(reduce_plan(blocks, BY_CORE, ROUTES), blocks, 3)
-        elif at > 0:
+            upstream, kept_all[at], first, vectors[2 + 6 * at : 8 + 6 * at], weights[at], bias, make_asides)
+        if not direct:
             sums[at] = whole_scatter(big, BY_CORE, rows_list)
+        elif extra[0] is not None:
+            sums[at + 1] = list(extra[1][:2]) + list(extra[0])
+            sums[at] = list(extra[1][2:])
     grad_emb = matmul_tn(masked, upstream.astype(low_type))
     vec_list = [jnp.sum(upstream * leading, 0), jnp.sum(upstream, 0)]
     for at in range(layer_total):
@@ -875,13 +1037,14 @@
         grad_emb.astype(low_type).reshape((devices, n_emb, 128)),
         vec_flat.reshape((devices, n_vec, 128)),
         jnp.zeros((devices, n_all - used, 128), low_type)], 1)
-    last_grads, last_rows, last_core = list(big) + [small], rows_list + [n_all], BY_CORE + (False,)
     if direct:
-        routes = ROUTES + (("zyx",),)
+        last_grads, last_rows, last_core = list(big[:2]) + [small], rows_list[:2] + [n_all], BY_CORE[:2] + (False,)
+        routes = (("xzy", "yzx", "zyx"), ("zxy",), ("zxy", "zyx"))
         blocks = as_blocks(last_grads, last_core, last_rows, routes)
-        *sums[0], small_sum = reduce_scatter_layer(blocks, last_core, routes, 4)
+        qkv_sum, out_sum, small_sum = reduce_scatter_layer(blocks, last_core, routes, 4)
+        sums[0] = [qkv_sum, out_sum] + sums[0]
     else:
-        *sums[0], small_sum = whole_scatter(last_grads, last_core, last_rows)
+        small_sum = whole_scatter([small], (False,), [n_all])[0]
     small_sum = small_sum.reshape((n_all, 128))
 
     square = sum(jnp.sum(p * p) for ps in sums for p in ps) + jnp.sum(small_sum * small_sum)

time: 713 us -> 709 us (level)
  Pallas kernels: 400 us -> 534 us
  matrix products: 159 us -> 45.8 us
  other arithmetic: 73.9 us -> 58.1 us
    pallas_call x2 -> x4, Pallas kernels: 158 us -> 301 us  [with_aside(): pl.pallas_call(kernel, grid=grid, in_specs=list(in_specs) + plan.in_specs...]
    dot_general x15 -> x3, matrix products: 88.6 us -> 3.75 us  [contract(): lax.dot_general(first_op, second_op, (((first_dim,), (second_dim,)), ((),...]
    pallas_call x3, Pallas kernels: 222 us -> 184 us  [exchange(): pl.pallas_call(kernel, out_shape=tuple(plan.out_shape()), in_specs=plan.i...]
    dot_general x8 -> x2, matrix products: 35.4 us -> 3.48 us  [matmul(): return jnp.dot(first_op, second_op, preferred_element_type=wide_type)]
    pallas_call x2 -> x4, Pallas kernels: 19.9 us -> 49.4 us  [with_aside(): pl.pallas_call(body, grid=grid, in_specs=in_specs, out_specs=out_specs, o...]
    reshape x0 -> x8, local copies, waits for them, and re-layouts: none -> 10.3 us  [the longest x6 6.21 us: layer_norm(): return center * lax.rsqrt(spread + eps_norm) * gain_row + shift_row]
where the time goes in v3:
time: 709 us; the launch traced here: 701 us
  Pallas kernels  534 us (75%)
  other arithmetic  58.1 us (8%)
  local copies, waits for them, and re-layouts  49.4 us (7%)
  matrix products  45.8 us (6%)
  between operations  14.3 us (2%)
    pallas_call x4, Pallas kernels, with_aside(): pl.pallas_call(kernel, grid=grid, in_specs=list(in_specs) + plan.in_specs...  301 us
    pallas_call x3, Pallas kernels, exchange(): pl.pallas_call(kernel, out_shape=tuple(plan.out_shape()), in_specs=plan.i...  184 us
    pallas_call x4, Pallas kernels, with_aside(): pl.pallas_call(body, grid=grid, in_specs=in_specs, out_specs=out_specs, o...  49.4 us

profile of v3, /device:TPU:0, one launch (start us, length us, event | category | flops | bytes accessed | tf_op | source)
XLA Modules:
  0.0 701.3 jit_solution(1169306262343073339)
XLA Ops:
  0.7 1.6 slice_reduce_fusion.4
  3.7 1.8 fusion.67
  7.1 1.7 add_convert_fusion.1
  9.2 1.8 slice_reduce_fusion
  13.9 68.0 %shard_map.434 = (bf16[2,16,1,48,1152]{4,3,2,1,0:T(8,128)(2,1)}, bf16[2,16,1,24,768]{4,3,2,1,0:T(8,128)(2,1)}, bf16[16,2,1,24,3072]{4,3,2,1,0:T(8,128)(2,1)}, bf16[16,2,1,96,768]{4,3,2,1,0:T(8,128)(2,1)}) custom-call(bf16[1,48,1152]{2,1,0:T(8,128)(2,1)} %convert_element_type.165.refs_0_, bf16[1,24,768]{2,1,0:T(8,128)(2,1)} %get-tuple-element.217.refs_1_, ...), custom_call_target="tpu_custom_call" | custom-call | bytes 14155776 | tf_op jit(solution)/shard_map/pallas_call | solution.py:477
  82.0 5.5 convert_bitcast_fusion.1.refs_1_.refs_2_
  87.5 3.8 fusion.16.refs_0_
  93.5 66.8 %shard_map.435 = (bf16[1024,768]{1,0:T(8,128)(2,1)}, f32[6,2,1024]{2,1,0:T(2,128)}, bf16[16,2,1,24,3072]{4,3,2,1,0:T(8,128)(2,1)}, bf16[16,2,1,96,768]{4,3,2,1,0:T(8,128)(2,1)}) custom-call(bf16[2,1024,384]{2,1,0:T(8,128)(2,1)} %fusion.16.refs_0_, bf16[2,768,768]{2,1,0:T(8,128)(2,1)} %convert_bitcast_fusion.1.refs_1_.refs_2_, ...), custom_call_target="tpu_custom_call" | custom-call | flops 2415919104 | bytes 6291456 | tf_op jit(solution)/shard_map/pallas_call | solution.py:458
  160.3 1.4 fusion.65
  161.6 1.6 convert_element_type.175.refs_6_
  163.3 52.7 %shard_map.436 = (f32[1024,768]{1,0:T(8,128)}, f32[1024,768]{1,0:T(8,128)}, bf16[1024,3072]{1,0:T(8,128)(2,1)}, bf16[2,16,1,48,1152]{4,3,2,1,0:T(8,128)(2,1)}, bf16[2,16,1,24,768]{4,3,2,1,0:T(8,128)(2,1)}) custom-call(f32[1024,768]{1,0:T(8,128)} %copy-done.2, bf16[1024,768]{1,0:T(8,128)(2,1)} %get-tuple-element.69.refs_1_.refs_2_.refs_5_, ...), custom_call_target="tpu_custom_call" | custom-call | flops 10871635968 | bytes 18874368 | tf_op jit(solution)/shard_map/pallas_call | solution.py:458
  216.0 2.3 reduce_sum.301
  220.5 2.0 copy-done.17
  222.5 3.4 convert_bitcast_fusion.k_ref.v_ref
  227.1 10.0 %shard_map.437 = (bf16[256,768]{1,0:T(8,128)(2,1)}, f32[6,2,256]{2,1,0:T(2,128)}) custom-call(bf16[2,256,384]{2,1,0:T(8,128)(2,1)} %fusion.28.q_ref, bf16[2,768,768]{2,1,0:T(8,128)(2,1)} %convert_bitcast_fusion.k_ref.v_ref, bf16[2,768,768]{2,1,0:T(8,128)(2,1)} %convert_bitcast_fusion.k_ref.v_ref, bf16[768,128]{1,0:T(8,128)(2,1)} %broadcast_in_dim.28.refs_3_.bias_ref), custom_call_target="tpu_custom_call" | custom-call | flops 603979776 | bytes 1572864 | tf_op jit(solution)/shard_map/pallas_call | solution.py:420
  237.1 11.1 %shard_map.438 = (f32[256,768]{1,0:T(8,128)}, f32[256,768]{1,0:T(8,128)}, bf16[256,3072]{1,0:T(8,128)(2,1)}) custom-call(f32[1024,768]{1,0:T(8,128)} %get-tuple-element.74.res_ref, bf16[256,768]{1,0:T(8,128)(2,1)} %get-tuple-element.75.mixed_ref.o_ref, bf16[768,768]{1,0:T(8,128)(2,1)} %bitcast.136, bf16[768,3072]{1,0:T(8,128)(2,1)} %bitcast.124, ...), custom_call_target="tpu_custom_call" | custom-call | flops 2717908992 | bytes 4718592 | tf_op jit(solution)/shard_map/pallas_call | solution.py:420
  248.2 1.4 reduce_sum.303
  249.6 1.4 multiply_reduce_fusion.9
  251.0 1.7 fusion.68
  253.6 1.5 convolution_convert_fusion.6
  255.1 2.3 reshape.381
  260.0 18.8 %shard_map.439 = (bf16[768,3072]{1,0:T(8,128)(2,1)}, bf16[3072,768]{1,0:T(8,128)(2,1)}, bf16[768,768]{1,0:T(8,128)(2,1)}, bf16[256,768]{1,0:T(8,128)(2,1)}, f32[256,768]{1,0:T(8,128)}, /*index=5*/f32[8,768]{1,0:T(8,128)}) custom-call(f32[256,768]{1,0:T(8,128)} %broadcast_add_fusion.u_ref, f32[256,768]{1,0:T(8,128)} %get-tuple-element.80.middle_ref, ...), custom_call_target="tpu_custom_call" | custom-call | flops 5435817984 | bytes 7864320 | tf_op jit(solution)/shard_map/pallas_call | solution.py:420
  278.8 9.6 %shard_map.440 = (bf16[2,256,384]{2,1,0:T(8,128)(2,1)}, bf16[2,768,384]{2,1,0:T(8,128)(2,1)}, bf16[2,768,384]{2,1,0:T(8,128)(2,1)}) custom-call(bf16[2,256,384]{2,1,0:T(8,128)(2,1)} %fusion.28.q_ref, bf16[2,768,768]{2,1,0:T(8,128)(2,1)} %convert_bitcast_fusion.k_ref.v_ref, bf16[2,768,768]{2,1,0:T(8,128)(2,1)} %convert_bitcast_fusion.k_ref.v_ref, ...), custom_call_target="tpu_custom_call" | custom-call | flops 1509949440 | bytes 3145728 | tf_op jit(solution)/shard_map/pallas_call | solution.py:420
  288.4 1.6 fusion.23
  290.0 2.9 fusion.24
  294.4 3.9 copy.110
  298.2 2.0 convolution_bitcast_fusion
  300.2 2.5 fusion.33
  302.8 2.6 bitcast_add_fusion.2
  305.4 2.5 multiply_reduce_fusion
  307.9 1.7 fusion.61
  309.7 2.0 pad_add_fusion.refs_0_
  311.7 77.9 %shard_map.441 = (bf16[768,3072]{1,0:T(8,128)(2,1)}, bf16[3072,768]{1,0:T(8,128)(2,1)}, bf16[768,768]{1,0:T(8,128)(2,1)}, bf16[1024,768]{1,0:T(8,128)(2,1)}, f32...) custom-call(f32[1024,768]{1,0:T(8,128)} %pad_add_fusion.refs_0_, ...), custom_call_target="tpu_custom_call" | custom-call | flops 21743271936 | bytes 31457280 | tf_op jit(solution)/shard_map/pallas_call | solution.py:458
  389.6 103.2 %shard_map.442 = (bf16[2,1024,384]{2,1,0:T(8,128)(2,1)}, bf16[2,768,384]{2,1,0:T(8,128)(2,1)}, bf16[2,768,384]{2,1,0:T(8,128)(2,1)}, f32[1,48,1152]{2,1,0:T(8,12...) custom-call(bf16[2,1024,384]{2,1,0:T(8,128)(2,1)} %fusion.16.refs_0_, ...), custom_call_target="tpu_custom_call" | custom-call | flops 6039797760 | bytes 12582912 | tf_op jit(solution)/shard_map/pallas_call | solution.py:458
  492.8 2.9 fusion.30
  498.3 2.7 multiply_reduce_fusion.1
  501.1 1.5 fusion.60
  505.0 1.8 reshape.382
  507.9 1.3 reshape.383
  509.2 1.3 reshape.384
  515.6 2.7 stack.61
  518.3 1.4 convert_element_type.203
  519.8 2.3 maximum_maximum_fusion
  522.1 2.9 fusion.20
  527.6 3.8 copy.114
  531.4 77.8 %shard_map.443 = (f32[3,16,1152]{2,1,0:T(8,128)}, f32[1,24,768]{2,1,0:T(8,128)}, f32[2,64,128]{2,1,0:T(8,128)}) custom-call(bf16[2,16,3,16,1152]{4,3,2,1,0:T(8,128)(2,1)} %bitcast.117, bf16[2,16,1,24,768]{4,3,2,1,0:T(8,128)(2,1)} %bitcast.135, bf16[16,2,2,64,128]{4,3,2,1,0:T(8,128)(2,1)} %bitcast.128), custom_call_target="tpu_custom_call" | custom-call | bytes 184549376 | tf_op jit(solution)/shard_map/pallas_call | solution.py:477
  609.2 1.6 multiply_reduce_fusion.15
  610.8 1.5 multiply_reduce_fusion.17
  613.6 1.6 multiply_reduce_fusion.13
  615.9 1.6 multiply_reduce_fusion.12
  618.2 1.6 multiply_reduce_fusion.14
  620.4 1.5 multiply_reduce_fusion.16
  622.6 1.6 multiply_reduce_fusion.11
  624.9 1.6 multiply_reduce_fusion.10
  627.2 1.5 multiply_reduce_fusion.18
  629.3 1.3 convert_reduce_fusion
  630.6 1.4 fusion.58
  632.0 1.5 pad_maximum_fusion.2
  633.4 37.8 %shard_map.444 = f32[16,2,2,64,128]{4,3,2,1,0:T(8,128)} custom-call(f32[2,64,128]{2,1,0:T(8,128)} %bitcast.145), custom_call_target="tpu_custom_call" | custom-call | bytes 1048576 | tf_op jit(solution)/shard_map/pallas_call | solution.py:477
  674.9 1.5 slice_multiply_fusion
  676.4 1.4 mul.647
  678.4 5.4 multiply_add_fusion.1
  683.9 1.4 multiply_add_fusion.4
  686.0 1.4 multiply_add_fusion.6
  (232 shorter events, 42.5 us)
Async XLA Ops:
  2.3 4.9 copy-start.59
  3.0 2.5 copy-start.67
  3.7 2.4 copy-start.74
  5.5 3.4 copy-start.2
  5.5 3.3 copy-start.50
  6.1 2.8 copy-start.61
  7.1 4.6 copy-start.11
  8.8 3.7 copy-start.13
  8.9 4.4 copy-start.36
  82.0 5.5 copy-start.18
  87.5 3.8 copy-start.80
  216.0 2.8 copy-start
  219.9 2.6 copy-start.17
  220.5 5.4 copy-start.9
  248.2 2.8 copy-start.5
  248.2 4.5 copy-start.73
  248.2 4.8 copy-start.76
  248.2 5.4 copy-start.4
  248.2 5.4 copy-start.54
  248.2 5.4 copy-start.69
  290.0 2.9 copy-start.10
  290.0 2.9 copy-start.26
  298.2 2.0 copy-start.79
  300.2 2.5 copy-start.27
  302.7 2.6 copy-start.1
  302.7 2.6 copy-start.49
  302.7 2.6 copy-start.53
  302.8 2.6 copy-start.56
  305.4 2.5 copy-start.66
  492.8 2.9 copy-start.25
  492.8 3.1 copy-start.40
  495.9 1.9 copy-start.3
  495.9 1.9 copy-start.51
  495.9 1.9 copy-start.60
  495.9 1.9 copy-start.62
  495.9 2.4 copy-start.77
  498.3 2.7 copy-start.64
  501.0 1.9 copy-start.7
  503.6 7.6 %copy-start.72 = (bf16[768]{0:T(1024)(128)(2,1)S(1)}, bf16[768]{0:T(1024)(128)(2,1)}, u32[]{:S(2)}) copy-start(bf16[768]{0:T(1024)(128)(2,1)} %get-tuple-element.159) | copy-start | bytes 4612
  503.6 8.2 %copy-start.71 = (bf16[768]{0:T(1024)(128)(2,1)S(1)}, bf16[768]{0:T(1024)(128)(2,1)}, u32[]{:S(2)}) copy-start(bf16[768]{0:T(1024)(128)(2,1)} %get-tuple-element.163) | copy-start | bytes 4612
  503.6 16.2 %copy-start.8 = (bf16[32,96,128]{2,1,0:T(8,128)(2,1)S(1)}, bf16[32,96,128]{2,1,0:T(8,128)(2,1)}, u32[]{:S(2)}) copy-start(bf16[32,96,128]{2,1,0:T(8,128)(2,1)} %reshape.381) | copy-start | bytes 2359300
  503.6 18.5 %copy-start.19 = (bf16[1024,768]{1,0:T(8,128)(2,1)S(1)}, bf16[1024,768]{1,0:T(8,128)(2,1)}, u32[]{:S(2)}) copy-start(bf16[1024,768]{1,0:T(8,128)(2,1)} %add_convert_fusion.1) | copy-start | bytes 4718596
  522.1 3.0 copy-start.78
  676.4 1.9 copy-start.6
  678.4 5.5 copy-start.12
  678.4 5.5 copy-start.22
  678.4 5.5 copy-start.24
  678.4 5.5 copy-start.32
  678.4 5.5 copy-start.33
  683.8 2.1 copy-start.34
  683.8 2.2 copy-start.35
  685.2 2.2 copy-start.37
  685.2 2.2 copy-start.44
  685.2 2.2 copy-start.45
  685.2 2.2 copy-start.46
  685.3 2.2 copy-start.47
  686.0 2.3 copy-start.30
  686.0 2.4 copy-start.29
  688.9 4.9 copy-start.43
  688.9 4.9 copy-start.57
  688.9 4.9 copy-start.58
  689.1 6.5 copy-start.20
  689.1 6.5 copy-start.41
  689.1 6.5 copy-start.42
  (17 other events, 23.4 us)

commit v4 on v3

--- a/solution.py
+++ b/solution.py
@@ -30,27 +30,28 @@
         core = 1 - self.core if way == "c" else self.core
         return (self.chip + step, core)
 
+    def group(self, k):
+        return (
+            1 - self.y if k & 4 else self.y, 1 - self.x if k & 2 else self.x, 1 - self.core if k & 1 else self.core)
+
     def block(self, k, ax, ay):
         sx = self.x if ax == 0 else 1 - self.x
         sy = self.y if ay == 0 else 1 - self.y
         return self.z_from[k] * 4 + sy * 2 + sx
 
 
-def meet(place):
+def meet(place, wide=False):
     barrier = pltpu.get_barrier_semaphore()
-    for way in "xyc":
-        pl.semaphore_signal(barrier, inc=1, device_id=place.peer(way), device_id_type=MESH)
-
-    @pl.when(place.z < 3)
-    def _():
-        pl.semaphore_signal(barrier, inc=1, device_id=place.peer("u"), device_id_type=MESH)
-
-    @pl.when(place.z > 0)
-    def _():
-        pl.semaphore_signal(barrier, inc=1, device_id=place.peer("d"), device_id_type=MESH)
-
-    ends = place.z * (3 - place.z)
-    pl.semaphore_wait(barrier, 4 + ends // 2)
+    to = [place.peer(way) for way in "xyc"]
+    if wide:
+        to = []
+        for k in range(1, 8):
+            y, x, core = place.group(k)
+            to.append((place.z * 4 + y * 2 + x, core))
+    to += [(place.chip + 4 * ((place.z + d) % 4 - place.z), place.core) for d in (1, 2, 3)]
+    for device in to:
+        pl.semaphore_signal(barrier, inc=1, device_id=device, device_id_type=MESH)
+    pl.semaphore_wait(barrier, len(to))
 
 
 def at_block(ref, chip, core, piece, by_core):
@@ -171,240 +172,271 @@
         return [functools.partial(entry, *e) for e in entries] + [finish]
 
 
+QUARTERS = ((True, True), (True, False), (False, True), (False, False))
+
+
+def as_grid(array, kind):
+    lead = {True: (2, 4, 2, 2), False: (4, 2, 2, 2), "group": (2, 2, 2, 4)}[kind]
+    return array.reshape(lead + array.shape[2:])
+
+
+def quarter_of(ref, kind, core, y, x, c):
+    if kind == "group":
+        return ref.at[y, x, core, :, c]
+    return ref.at[core, :, y, x, c] if kind else ref.at[:, y, x, core, c]
+
+
 class Reduce:
-    def __init__(self, by_core, orders, shapes):
-        self.by_core, self.orders, self.shapes = by_core, orders, shapes
-        self.n, self.pieces = len(by_core), max(map(len, orders))
+    def __init__(self, kinds, orders, shapes):
+        self.kinds, self.orders, self.shapes = kinds, orders, shapes
+        self.n, self.pieces = len(kinds), max(map(len, orders))
 
     def in_specs(self):
         return [pl.BlockSpec(memory_space=pl.ANY)] * self.n
 
     def out_specs(self):
-        return [pl.BlockSpec(memory_space=pltpu.VMEM)] * self.n
+        return [pl.BlockSpec(memory_space=pltpu.VMEM)] * (self.n + 1)
 
     def out_shape(self):
-        return [jax.ShapeDtypeStruct(s, jnp.float32) for s in self.shapes]
-
-    def room(self, a, way):
-        most = 1
-        for order in self.orders[a]:
-            if way in "ud":
-                most = max(most, 4 if order[0] == "z" else 8)
-            else:
-                most = max(most, {2: 8, 1: 4, 0: 1}[order.index(way)])
-        return most
+        return [jax.ShapeDtypeStruct(s, jnp.float32) for s in self.shapes + [(1, 128)]]
 
     def scratch(self):
         n, pieces = self.n, self.pieces
         buffers = []
-        for sizes in ([16] * n, [16] * n, *[[self.room(a, w) for a in range(n)] for w in "xyud"]):
-            buffers += [pltpu.VMEM((k,) + s, jnp.bfloat16) for k, s in zip(sizes, self.shapes)]
+        for lead in ((2, 2, 4), (2, 2, 4), (2, 4), (4,), (4,)):
+            buffers += [pltpu.VMEM(lead + s, jnp.bfloat16) for s in self.shapes]
         return buffers + [
+            pltpu.SemaphoreType.DMA((n, pieces, 4)),
+            pltpu.SemaphoreType.DMA((2, n, pieces, 4)),
+            pltpu.SemaphoreType.DMA((2, n, pieces, 2)),
+            pltpu.SemaphoreType.DMA((2, n, pieces)),
+            pltpu.SemaphoreType.DMA((2, n, pieces, 4)),
+        ]
+
+    def steps(self, ins, outs, scratch, meeting=True):
+        n, kinds = self.n, self.kinds
+        mine, other, first, second, line = [scratch[i * n : (i + 1) * n] for i in range(5)]
+        load_sem, core_sem, first_sem, second_sem, line_sem = scratch[5 * n :]
+        squares = outs[n]
+        place = Place()
+        items = [(a, c, order) for a in range(n) for c, order in enumerate(self.orders[a])]
+
+        def at(order, far_first, far_second):
+            far = {order[2]: far_first, order[1]: far_second}
+            return (1 - place.y if far["y"] else place.y, 1 - place.x if far["x"] else place.x)
+
+        def send(src, dst, sems, index, to, index_there=None):
+            return pltpu.make_async_remote_copy(
+                src_ref=src, dst_ref=dst, send_sem=sems.at[(0,) + index],
+                recv_sem=sems.at[(1,) + (index if index_there is None else index_there)],
+                device_id=to, device_id_type=MESH)
+
+        def load(a, c, y, x):
+            return pltpu.make_async_copy(
+                quarter_of(ins[a], kinds[a], place.core, y, x, c), mine[a].at[y, x, :, c], load_sem.at[a, c, y * 2 + x])
+
+        def to_core(a, c, y, x):
+            return send(
+                quarter_of(ins[a], kinds[a], 1 - place.core, y, x, c), other[a].at[y, x, :, c],
+                core_sem, (a, c, y * 2 + x), place.peer("c"))
+
+        def to_first(a, c, order, far):
+            y, x = at(order, True, far)
+            return send(
+                mine[a].at[y, x, :, c], first[a].at[int(far), :, c], first_sem, (a, c, int(far)), place.peer(order[2]))
+
+        def to_second(a, c, order):
+            y, x = at(order, False, True)
+            return send(mine[a].at[y, x, :, c], second[a].at[:, c], second_sem, (a, c), place.peer(order[1]))
+
+        def to_owner(a, c, d):
+            z = (place.z + d) % 4
+            return send(
+                mine[a].at[place.y, place.x, z, c], line[a].at[place.z, c], line_sem, (a, c, d),
+                (place.chip + 4 * (z - place.z), place.core), (a, c, place.z))
+
+        def from_line(a, c, d):
+            z = (place.z + d) % 4
+            return send(
+                mine[a].at[place.y, place.x, z, c], line[a].at[z, c], line_sem, (a, c, d),
+                (place.chip + 4 * (z - place.z), place.core), (a, c, z))
+
+        def add(a, c, y, x, more):
+            def one(z, carry):
+                mine[a][y, x, z, c] = mine[a][y, x, z, c] + more(z)
+                return carry
+            lax.fori_loop(0, 4, one, 0)
+
+        def begin():
+            if meeting:
+                meet(place)
+            squares[...] = jnp.zeros_like(squares)
+            for quarter in QUARTERS:
+                for a, c, order in items:
+                    y, x = at(order, *quarter)
+                    to_core(a, c, y, x).start()
+                    load(a, c, y, x).start()
+
+        def fold(item, quarter):
+            a, c, order = item
+            y, x = at(order, *quarter)
+            load(a, c, y, x).wait()
+            to_core(a, c, y, x).wait_recv()
+            add(a, c, y, x, lambda z: other[a][y, x, z, c])
+            if quarter[0]:
+                to_first(a, c, order, quarter[1]).start()
+
+        def take_first(item, far):
+            a, c, order = item
+            y, x = at(order, False, far)
+            to_first(a, c, order, far).wait_recv()
+            add(a, c, y, x, lambda z: first[a][int(far), z, c])
+            if far:
+                to_second(a, c, order).start()
+
+        def take_second(item):
+            a, c, order = item
+            to_second(a, c, order).wait_recv()
+            add(a, c, place.y, place.x, lambda z: second[a][z, c])
+            for d in (1, 2, 3):
+                to_owner(a, c, d).start()
+
+        def last(item):
+            a, c, order = item
+            total = mine[a][place.y, place.x, place.z, c].astype(jnp.float32)
+            for d in (1, 2, 3):
+                from_line(a, c, d).wait_recv()
+                total += line[a][(place.z + d) % 4, c].astype(jnp.float32)
+            outs[a][c] = total
+            by_lane = jnp.sum(total * total, 0, keepdims=True)
+            for k in range(by_lane.shape[1] // 128):
+                squares[...] += by_lane[:, k * 128 : (k + 1) * 128]
+
+        def finish():
+            for a, c, order in items:
+                for quarter in QUARTERS:
+                    to_core(a, c, *at(order, *quarter)).wait_send()
+                to_first(a, c, order, True).wait_send()
+                to_first(a, c, order, False).wait_send()
+                to_second(a, c, order).wait_send()
+                for d in (1, 2, 3):
+                    to_owner(a, c, d).wait_send()
+
+        part = functools.partial
+        out = [begin]
+        for quarter in QUARTERS:
+            out += [part(fold, it, quarter) for it in items]
+        for far in (True, False):
+            out += [part(take_first, it, far) for it in items]
+        out += [part(take_second, it) for it in items]
+        return out + [part(last, it) for it in items] + [finish]
+
+
+class Spread:
+    wide = True
+
+    def __init__(self, shapes, dtypes):
+        self.shapes, self.dtypes, self.n = shapes, dtypes, len(shapes)
+
+    def in_specs(self):
+        return [pl.BlockSpec(memory_space=pl.ANY)] * self.n
+
+    def out_specs(self):
+        return [pl.BlockSpec(memory_space=pl.ANY)] * self.n
+
+    def out_shape(self):
+        return [jax.ShapeDtypeStruct((2, 2, 2, 4) + s, d) for s, d in zip(self.shapes, self.dtypes)]
+
+    def scratch(self):
+        n = self.n
+        return [
             pltpu.SemaphoreType.DMA((n,)),
-            pltpu.SemaphoreType.DMA((n, pieces, 16)),
-            pltpu.SemaphoreType.DMA((n, pieces)),
-            pltpu.SemaphoreType.DMA((n, pieces, 4, 8)),
-            pltpu.SemaphoreType.DMA((n, pieces, 4)),
+            pltpu.SemaphoreType.DMA((2, n, 4)),
+            pltpu.SemaphoreType.DMA((2, n, 8)),
         ]
 
-    def steps(self, ins, outs, scratch):
-        n, orders, by_core = self.n, self.orders, self.by_core
-        mine, other = scratch[:n], scratch[n : 2 * n]
-        got = {w: scratch[(2 + i) * n : (3 + i) * n] for i, w in enumerate("xyud")}
-        load_sem, core_recv, core_send, recv, send = scratch[6 * n :]
-        ways = {"x": 0, "y": 1, "u": 2, "d": 3}
+    def steps(self, ins, outs, scratch, meeting=True):
+        local_sem, line_sem, group_sem = scratch
         place = Place()
 
-        def number(at):
-            sx, sy, sz = at
-            return sz * 4 + sy * 2 + sx
-
-        def load(a):
-            src = ins[a].at[place.core] if by_core[a] else ins[a].at[:, place.core]
-            return pltpu.make_async_copy(src, mine[a], load_sem.at[a])
-
-        def to_core(a, c, at):
-            chip = number(at)
+        def own(a):
+            return pltpu.make_async_copy(
+                ins[a], outs[a].at[place.y, place.x, place.core, place.z], local_sem.at[a])
+
+        def along(a, d, back):
+            z = (place.z + d) % 4
+            at = z if back else place.z
             return pltpu.make_async_remote_copy(
-                src_ref=at_block(ins[a], chip, 1 - place.core, c, by_core[a]), dst_ref=other[a].at[chip, c],
-                send_sem=core_send.at[a, c], recv_sem=core_recv.at[a, c, chip],
-                device_id=place.peer("c"), device_id_type=MESH)
-
-        def landing(order, at, way):
-            sx, sy, sz = at
-            if way in "ud":
-                return sz if order[0] == "z" else sz * 2 + (sx if order[0] == "x" else sy)
-            turn = order.index(way)
-            return (0, sz, sz * 2 + (sx if way == "y" else sy))[turn]
-
-        def hop(a, c, order, at, way):
-            spot = landing(order, at, way)
+                src_ref=ins[a], dst_ref=outs[a].at[place.y, place.x, place.core, at],
+                send_sem=line_sem.at[0, a, d], recv_sem=line_sem.at[1, a, at],
+                device_id=(place.chip + 4 * (z - place.z), place.core), device_id_type=MESH)
+
+        def across(a, k, back):
+            to = place.group(k)
+            y, x, core = to if back else (place.y, place.x, place.core)
+            part = outs[a].at[y, x, core]
             return pltpu.make_async_remote_copy(
-                src_ref=mine[a].at[number(at), c], dst_ref=got[way][a].at[spot, c],
-                send_sem=send.at[a, c, ways[way]], recv_sem=recv.at[a, c, ways[way], spot],
-                device_id=place.peer(way), device_id_type=MESH)
-
-        def take(a, c, order, at, way):
-            hop(a, c, order, at, way).wait_recv()
-            mine[a][number(at), c] = mine[a][number(at), c] + got[way][a][landing(order, at, way), c]
-
-        def fold(a, c, at):
-            to_core(a, c, at).wait_recv()
-            chip = number(at)
-            mine[a][chip, c] = mine[a][chip, c] + other[a][chip, c]
-
-        items = [(a, c, order) for a in range(n) for c, order in enumerate(orders[a])]
-        lined = [it for it in items if it[2][1] == "z"]
-        flat = [it for it in items if it[2][0] == "z"]
-        items = lined + flat
-
-        def side(dim, far):
-            m = place.x if dim == "x" else place.y
-            return 1 - m if far else m
-
-        def spot(order, wave, i, far):
-            sz = wave + (3 - 2 * wave) * (i // 2)
-            if order[2] == "y":
-                return (i % 2, side("y", far), sz)
-            return (side("x", far), i % 2, sz)
-
-        def loop(count, body):
-            def run(i, carry):
-                body(i)
-                return carry
-            lax.fori_loop(0, count, run, 0)
-
-        def start(wave, far):
-            for a, c, order in items:
-                loop(4, lambda i: to_core(a, c, spot(order, wave, i, far)).start())
+                src_ref=part, dst_ref=part, send_sem=group_sem.at[0, a, k], recv_sem=group_sem.at[1, a, k],
+                device_id=(place.z * 4 + to[0] * 2 + to[1], to[2]), device_id_type=MESH)
 
         def begin():
-            meet(place)
-            for a in range(n):
-                load(a).start()
-            for wave, far in ((0, True), (0, False), (1, True), (1, False)):
-                start(wave, far)
-            for a in range(n):
-                load(a).wait()
-
-        def far(wave):
-            for a, c, order in items:
-                def one(i):
-                    at = spot(order, wave, i, True)
-                    fold(a, c, at)
-                    hop(a, c, order, at, order[2]).start()
-                loop(4, one)
-
-        def near(wave):
-            for a, c, order in items:
-                loop(4, lambda i: fold(a, c, spot(order, wave, i, False)))
-
-        def second(it, wave):
-            a, c, order = it
-            if order[1] == "z":
-                loop(4, lambda i: take(a, c, order, spot(order, wave, i, False), order[2]))
-                return
-            for away in (True, False):
-                def one(i):
-                    sz = wave + (3 - 2 * wave) * i
-                    at = (side("x", away and order[1] == "x"), side("y", away and order[1] == "y"), sz)
-                    take(a, c, order, at, order[2])
-                    if away:
-                        hop(a, c, order, at, order[1]).start()
-                loop(2, one)
-
-        def third(it, wave):
-            a, c, order = it
-            loop(2, lambda i: take(a, c, order, (place.x, place.y, wave + (3 - 2 * wave) * i), order[1]))
-
-        def here(order):
-            if order[0] == "z":
-                return [(place.x, place.y)]
-            return [(side("x", order[0] == "x"), side("y", order[0] == "y")), (place.x, place.y)]
-
-        def line(it, j):
-            a, c, order = it
-            for way, target, active, inner in (
-                ("u", 3 - j, place.z < 3 - j, place.z > 0),
-                ("d", j, place.z > j, place.z < 3),
-            ):
-                @pl.when(active)
-                def _():
-                    for sx, sy in here(order):
-                        at = (sx, sy, target)
-
-                        @pl.when(inner)
-                        def _():
-                            take(a, c, order, at, way)
-                        hop(a, c, order, at, way).start()
-
-        def owned(it):
-            a, c, order = it
-            for first, (sx, sy) in enumerate(here(order)):
-                at = (sx, sy, place.z)
-
-                @pl.when(place.z > 0)
-                def _():
-                    take(a, c, order, at, "u")
-
-                @pl.when(place.z < 3)
-                def _():
-                    take(a, c, order, at, "d")
-                if order[0] != "z" and first == 0:
-                    hop(a, c, order, at, order[0]).start()
-
-        def last(it):
-            a, c, order = it
-            if order[0] != "z":
-                take(a, c, order, (place.x, place.y, place.z), order[0])
-            outs[a][c] = mine[a][place.chip, c].astype(jnp.float32)
-
-        def drain(a, c, sem, count):
-            part = other[a].at[pl.ds(0, count), c]
-            pltpu.make_async_remote_copy(
-                src_ref=part, dst_ref=part, send_sem=sem, recv_sem=recv.at[a, c, 0, 0],
-                device_id=place.peer("c"), device_id_type=MESH).wait_send()
-
-        def finish():
-            for it in lined:
-                last(it)
-            for a, c, order in items:
-                drain(a, c, core_send.at[a, c], 16)
-                left = 16
-                for turn in (2, 1, 0):
-                    dim = order[turn]
-                    if dim == "z":
-                        left //= 4
-                        for zz in range(4):
-                            @pl.when(place.z == zz)
-                            def _(zz=zz, left=left):
-                                if zz < 3:
-                                    drain(a, c, send.at[a, c, 2], left * (3 - zz))
-                                if zz > 0:
-                                    drain(a, c, send.at[a, c, 3], left * zz)
-                    else:
-                        left //= 2
-                        drain(a, c, send.at[a, c, ways[dim]], left)
-
-        part = functools.partial
-        out = [begin, part(far, 0), part(near, 0), part(far, 1)]
-        for it in lined:
-            out += [part(second, it, 0), part(line, it, 0)]
-        out += [part(second, it, 0) for it in flat]
-        out += [part(near, 1)]
-        for i, it in enumerate(lined):
-            out += [part(second, it, 1), part(line, it, 1), part(line, it, 2)]
-            if i == 0:
-                for fl in flat:
-                    out += [part(third, fl, 0), part(line, fl, 0)]
-        if not lined:
-            for fl in flat:
-                out += [part(third, fl, 0), part(line, fl, 0)]
-        out += [part(second, it, 1) for it in flat]
-        out += [part(owned, it) for it in lined]
-        for it in flat:
-            out += [part(third, it, 1), part(line, it, 1), part(line, it, 2), part(owned, it), part(last, it)]
-        return out + [finish]
+            if meeting:
+                meet(place, True)
+            for a in range(self.n):
+                for d in (1, 2, 3):
+                    along(a, d, False).start()
+                own(a).start()
+
+        def middle():
+            for a in range(self.n):
+                own(a).wait()
+                for d in (1, 2, 3):
+                    along(a, d, True).wait_recv()
+                for k in range(1, 8):
+                    across(a, k, False).start()
+
+        def end():
+            for a in range(self.n):
+                for k in range(1, 8):
+                    across(a, k, True).wait_recv()
+            for a in range(self.n):
+                for d in (1, 2, 3):
+                    along(a, d, False).wait_send()
+                for k in range(1, 8):
+                    across(a, k, False).wait_send()
+
+        return [begin, middle, end]
+
+
+class Both:
+    wide = True
+
+    def __init__(self, one, two):
+        self.parts, self.n = (one, two), one.n + two.n
+
+    def both(self, name):
+        return getattr(self.parts[0], name)() + getattr(self.parts[1], name)()
+
+    def in_specs(self):
+        return self.both("in_specs")
+
+    def out_specs(self):
+        return self.both("out_specs")
+
+    def out_shape(self):
+        return self.both("out_shape")
+
+    def scratch(self):
+        return self.both("scratch")
+
+    def steps(self, ins, outs, scratch, meeting=True):
+        one, two = self.parts
+        n_out, n_scratch = len(one.out_shape()), len(one.scratch())
+        lists = (
+            one.steps(ins[: one.n], outs[:n_out], scratch[:n_scratch], False),
+            two.steps(ins[one.n :], outs[n_out:], scratch[n_scratch:], False))
+        timed = [(i / (len(steps) - 1), step) for steps in lists for i, step in enumerate(steps)]
+        return [lambda: meet(Place(), True)] + [step for _, step in sorted(timed, key=lambda t: t[0])]
 
 
 VMEM_ALL = 64 * 1024 * 1024 - 65536
@@ -423,7 +455,7 @@
             compiler_params=pltpu.CompilerParams(vmem_limit_bytes=VMEM_ALL))(*operands)
         return out, None
     plan = aside.plan
-    n_in, n_out, n_scr, n = len(in_specs), len(out_specs), len(scratch_shapes), plan.n
+    n_in, n_out, n_scr, n, n_plan = len(in_specs), len(out_specs), len(scratch_shapes), plan.n, len(plan.out_shape())
     cells = 1
     for extent in grid:
         cells *= extent
@@ -433,7 +465,7 @@
         ins, refs = refs[:n_in], refs[n_in:]
         plan_ins, refs = refs[:n], refs[n:]
         outs, refs = refs[:n_out], refs[n_out:]
-        plan_outs, refs = refs[:n], refs[n:]
+        plan_outs, refs = refs[:n_plan], refs[n_plan:]
         scratch, plan_scratch = refs[:n_scr], refs[n_scr:]
         steps = plan.steps(plan_ins, plan_outs, plan_scratch)
         cell = 0
@@ -468,9 +500,10 @@
 
 def exchange(plan, arrays, collective_id):
     n = plan.n
+    n_all = n + len(plan.out_shape())
 
     def kernel(*refs):
-        for step in plan.steps(refs[:n], refs[n : 2 * n], refs[2 * n :]):
+        for step in plan.steps(refs[:n], refs[n:n_all], refs[n_all:]):
             step()
 
     moved = sum(a.size for a in arrays) * 2
@@ -490,16 +523,21 @@
     return Gather(by_core, orders, [a.shape for a in arrays], arrays[0].dtype)
 
 
-def reduce_plan(arrays, by_core, orders):
-    return Reduce(by_core, orders, [a.shape[2:] for a in arrays])
+def reduce_plan(arrays, kinds, orders):
+    return Reduce(kinds, orders, [a.shape[2:] for a in arrays]), [as_grid(a, kind) for a, kind in zip(arrays, kinds)]
+
+
+def spread_plan(arrays):
+    return Spread([a.shape for a in arrays], [a.dtype for a in arrays])
 
 
 def all_gather_layer(arrays, by_core, orders, collective_id):
     return exchange(gather_plan(arrays, by_core, orders), arrays, collective_id)
 
 
-def reduce_scatter_layer(arrays, by_core, orders, collective_id):
-    return exchange(reduce_plan(arrays, by_core, orders), arrays, collective_id)
+def reduce_scatter_layer(arrays, kinds, orders, collective_id):
+    plan, operands = reduce_plan(arrays, kinds, orders)
+    return exchange(plan, operands, collective_id)
 
 
 HD = 64
@@ -847,25 +885,27 @@
     )
 
 
-def layer_forward(residual, first, vec_rows, weights, bias, asides):
+def layer_forward(residual, first, vec_rows, weights, bias, asides, as_rest):
     w_joined = weights[0]
     width = w_joined.shape[2] // 3
     normed = layer_norm(residual, vec_rows[0], vec_rows[1]).astype(low_type)
     queries = grouped(normed[first:], w_joined[:, :, :width]).astype(low_type)
     keys_values = grouped(normed[:CTX], w_joined[:, :, width:]).astype(low_type)
     mixed, lse, extra = attend(queries, keys_values, bias, asides[0])
+    if len(weights) == 1:
+        weights = weights + as_rest(extra)
     (output, middle, hidden), more = mlp_forward(residual, first, mixed, weights, vec_rows, asides[1])
-    return output, (extra, more), (residual, normed, queries, keys_values, mixed, lse, middle, hidden)
+    return output, weights, more, (residual, normed, queries, keys_values, mixed, lse, middle, hidden)
 
 
 def layer_backward(upstream, kept, first, vec_rows, weights, bias, make_asides):
     w_joined = weights[0]
     width = w_joined.shape[2] // 3
     residual, normed, queries, keys_values, mixed, lse, middle, hidden = kept
-    outs, extra = mlp_backward(upstream, middle, mixed, weights, vec_rows, hidden, make_asides(0, None))
+    outs, extra = mlp_backward(upstream, middle, mixed, weights, vec_rows, hidden, make_asides(0, None, None))
     grad_grow, grad_shrink, grad_mix, grad_mixed, grad_middle, mlp_vec = outs
     grad_q, grad_k, grad_v, more = attend_back(
-        queries, keys_values, bias, grad_mixed, mixed, lse, make_asides(1, (grad_grow, grad_shrink)))
+        queries, keys_values, bias, grad_mixed, mixed, lse, make_asides(1, (grad_mix, grad_grow, grad_shrink), extra))
 
     def weight_grad(rows, grads):
         return jnp.einsum("rd,grc->gdc", rows, grads, preferred_element_type=wide_type).astype(low_type)
@@ -897,7 +937,7 @@
 
 BY_CORE = (True, True, False, False)
 ROUTES = (("zxy",), ("zxy",), ("xzy",), ("yzx",))
-HALVES = (("zxy", "zyx"),)
+REDUCE_ROUTES = (("zxy",), ("zyx",), ("zyx",), ("zxy",))
 
 
 def whole_gather(shard_list, by_core):
@@ -943,26 +983,27 @@
             w_down[at].astype(low_type)[None],
         ]
 
-    def as_weights(gathered):
-        qkv, out, up, down = gathered
-        return (
-            qkv.reshape((cores, width, kinds)),
-            out.reshape((width, width)),
-            up.reshape((width, -1)),
-            down.reshape((-1, width)),
-        )
+    def as_joined(qkv):
+        return (qkv.reshape((cores, width, kinds)),)
+
+    def as_rest(gathered):
+        out, up, down = gathered
+        return (out.reshape((width, width)), up.reshape((width, -1)), down.reshape((-1, width)))
 
     own = [own_weights(at) for at in range(layer_total)]
     forward_asides = [[None, None] for _ in own]
     if direct:
-        gathered = [all_gather_layer(own[0], BY_CORE, ROUTES, 1)]
-        first_two, last_two = own[1][:2], own[1][2:]
-        forward_asides[0] = [
-            Aside(gather_plan(last_two, BY_CORE[2:], (("zxy",), ("zyx",))), last_two, 2),
-            Aside(gather_plan(first_two, BY_CORE[:2], (("zxy",), ("zyx",))), first_two, 6),
-        ]
+        joined = own[0][0].reshape((3, joined_rows // 3, kinds))
+        weights = [as_joined(all_gather_layer([joined], (True,), (("xzy", "yzx", "zxy"),), 1)[0])]
+        for at, layer in enumerate(own):
+            if at == 0:
+                forward_asides[at][0] = Aside(
+                    gather_plan(layer[1:], BY_CORE[1:], (("xzy",), ("zxy",), ("zyx",))), layer[1:], 2)
+            else:
+                forward_asides[at - 1][1] = Aside(gather_plan(layer, BY_CORE, ROUTES), layer, 10 + at)
     else:
         gathered = [whole_gather(o, BY_CORE) for o in own]
+        weights = [as_joined(g[0]) + as_rest(g[1:]) for g in gathered]
 
     table = lax.axis_index("dp") * cores + lax.axis_index("head")
     count = lax.dynamic_slice_in_dim(counts, table, 1, 0)
@@ -972,14 +1013,12 @@
     leading = jnp.concatenate([ctx_vals[0], jnp.zeros((row_count - CTX,), wide_type)])[:, None]
     residual = matmul(masked, w_emb.astype(low_type)) + vectors[1] + leading * vectors[0]
     kept_all = []
-    weights = []
     for at in range(layer_total):
         first = CTX if at == layer_total - 1 else 0
-        weights.append(as_weights(gathered[at]))
-        residual, extra, kept = layer_forward(
-            residual, first, vectors[2 + 6 * at : 8 + 6 * at], weights[at], bias, forward_asides[at])
-        if extra[0] is not None:
-            gathered.append(list(extra[1]) + list(extra[0]))
+        residual, weights[at], extra, kept = layer_forward(
+            residual, first, vectors[2 + 6 * at : 8 + 6 * at], weights[at], bias, forward_asides[at], as_rest)
+        if extra is not None:
+            weights.append(as_joined(extra[0]) + as_rest(extra[1:]))
         kept_all.append(kept)
 
     head_low = w_head.astype(low_type)
@@ -996,73 +1035,75 @@
     upstream, gain_final, shift_final = norm_back(
         residual, vectors[-2], vectors[-1], matmul_nt(grad_logits, head_low))
 
+    devices = chips * cores
     rows_list = [joined_rows, w_out.shape[2], w_up.shape[1], w_down.shape[1]]
     sums = [None] * layer_total
     vec_grads = [None] * layer_total
+    squares = []
     big = None
     for at in reversed(range(layer_total)):
         first = CTX if at == layer_total - 1 else 0
         above = big
 
-        def make_asides(turn, ready):
+        def make_asides(turn, ready, earlier):
             if not direct or above is None:
                 return None
             if turn == 0:
-                blocks = as_blocks(above[2:], BY_CORE[2:], rows_list[2:], ROUTES[2:])
-                return Aside(reduce_plan(blocks, BY_CORE[2:], ROUTES[2:]), blocks, 3)
-            blocks = as_blocks(list(above[:2]) + list(ready), BY_CORE, rows_list, ROUTES)
-            return Aside(reduce_plan(blocks, BY_CORE, ROUTES), blocks, 7)
+                blocks = as_blocks(
+                    list(above) + [grad_head], BY_CORE + (False,), rows_list + [w_head.shape[0] // devices],
+                    REDUCE_ROUTES + (("zyx",),))
+                plan, operands = reduce_plan(blocks, BY_CORE + ("group",), REDUCE_ROUTES + (("zyx",),))
+                return Aside(plan, operands, 3)
+            blocks = as_blocks(ready, BY_CORE[1:], rows_list[1:], REDUCE_ROUTES[1:])
+            plan, operands = reduce_plan(blocks, BY_CORE[1:], REDUCE_ROUTES[1:])
+            head_sum = [earlier[4][0].astype(low_type)]
+            return Aside(Both(plan, spread_plan(head_sum)), operands + head_sum, 7)
 
         upstream, extra, big, vec_grads[at] = layer_backward(
             upstream, kept_all[at], first, vectors[2 + 6 * at : 8 + 6 * at], weights[at], bias, make_asides)
         if not direct:
             sums[at] = whole_scatter(big, BY_CORE, rows_list)
         elif extra[0] is not None:
-            sums[at + 1] = list(extra[1][:2]) + list(extra[0])
-            sums[at] = list(extra[1][2:])
+            sums[at + 1] = list(extra[0][:4])
+            sums[at] = list(extra[1][:3])
+            squares += [extra[0][5], extra[1][3]]
+            head_all = extra[1][4]
     grad_emb = matmul_tn(masked, upstream.astype(low_type))
     vec_list = [jnp.sum(upstream * leading, 0), jnp.sum(upstream, 0)]
     for at in range(layer_total):
         vec_list = vec_list + vec_grads[at]
     grad_vec = jnp.stack(vec_list + [gain_final, shift_final])
 
-    devices = chips * cores
-    n_head, n_emb = w_head.size // (devices * 128), w_emb.size // (devices * 128)
-    n_vec = -(-vectors.size // (devices * 128))
-    vec_flat = jnp.pad(grad_vec.astype(low_type).reshape(-1), (0, n_vec * devices * 128 - vectors.size))
-    used = n_head + n_emb + n_vec
-    n_all = -(-(used + 1) // 32) * 32
-    small = jnp.concatenate([
-        grad_head.reshape((devices, n_head, 128)),
-        grad_emb.astype(low_type).reshape((devices, n_emb, 128)),
-        vec_flat.reshape((devices, n_vec, 128)),
-        jnp.zeros((devices, n_all - used, 128), low_type)], 1)
+    scalars = [loss_part, jnp.sum(row_weight)]
     if direct:
-        last_grads, last_rows, last_core = list(big[:2]) + [small], rows_list[:2] + [n_all], BY_CORE[:2] + (False,)
-        routes = (("xzy", "yzx", "zyx"), ("zxy",), ("zxy", "zyx"))
-        blocks = as_blocks(last_grads, last_core, last_rows, routes)
-        qkv_sum, out_sum, small_sum = reduce_scatter_layer(blocks, last_core, routes, 4)
-        sums[0] = [qkv_sum, out_sum] + sums[0]
+        feats, vec_total = w_emb.shape[0], vectors.shape[0]
+        n_small = -(-(feats + vec_total) // (8 * devices)) * 8
+        small = jnp.concatenate([grad_emb, grad_vec], 0).astype(low_type)
+        small = jnp.pad(small, ((0, n_small * devices - feats - vec_total), (0, 0)))
+        kinds_last, routes = (True, "group"), (("zxy", "zyx"), ("zyx",))
+        blocks = as_blocks([big[0], small], (True, False), [joined_rows, n_small], routes)
+        qkv_sum, small_sum, square = reduce_scatter_layer(blocks, kinds_last, routes, 4)
+        sums[0] = [qkv_sum] + sums[0]
+        scalars = jnp.stack([jnp.sum(sum(squares + [square]))] + scalars)
+        scalars = jnp.broadcast_to(jnp.pad(scalars, (0, 125))[None], (8, 128))
+        last_parts = [small_sum[0].astype(low_type), scalars]
+        small_all, totals = exchange(spread_plan(last_parts), last_parts, 5)
+        small_all = small_all.reshape((devices * n_small, width)).astype(wide_type)
+        totals = jnp.sum(totals[..., 0, :3].reshape((devices, 3)), 0)
+        grad_emb, grad_vec = small_all[:feats], small_all[feats : feats + vec_total]
+        grad_head = head_all.reshape(w_head.shape).astype(wide_type)
     else:
-        small_sum = whole_scatter([small], (False,), [n_all])[0]
-    small_sum = small_sum.reshape((n_all, 128))
-
-    square = sum(jnp.sum(p * p) for ps in sums for p in ps) + jnp.sum(small_sum * small_sum)
-    scalars = jnp.pad(jnp.stack([square, loss_part, jnp.sum(row_weight)]), (0, 125))
-    small_sum = jnp.concatenate([small_sum[: n_all - 1], scalars[None]], 0)
-    if direct:
-        small_all = all_gather_layer([small_sum.reshape((2, n_all // 2, 128))], (False,), HALVES, 5)[0]
-    else:
-        small_all = whole_gather([small_sum], (False,))[0]
-    small_all = small_all.reshape((devices, n_all, 128))
-    totals = jnp.sum(small_all[:, n_all - 1, :3], 0)
+        names = ("dp", "head")
+        square = sum(jnp.sum(p * p) for ps in sums for p in ps)
+        totals = lax.psum(jnp.stack([square] + scalars), names)
+        grad_head = lax.psum(grad_head.astype(wide_type), names)
+        grad_emb, grad_vec = lax.psum(grad_emb, names), lax.psum(grad_vec, names)
+        alike = sum(jnp.sum(g * g) for g in (grad_head, grad_emb, grad_vec))
+        totals = jnp.stack([totals[0] + alike, totals[1], totals[2]])
     pooled = totals[2]
     loss = totals[1] / pooled
     grad_norm = jnp.sqrt(totals[0]) / pooled
     scale = jnp.minimum(1.0, clip_at / grad_norm) / pooled
-    grad_head = small_all[:, :n_head].reshape(w_head.shape)
-    grad_emb = small_all[:, n_head : n_head + n_emb].reshape(w_emb.shape)
-    grad_vec = small_all[:, n_head + n_emb : used].reshape(-1)[: vectors.size].reshape(vectors.shape)
 
     def big_update(weight, moment_old, average, kind):
         grad = jnp.stack([sums[at][kind].reshape(weight.shape[1:]) for at in range(layer_total)])

time: 709 us -> 623 us (0.88)
  Pallas kernels: 534 us -> 487 us
  local copies, waits for them, and re-layouts: 49.4 us -> 33.3 us
  other arithmetic: 58.1 us -> 42.2 us
    pallas_call x3, Pallas kernels: 184 us -> 84.4 us  [exchange(): pl.pallas_call(kernel, out_shape=tuple(plan.out_shape()), in_specs=plan.i...]
    pallas_call x4, Pallas kernels: 301 us -> 354 us  [with_aside(): pl.pallas_call(kernel, grid=grid, in_specs=list(in_specs) + plan.in_specs...]
    reduce_sum x11 -> x3, other arithmetic: 16.5 us -> 3.63 us  [the longest x1 1.29 us: shards(): scalars = [loss_part, jnp.sum(row_weight)]]
where the time goes in v4:
time: 623 us; the launch traced here: 617 us
  Pallas kernels  487 us (78%)
  matrix products  45 us (7%)
  other arithmetic  42.2 us (7%)
  local copies, waits for them, and re-layouts  33.3 us (5%)
  between operations  8.67 us (1%)
    pallas_call x4, Pallas kernels, with_aside(): pl.pallas_call(kernel, grid=grid, in_specs=list(in_specs) + plan.in_specs...  354 us
    pallas_call x3, Pallas kernels, exchange(): pl.pallas_call(kernel, out_shape=tuple(plan.out_shape()), in_specs=plan.i...  84.4 us
    pallas_call x4, Pallas kernels, with_aside(): pl.pallas_call(body, grid=grid, in_specs=in_specs, out_specs=out_specs, o...  49.2 us
    dot_general x4, matrix products, grouped(): jnp.einsum('rd,gdc->grc', rows, weight, preferred_element_type=wide_type)  14.2 us
    dot_general x6, matrix products, row_grad(): jnp.einsum('grc,gdc->rd', grads, w_joined[:, :, part * width:(part + 1) *...  13.3 us

profile of v4, /device:TPU:0, one launch (start us, length us, event | category | flops | bytes accessed | tf_op | source)
XLA Modules:
  0.0 616.6 jit_solution(1429954114091421031)
XLA Ops:
  0.7 1.6 slice_reduce_fusion.4
  3.7 1.8 fusion.67
  6.1 0.9 copy-done.63
  7.0 1.7 add_convert_fusion.1
  9.1 1.8 slice_reduce_fusion
  11.6 32.5 %shard_map.434 = bf16[2,16,3,16,1152]{4,3,2,1,0:T(8,128)(2,1)} custom-call(bf16[3,16,1152]{2,1,0:T(8,128)(2,1)} %convert_element_type.177.refs_0_), custom_call_target="tpu_custom_call" | custom-call | bytes 3538944 | tf_op jit(solution)/shard_map/pallas_call | solution.py:510
  44.1 5.6 convert_bitcast_fusion.1.refs_1_.refs_2_
  49.8 3.9 fusion.16.refs_0_
  54.9 0.8 broadcast_in_dim.26.refs_3_.bias_ref
  58.0 74.7 %shard_map.435 = (bf16[1024,768]{1,0:T(8,128)(2,1)}, f32[6,2,1024]{2,1,0:T(2,128)}, bf16[2,16,1,24,768]{4,3,2,1,0:T(8,128)(2,1)}, bf16[16,2,1,24,3072]{4,3,2,1,0:T(8,128)(2,1)}, bf16[16,2,1,96,768]{4,3,2,1,0:T(8,128)(2,1)}) custom-call(bf16[2,1024,384]{2,1,0:T(8,128)(2,1)} %fusion.16.refs_0_, bf16[2,768,768]{2,1,0:T(8,128)(2,1)} %convert_bitcast_fusion.1.refs_1_.refs_2_, ...), custom_call_target="tpu_custom_call" | custom-call | flops 2415919104 | bytes 6291456 | tf_op jit(solution)/shard_map/pallas_call | solution.py:490
  132.7 1.4 fusion.65
  134.1 1.6 convert_element_type.184.refs_6_
  135.7 72.9 %shard_map.436 = (f32[1024,768]{1,0:T(8,128)}, f32[1024,768]{1,0:T(8,128)}, bf16[1024,3072]{1,0:T(8,128)(2,1)}, bf16[2,16,1,48,1152]{4,3,2,1,0:T(8,128)(2,1)}, b...) custom-call(f32[1024,768]{1,0:T(8,128)} %copy-done.2, ...), custom_call_target="tpu_custom_call" | custom-call | flops 10871635968 | bytes 18874368 | tf_op jit(solution)/shard_map/pallas_call | solution.py:490
  208.6 2.3 reduce_sum.231
  213.1 2.0 copy-done.17
  215.1 3.5 convert_bitcast_fusion.k_ref.v_ref
  218.6 1.2 fusion.28.q_ref
  219.8 10.0 %shard_map.437 = (bf16[256,768]{1,0:T(8,128)(2,1)}, f32[6,2,256]{2,1,0:T(2,128)}) custom-call(bf16[2,256,384]{2,1,0:T(8,128)(2,1)} %fusion.28.q_ref, bf16[2,768,768]{2,1,0:T(8,128)(2,1)} %convert_bitcast_fusion.k_ref.v_ref, bf16[2,768,768]{2,1,0:T(8,128)(2,1)} %convert_bitcast_fusion.k_ref.v_ref, bf16[768,128]{1,0:T(8,128)(2,1)} %broadcast_in_dim.26.refs_3_.bias_ref), custom_call_target="tpu_custom_call" | custom-call | flops 603979776 | bytes 1572864 | tf_op jit(solution)/shard_map/pallas_call | solution.py:452
  229.8 11.1 %shard_map.438 = (f32[256,768]{1,0:T(8,128)}, f32[256,768]{1,0:T(8,128)}, bf16[256,3072]{1,0:T(8,128)(2,1)}) custom-call(f32[1024,768]{1,0:T(8,128)} %get-tuple-element.79.res_ref, bf16[256,768]{1,0:T(8,128)(2,1)} %get-tuple-element.80.mixed_ref.o_ref, bf16[768,768]{1,0:T(8,128)(2,1)} %bitcast.150, bf16[768,3072]{1,0:T(8,128)(2,1)} %bitcast.138, ...), custom_call_target="tpu_custom_call" | custom-call | flops 2717908992 | bytes 4718592 | tf_op jit(solution)/shard_map/pallas_call | solution.py:452
  240.9 1.4 reduce_sum.233
  242.3 1.4 multiply_reduce_fusion.9
  243.7 1.7 fusion.68
  246.3 1.6 convolution_convert_fusion.6
  247.9 1.2 multiply_reduce_fusion.7
  249.4 1.0 broadcast_add_fusion.u_ref
  250.5 18.6 %shard_map.439 = (bf16[768,3072]{1,0:T(8,128)(2,1)}, bf16[3072,768]{1,0:T(8,128)(2,1)}, bf16[768,768]{1,0:T(8,128)(2,1)}, bf16[256,768]{1,0:T(8,128)(2,1)}, f32[256,768]{1,0:T(8,128)}, /*index=5*/f32[8,768]{1,0:T(8,128)}) custom-call(f32[256,768]{1,0:T(8,128)} %broadcast_add_fusion.u_ref, f32[256,768]{1,0:T(8,128)} %get-tuple-element.85.middle_ref, ...), custom_call_target="tpu_custom_call" | custom-call | flops 5435817984 | bytes 7864320 | tf_op jit(solution)/shard_map/pallas_call | solution.py:452
  269.0 9.5 %shard_map.440 = (bf16[2,256,384]{2,1,0:T(8,128)(2,1)}, bf16[2,768,384]{2,1,0:T(8,128)(2,1)}, bf16[2,768,384]{2,1,0:T(8,128)(2,1)}) custom-call(bf16[2,256,384]{2,1,0:T(8,128)(2,1)} %fusion.28.q_ref, bf16[2,768,768]{2,1,0:T(8,128)(2,1)} %convert_bitcast_fusion.k_ref.v_ref, bf16[2,768,768]{2,1,0:T(8,128)(2,1)} %convert_bitcast_fusion.k_ref.v_ref, ...), custom_call_target="tpu_custom_call" | custom-call | flops 1509949440 | bytes 3145728 | tf_op jit(solution)/shard_map/pallas_call | solution.py:452
  278.6 1.6 fusion.23
  280.2 2.9 fusion.24
  283.2 1.1 fusion.25
  284.6 3.9 copy.96
  288.5 2.0 convolution_bitcast_fusion
  290.5 2.5 fusion.33
  293.0 2.6 bitcast_add_fusion.2
  295.7 2.5 multiply_reduce_fusion
  298.2 1.7 fusion.61
  300.0 2.0 pad_add_fusion.refs_0_
  302.0 114.2 %shard_map.441 = (bf16[768,3072]{1,0:T(8,128)(2,1)}, bf16[3072,768]{1,0:T(8,128)(2,1)}, bf16[768,768]{1,0:T(8,128)(2,1)}, bf16[1024,768]{1,0:T(8,128)(2,1)}, f32...) custom-call(f32[1024,768]{1,0:T(8,128)} %pad_add_fusion.refs_0_, ...), custom_call_target="tpu_custom_call" | custom-call | flops 21743271936 | bytes 31457280 | tf_op jit(solution)/shard_map/pallas_call | solution.py:490
  416.2 1.4 convert_bitcast_fusion.2.refs_10_
  417.6 92.0 %shard_map.442 = (bf16[2,1024,384]{2,1,0:T(8,128)(2,1)}, bf16[2,768,384]{2,1,0:T(8,128)(2,1)}, bf16[2,768,384]{2,1,0:T(8,128)(2,1)}, f32[1,24,768]{2,1,0:T(8,128...) custom-call(bf16[2,1024,384]{2,1,0:T(8,128)(2,1)} %fusion.16.refs_0_, ...), custom_call_target="tpu_custom_call" | custom-call | flops 6039797760 | bytes 12582912 | tf_op jit(solution)/shard_map/pallas_call | solution.py:490
  509.6 2.9 fusion.30
  512.7 1.1 bitcast_add_fusion.1
  515.1 2.2 multiply_reduce_fusion.1
  517.3 1.5 fusion.60
  523.1 2.9 fusion.20
  526.1 1.1 fusion.26
  527.2 1.1 fusion.27
  528.6 3.8 copy.100
  532.5 38.2 %shard_map.443 = (f32[2,24,1152]{2,1,0:T(8,128)}, f32[1,8,768]{2,1,0:T(8,128)}, f32[1,128]{1,0:T(1,128)}) custom-call(bf16[2,4,2,2,2,24,1152]{6,5,4,3,2,1,0:T(8,128)(2,1)} %bitcast.132, bf16[2,2,2,4,1,8,768]{6,5,4,3,2,1,0:T(8,128)(2,1)} %bitcast.149), custom_call_target="tpu_custom_call" | custom-call | bytes 125829120 | tf_op jit(solution)/shard_map/pallas_call | solution.py:510
  570.6 1.3 add_reduce_fusion
  571.9 1.3 convert_reduce_fusion
  573.2 2.0 select_maximum_fusion
  575.8 1.3 convert_bitcast_fusion.3.refs_0_
  577.2 13.7 %shard_map.444 = (bf16[2,2,2,4,8,768]{5,4,3,2,1,0:T(8,128)(2,1)}, f32[2,2,2,4,8,128]{5,4,3,2,1,0:T(8,128)}) custom-call(bf16[8,768]{1,0:T(8,128)(2,1)} %convert_bitcast_fusion.3.refs_0_, f32[8,128]{1,0:T(8,128)} %broadcast_in_dim.33.refs_1_), custom_call_target="tpu_custom_call" | custom-call | bytes 458752 | tf_op jit(solution)/shard_map/pallas_call | solution.py:510
  590.9 1.1 slice_reduce_fusion.2
  594.7 1.3 convert_multiply_fusion
  596.1 4.8 multiply_add_fusion.1
  600.9 1.4 multiply_add_fusion.3
  603.1 1.4 multiply_add_fusion.5
  604.5 0.8 multiply_add_fusion.9
  606.2 1.2 copy.107
  607.4 1.2 copy.108
  608.7 1.2 copy.109
  610.7 1.1 multiply_add_fusion.7
  (222 shorter events, 19.6 us)
Async XLA Ops:
  2.3 4.8 copy-start.59
  3.0 2.5 copy-start.67
  5.5 3.3 copy-start.2
  5.5 3.2 copy-start.50
  6.1 2.7 copy-start.61
  44.1 5.6 copy-start.18
  49.8 3.9 copy-start.80
  49.8 6.0 copy-start.11
  49.8 6.8 %copy-start.13 = (f32[2,24,3072]{2,1,0:T(8,128)S(1)}, f32[2,24,3072]{2,1,0:T(8,128)}, u32[]{:S(2)}) copy-start(f32[2,24,3072]{2,1,0:T(8,128)} %param.45) | copy-start | bytes 1769476
  53.7 3.6 copy-start.30
  208.6 2.8 copy-start
  212.5 2.6 copy-start.17
  213.1 5.5 copy-start.9
  240.9 2.8 copy-start.5
  240.9 4.5 copy-start.75
  240.9 4.8 copy-start.78
  240.9 5.5 copy-start.4
  240.9 5.4 copy-start.54
  240.9 5.4 copy-start.69
  280.2 2.9 copy-start.10
  280.2 2.9 copy-start.22
  288.5 2.0 copy-start.79
  290.5 2.5 copy-start.23
  293.0 2.6 copy-start.1
  293.0 2.6 copy-start.47
  293.0 2.6 copy-start.53
  293.0 2.6 copy-start.56
  295.7 2.5 copy-start.66
  509.6 2.9 copy-start.7
  509.6 3.0 copy-start.21
  512.7 1.9 copy-start.60
  512.7 1.9 copy-start.62
  512.7 2.4 copy-start.81
  515.1 2.2 copy-start.64
  517.3 1.9 copy-start.8
  519.2 2.2 copy-start.74
  519.2 2.2 copy-start.73
  519.2 2.9 copy-start.72
  519.2 2.9 copy-start.71
  519.9 3.2 copy-start.19
  523.1 3.0 copy-start.82
  590.9 5.1 copy-start.6
  596.0 4.9 copy-start.12
  596.0 4.9 copy-start.26
  596.1 4.9 copy-start.27
  596.1 4.9 copy-start.39
  596.1 4.9 copy-start.41
  600.9 2.1 copy-start.29
  600.9 2.1 copy-start.38
  600.9 2.2 copy-start.40
  602.3 2.2 copy-start.31
  602.3 2.2 copy-start.44
  602.3 2.2 copy-start.45
  602.3 2.2 copy-start.48
  602.3 2.2 copy-start.49
  603.1 2.3 copy-start.43
  603.1 2.4 copy-start.42
  605.9 3.9 copy-start.34
  606.1 3.8 copy-start.37
  606.2 3.8 copy-start.57
  606.2 3.8 copy-start.58
  606.2 4.5 copy-start.20
  606.2 4.5 copy-start.35
  606.2 4.5 copy-start.36
  (19 other events, 27.4 us)

commit v5 on v4

--- a/solution.py
+++ b/solution.py
@@ -84,7 +84,7 @@
             pltpu.SemaphoreType.DMA((n,)),
         ]
 
-    def steps(self, ins, outs, scratch):
+    def steps(self, ins, outs, scratch, meeting=True):
         n, orders = self.n, self.orders
         local_sem, recv, core_recv, send, core_send = scratch
         place = Place()
@@ -125,7 +125,8 @@
 
         def entry(k, ax, ay):
             if (k, ax, ay) == (0, 0, 0):
-                meet(place)
+                if meeting:
+                    meet(place)
             for a in range(n):
                 for c, order in enumerate(orders[a]):
                     chip = place.block(k, ax, ay)
@@ -187,8 +188,8 @@
 
 
 class Reduce:
-    def __init__(self, kinds, orders, shapes):
-        self.kinds, self.orders, self.shapes = kinds, orders, shapes
+    def __init__(self, kinds, orders, shapes, waves):
+        self.kinds, self.orders, self.shapes, self.waves = kinds, orders, shapes, waves
         self.n, self.pieces = len(kinds), max(map(len, orders))
 
     def in_specs(self):
@@ -271,11 +272,12 @@
             if meeting:
                 meet(place)
             squares[...] = jnp.zeros_like(squares)
-            for quarter in QUARTERS:
-                for a, c, order in items:
-                    y, x = at(order, *quarter)
-                    to_core(a, c, y, x).start()
-                    load(a, c, y, x).start()
+            for wave in self.waves:
+                for quarter in QUARTERS:
+                    for a, c, order in (items[i] for i in wave):
+                        y, x = at(order, *quarter)
+                        to_core(a, c, y, x).start()
+                        load(a, c, y, x).start()
 
         def fold(item, quarter):
             a, c, order = item
@@ -322,14 +324,24 @@
                 for d in (1, 2, 3):
                     to_owner(a, c, d).wait_send()
 
-        part = functools.partial
+        def stage(turn, chosen):
+            part = functools.partial
+            if turn < 4:
+                return [part(fold, items[i], QUARTERS[turn]) for i in chosen]
+            if turn < 6:
+                return [part(take_first, items[i], turn == 4) for i in chosen]
+            return [part((take_second, last)[turn - 6], items[i]) for i in chosen]
+
         out = [begin]
-        for quarter in QUARTERS:
-            out += [part(fold, it, quarter) for it in items]
-        for far in (True, False):
-            out += [part(take_first, it, far) for it in items]
-        out += [part(take_second, it) for it in items]
-        return out + [part(last, it) for it in items] + [finish]
+        for w, chosen in enumerate(self.waves):
+            out += stage(0, chosen) + stage(1, chosen)
+            if w > 0:
+                out += stage(5, self.waves[w - 1]) + stage(6, self.waves[w - 1])
+            out += stage(2, chosen) + stage(3, chosen) + stage(4, chosen)
+        out += stage(5, self.waves[-1]) + stage(6, self.waves[-1])
+        for chosen in self.waves:
+            out += stage(7, chosen)
+        return out + [finish]
 
 
 class Spread:
@@ -443,15 +455,16 @@
 
 
 class Aside:
-    def __init__(self, plan, arrays, collective_id):
-        self.plan, self.arrays, self.collective_id = plan, arrays, collective_id
-
-
-def with_aside(body, aside, *, grid, in_specs, out_specs, out_shape, scratch_shapes=(), cost, operands):
+    def __init__(self, plan, arrays, collective_id, pace):
+        self.plan, self.arrays, self.collective_id, self.pace = plan, arrays, collective_id, pace
+
+
+def with_aside(
+    body, aside, *, ticks, grid, in_specs, out_specs, out_shape, scratch_shapes=(), cost, operands):
     if aside is None:
         out = pl.pallas_call(
-            body, grid=grid, in_specs=in_specs, out_specs=out_specs, out_shape=tuple(out_shape),
-            scratch_shapes=scratch_shapes, cost_estimate=cost,
+            functools.partial(body, tick=lambda i: None), grid=grid, in_specs=in_specs, out_specs=out_specs,
+            out_shape=tuple(out_shape), scratch_shapes=scratch_shapes, cost_estimate=cost,
             compiler_params=pltpu.CompilerParams(vmem_limit_bytes=VMEM_ALL))(*operands)
         return out, None
     plan = aside.plan
@@ -471,21 +484,24 @@
         cell = 0
         for axis, extent in enumerate(grid):
             cell = cell * extent + pl.program_id(axis)
-        by_cell = {}
-        for i, step in enumerate(steps):
-            by_cell.setdefault(i * (cells - 1) // (len(steps) - 1), []).append(step)
-        for index in sorted(by_cell):
-            if index < cells - 1:
-                @pl.when(cell == index)
-                def _():
-                    for step in by_cell[index]:
-                        step()
-        body(*ins, *outs, *scratch)
+        by_slot = {}
+        for i, step in enumerate(steps[:-1]):
+            at = (i / (len(steps) - 1)) ** aside.pace
+            by_slot.setdefault(int(at * cells * ticks), []).append(step)
+
+        def tick(i):
+            for slot in sorted(by_slot):
+                if slot % ticks == i:
+                    @pl.when(cell == slot // ticks)
+                    def _():
+                        for step in by_slot[slot]:
+                            step()
+
+        body(*ins, *outs, *scratch, tick=tick)
 
         @pl.when(cell == cells - 1)
         def _():
-            for step in by_cell[cells - 1]:
-                step()
+            steps[-1]()
 
     out = pl.pallas_call(
         kernel, grid=grid,
@@ -523,8 +539,9 @@
     return Gather(by_core, orders, [a.shape for a in arrays], arrays[0].dtype)
 
 
-def reduce_plan(arrays, kinds, orders):
-    return Reduce(kinds, orders, [a.shape[2:] for a in arrays]), [as_grid(a, kind) for a, kind in zip(arrays, kinds)]
+def reduce_plan(arrays, kinds, orders, waves):
+    plan = Reduce(kinds, orders, [a.shape[2:] for a in arrays], waves)
+    return plan, [as_grid(a, kind) for a, kind in zip(arrays, kinds)]
 
 
 def spread_plan(arrays):
@@ -535,8 +552,8 @@
     return exchange(gather_plan(arrays, by_core, orders), arrays, collective_id)
 
 
-def reduce_scatter_layer(arrays, kinds, orders, collective_id):
-    plan, operands = reduce_plan(arrays, kinds, orders)
+def reduce_scatter_layer(arrays, kinds, orders, waves, collective_id):
+    plan, operands = reduce_plan(arrays, kinds, orders, waves)
     return exchange(plan, operands, collective_id)
 
 
@@ -593,12 +610,13 @@
     return mine, lane == (HD if head == 0 else 0)
 
 
-def attend_kernel(q_ref, k_ref, v_ref, bias_ref, out_ref, lse_ref):
+def attend_kernel(q_ref, k_ref, v_ref, bias_ref, out_ref, lse_ref, *, tick):
     q_block = q_ref[0] * jnp.asarray(HD ** -0.5, low_type)
     k_block, v_block, bias = k_ref[0], v_ref[0], bias_ref[...]
     v_turned = v_block.T
     parts = []
     for head in range(2):
+        tick(head)
         q_mine, q_one = head_lanes(q_block.shape, head)
         k_mine, _ = head_lanes(k_block.shape, head)
         one = jnp.where(q_one, jnp.ones_like(q_block), jnp.zeros_like(q_block))
@@ -620,6 +638,7 @@
     (mixed, lse), extra = with_aside(
         attend_kernel,
         aside,
+        ticks=2,
         grid=grid,
         in_specs=[
             pl.BlockSpec((1, block, 128), lambda p, i: (p // pairs, i, p % pairs)),
@@ -643,7 +662,7 @@
     return mixed, lse, extra
 
 
-def attend_back_kernel(q_ref, k_ref, v_ref, bias_ref, g_ref, o_ref, lse_ref, gq_ref, gk_ref, gv_ref, k_sum, v_sum):
+def attend_back_kernel(q_ref, k_ref, v_ref, bias_ref, g_ref, o_ref, lse_ref, gq_ref, gk_ref, gv_ref, k_sum, v_sum, *, tick):
     step = pl.program_id(1)
 
     @pl.when(step == 0)
@@ -659,6 +678,7 @@
     both = (g_block.astype(wide_type) * o_ref[...].astype(wide_type)).T
     parts = []
     for head in range(2):
+        tick(head)
         q_mine, q_one = head_lanes(q_block.shape, head)
         k_mine, _ = head_lanes(k_block.shape, head)
         nothing = jnp.zeros_like(q_block)
@@ -690,6 +710,7 @@
     grads, extra = with_aside(
         attend_back_kernel,
         aside,
+        ticks=2,
         grid=grid,
         in_specs=[
             pl.BlockSpec((1, block, 128), lambda p, i: (p // pairs, i, p % pairs)),
@@ -732,9 +753,10 @@
     return center, lax.rsqrt(jnp.mean(center * center, -1, keepdims=True) + eps_norm)
 
 
-def mlp_kernel(res_ref, mixed_ref, mix_ref, up_ref, down_ref, vec_ref, out_ref, middle_ref, hidden_ref, normed, total):
+def mlp_kernel(res_ref, mixed_ref, mix_ref, up_ref, down_ref, vec_ref, out_ref, middle_ref, hidden_ref, normed, total, *, tick):
     step, last = pl.program_id(1), pl.num_programs(1) - 1
     size = hidden_ref.shape[1]
+    tick(0)
 
     @pl.when(step == 0)
     def _():
@@ -749,6 +771,7 @@
     hidden_ref[...] = hidden.astype(low_type)
     inner = jnp.tanh(GELU_K * (hidden + GELU_C * hidden * hidden * hidden))
     active = (0.5 * hidden * (1.0 + inner)).astype(low_type)
+    tick(1)
     total[...] += matmul(active, down_ref[part, :])
 
     @pl.when(step == last)
@@ -770,6 +793,7 @@
     outs, extra = with_aside(
         mlp_kernel,
         aside,
+        ticks=2,
         grid=(rows // block, wide // chunk),
         in_specs=[
             pl.BlockSpec((block, width), lambda i, j: (i + skip, 0)), row_spec,
@@ -792,11 +816,12 @@
 def mlp_back_kernel(
     u_ref, middle_ref, mixed_ref, mix_ref, up_ref, down_ref, vec_ref, hidden_ref,
     up_grad_ref, down_grad_ref, mix_grad_ref, mixed_grad_ref, mid_grad_ref, vec_grad_ref,
-    u_low, normed_turned, normed_grad,
+    u_low, normed_turned, normed_grad, *, tick,
 ):
     step, last = pl.program_id(0), pl.num_programs(0) - 1
     rows, width = u_ref.shape
     block = 256
+    tick(0)
 
     @pl.when(step == 0)
     def _():
@@ -817,7 +842,9 @@
     slope = half + 0.5 * hidden * (1.0 - inner * inner) * (GELU_K * (1.0 + 3.0 * GELU_C * square))
     grad = (matmul_nt(u_low[...], down_ref[...]) * slope).astype(low_type)
     down_grad_ref[...] = matmul(active.T, u_low[...]).astype(low_type)
+    tick(1)
     up_grad_ref[...] = matmul(normed_turned[...], grad).astype(low_type)
+    tick(2)
     normed_grad[...] += matmul_nt(grad, up_ref[...])
 
     @pl.when(step == last)
@@ -862,6 +889,7 @@
     return with_aside(
         mlp_back_kernel,
         aside,
+        ticks=3,
         grid=(wide // chunk,),
         in_specs=[
             whole(row_shape), whole(row_shape), whole(row_shape), whole(square), up_spec, down_spec,
@@ -914,8 +942,8 @@
         return jnp.einsum(
             "grc,gdc->rd", grads, w_joined[:, :, part * width : (part + 1) * width], preferred_element_type=wide_type)
 
-    grad_joined = jnp.concatenate(
-        [weight_grad(normed[first:], grad_q), weight_grad(normed[:CTX], grad_k), weight_grad(normed[:CTX], grad_v)], 2)
+    grads_joined = (
+        weight_grad(normed[first:], grad_q), weight_grad(normed[:CTX], grad_k), weight_grad(normed[:CTX], grad_v))
     from_q = row_grad(grad_q, 0)
     from_kv = row_grad(grad_k, 1) + row_grad(grad_v, 2)
     rows = residual.shape[0]
@@ -925,7 +953,7 @@
     grad_input, gain_attn, shift_attn = norm_back(residual, vec_rows[0], vec_rows[1], grad_normed)
     vec_grads = [gain_attn, shift_attn, mlp_vec[0], mlp_vec[1], mlp_vec[2], mlp_vec[3]]
     grad_out = grad_input + jnp.concatenate([below, grad_middle], 0)
-    return grad_out, (extra, more), (grad_joined, grad_mix, grad_grow, grad_shrink), vec_grads
+    return grad_out, (extra, more), grads_joined + (grad_mix, grad_grow, grad_shrink), vec_grads
 
 
 def update(weight, moment_old, average, grad_in, scale):
@@ -936,8 +964,10 @@
 
 
 BY_CORE = (True, True, False, False)
-ROUTES = (("zxy",), ("zxy",), ("xzy",), ("yzx",))
-REDUCE_ROUTES = (("zxy",), ("zyx",), ("zyx",), ("zxy",))
+GATHER_ROUTES = (("zxy",), ("zxy",), ("xzy",), ("yzx",))
+FORE_PACE, BACK_PACE = (1.0, 1.0), (1.0, 1.0)
+BY_GRAD = (True, True, True, True, False, False)
+ROUTES = (("zxy",), ("zyx",), ("zxy",), ("zyx",), ("zyx",), ("zxy",))
 
 
 def whole_gather(shard_list, by_core):
@@ -993,14 +1023,15 @@
     own = [own_weights(at) for at in range(layer_total)]
     forward_asides = [[None, None] for _ in own]
     if direct:
-        joined = own[0][0].reshape((3, joined_rows // 3, kinds))
-        weights = [as_joined(all_gather_layer([joined], (True,), (("xzy", "yzx", "zxy"),), 1)[0])]
+        joined = own[0][0].reshape((2, joined_rows // 2, kinds))
+        weights = [as_joined(all_gather_layer([joined], (True,), (("zxy", "zyx"),), 1)[0])]
         for at, layer in enumerate(own):
             if at == 0:
                 forward_asides[at][0] = Aside(
-                    gather_plan(layer[1:], BY_CORE[1:], (("xzy",), ("zxy",), ("zyx",))), layer[1:], 2)
+                    gather_plan(layer[1:], BY_CORE[1:], (("zxy",), ("xzy",), ("yzx",))), layer[1:], 2, FORE_PACE[0])
             else:
-                forward_asides[at - 1][1] = Aside(gather_plan(layer, BY_CORE, ROUTES), layer, 10 + at)
+                forward_asides[at - 1][1] = Aside(
+                    gather_plan(layer, BY_CORE, GATHER_ROUTES), layer, 10 + at, FORE_PACE[1])
     else:
         gathered = [whole_gather(o, BY_CORE) for o in own]
         weights = [as_joined(g[0]) + as_rest(g[1:]) for g in gathered]
@@ -1036,7 +1067,7 @@
         residual, vectors[-2], vectors[-1], matmul_nt(grad_logits, head_low))
 
     devices = chips * cores
-    rows_list = [joined_rows, w_out.shape[2], w_up.shape[1], w_down.shape[1]]
+    rows_list = [joined_rows] * 3 + [w_out.shape[2], w_up.shape[1], w_down.shape[1]]
     sums = [None] * layer_total
     vec_grads = [None] * layer_total
     squares = []
@@ -1050,23 +1081,24 @@
                 return None
             if turn == 0:
                 blocks = as_blocks(
-                    list(above) + [grad_head], BY_CORE + (False,), rows_list + [w_head.shape[0] // devices],
-                    REDUCE_ROUTES + (("zyx",),))
-                plan, operands = reduce_plan(blocks, BY_CORE + ("group",), REDUCE_ROUTES + (("zyx",),))
-                return Aside(plan, operands, 3)
-            blocks = as_blocks(ready, BY_CORE[1:], rows_list[1:], REDUCE_ROUTES[1:])
-            plan, operands = reduce_plan(blocks, BY_CORE[1:], REDUCE_ROUTES[1:])
-            head_sum = [earlier[4][0].astype(low_type)]
-            return Aside(Both(plan, spread_plan(head_sum)), operands + head_sum, 7)
+                    list(above) + [grad_head], BY_GRAD + (False,), rows_list + [w_head.shape[0] // devices],
+                    ROUTES + (("zyx",),))
+                plan, operands = reduce_plan(
+                    blocks, BY_GRAD + ("group",), ROUTES + (("zyx",),), ((4, 5), (0, 1, 2, 3, 6)))
+                return Aside(plan, operands, 3, BACK_PACE[0])
+            blocks = as_blocks(ready, BY_GRAD[3:], rows_list[3:], ROUTES[3:])
+            plan, operands = reduce_plan(blocks, BY_GRAD[3:], ROUTES[3:], ((1, 2), (0,)))
+            head_sum = [earlier[6][0].astype(low_type)]
+            return Aside(Both(plan, spread_plan(head_sum)), operands + head_sum, 7, BACK_PACE[1])
 
         upstream, extra, big, vec_grads[at] = layer_backward(
             upstream, kept_all[at], first, vectors[2 + 6 * at : 8 + 6 * at], weights[at], bias, make_asides)
         if not direct:
-            sums[at] = whole_scatter(big, BY_CORE, rows_list)
+            sums[at] = whole_scatter(big, BY_GRAD, rows_list)
         elif extra[0] is not None:
-            sums[at + 1] = list(extra[0][:4])
+            sums[at + 1] = list(extra[0][:6])
             sums[at] = list(extra[1][:3])
-            squares += [extra[0][5], extra[1][3]]
+            squares += [extra[0][7], extra[1][3]]
             head_all = extra[1][4]
     grad_emb = matmul_tn(masked, upstream.astype(low_type))
     vec_list = [jnp.sum(upstream * leading, 0), jnp.sum(upstream, 0)]
@@ -1080,10 +1112,10 @@
         n_small = -(-(feats + vec_total) // (8 * devices)) * 8
         small = jnp.concatenate([grad_emb, grad_vec], 0).astype(low_type)
         small = jnp.pad(small, ((0, n_small * devices - feats - vec_total), (0, 0)))
-        kinds_last, routes = (True, "group"), (("zxy", "zyx"), ("zyx",))
-        blocks = as_blocks([big[0], small], (True, False), [joined_rows, n_small], routes)
-        qkv_sum, small_sum, square = reduce_scatter_layer(blocks, kinds_last, routes, 4)
-        sums[0] = [qkv_sum] + sums[0]
+        kinds_last, routes = BY_GRAD[:3] + ("group",), ROUTES[:3] + (("zyx",),)
+        blocks = as_blocks(list(big[:3]) + [small], BY_GRAD[:3] + (False,), rows_list[:3] + [n_small], routes)
+        *joined_sums, small_sum, square = reduce_scatter_layer(blocks, kinds_last, routes, ((0, 1, 2, 3),), 4)
+        sums[0] = joined_sums + sums[0]
         scalars = jnp.stack([jnp.sum(sum(squares + [square]))] + scalars)
         scalars = jnp.broadcast_to(jnp.pad(scalars, (0, 125))[None], (8, 128))
         last_parts = [small_sum[0].astype(low_type), scalars]
@@ -1105,16 +1137,21 @@
     grad_norm = jnp.sqrt(totals[0]) / pooled
     scale = jnp.minimum(1.0, clip_at / grad_norm) / pooled
 
+    def joined_update(weight, moment_old, average):
+        grad = jnp.stack([jnp.stack([p.reshape((joined_rows, -1)) for p in sums[at][:3]], 1) for at in range(layer_total)])
+        flat = [a.reshape((-1, 128)) for a in (weight, moment_old, average, grad)]
+        return [a.reshape(weight.shape) for a in update(*flat, scale)]
+
     def big_update(weight, moment_old, average, kind):
         grad = jnp.stack([sums[at][kind].reshape(weight.shape[1:]) for at in range(layer_total)])
         return update(weight, moment_old, average, grad, scale)
 
     e_w, e_m, e_a = update(w_emb, m_emb, a_emb, grad_emb, scale)
     v_w, v_m, v_a = update(vectors, m_vec, a_vec, grad_vec, scale)
-    q_w, q_m, q_a = big_update(w_qkv, m_qkv, a_qkv, 0)
-    o_w, o_m, o_a = big_update(w_out, m_out, a_out, 1)
-    u_w, u_m, u_a = big_update(w_up, m_up, a_up, 2)
-    d_w, d_m, d_a = big_update(w_down, m_down, a_down, 3)
+    q_w, q_m, q_a = joined_update(w_qkv, m_qkv, a_qkv)
+    o_w, o_m, o_a = big_update(w_out, m_out, a_out, 3)
+    u_w, u_m, u_a = big_update(w_up, m_up, a_up, 4)
+    d_w, d_m, d_a = big_update(w_down, m_down, a_down, 5)
     h_w, h_m, h_a = update(w_head, m_head, a_head, grad_head, scale)
     return (
         loss, grad_norm, e_w, e_m, e_a, v_w, v_m, v_a, q_w, q_m, q_a, o_w, o_m, o_a,

time: 623 us -> 604 us (0.970)
  Pallas kernels: 487 us -> 466 us
    pallas_call x4, Pallas kernels: 354 us -> 336 us  [with_aside(): pl.pallas_call(kernel, grid=grid, in_specs=list(in_specs) + plan.in_specs...]
    convert_element_type x0 -> x6, local copies, waits for them, and re-layouts: none -> 9.45 us  [weight_grad(): jnp.einsum('rd,grc->gdc', rows, grads, preferred_element_type=wide_type)]
    concatenate x2 -> x0, local copies, waits for them, and re-layouts: 7.72 us -> none  [layer_backward(): jnp.concatenate([weight_grad(normed[first:], grad_q), weight_grad(normed[...]
where the time goes in v5:
time: 604 us; the launch traced here: 598 us
  Pallas kernels  466 us (77%)
  matrix products  46.9 us (8%)
  other arithmetic  41.7 us (7%)
  local copies, waits for them, and re-layouts  34.7 us (6%)
  between operations  8.32 us (1%)
    pallas_call x4, Pallas kernels, with_aside(): pl.pallas_call(kernel, grid=grid, in_specs=list(in_specs) + plan.in_specs...  336 us
    pallas_call x3, Pallas kernels, exchange(): pl.pallas_call(kernel, out_shape=tuple(plan.out_shape()), in_specs=plan.i...  81.4 us
    pallas_call x4, Pallas kernels, with_aside(): pl.pallas_call(functools.partial(body, tick=lambda i: None), grid=grid, i...  49.2 us
    dot_general x4, matrix products, grouped(): jnp.einsum('rd,gdc->grc', rows, weight, preferred_element_type=wide_type)  14.2 us
    dot_general x6, matrix products, row_grad(): jnp.einsum('grc,gdc->rd', grads, w_joined[:, :, part * width:(part + 1) *...  13.1 us
    dot_general x6, matrix products, weight_grad(): jnp.einsum('rd,grc->gdc', rows, grads, preferred_element_type=wide_type)  13 us

profile of v5, /device:TPU:0, one launch (start us, length us, event | category | flops | bytes accessed | tf_op | source)
XLA Modules:
  0.0 597.9 jit_solution(1443363802188101758)
XLA Ops:
  0.7 1.6 slice_reduce_fusion.4
  3.7 1.8 fusion.67
  7.0 1.7 add_convert_fusion.1
  9.0 1.8 slice_reduce_fusion
  11.6 32.2 %shard_map.434 = bf16[2,16,2,24,1152]{4,3,2,1,0:T(8,128)(2,1)} custom-call(bf16[2,24,1152]{2,1,0:T(8,128)(2,1)} %convert_element_type.177.refs_0_), custom_call_target="tpu_custom_call" | custom-call | bytes 3538944 | tf_op jit(solution)/shard_map/pallas_call | solution.py:526
  43.8 5.6 convert_bitcast_fusion.1.refs_1_.refs_2_
  49.4 3.9 fusion.16.refs_0_
  57.6 69.9 %shard_map.435 = (bf16[1024,768]{1,0:T(8,128)(2,1)}, f32[6,2,1024]{2,1,0:T(2,128)}, bf16[2,16,1,24,768]{4,3,2,1,0:T(8,128)(2,1)}, bf16[16,2,1,24,3072]{4,3,2,1,0:T(8,128)(2,1)}, bf16[16,2,1,96,768]{4,3,2,1,0:T(8,128)(2,1)}) custom-call(bf16[2,1024,384]{2,1,0:T(8,128)(2,1)} %fusion.16.refs_0_, bf16[2,768,768]{2,1,0:T(8,128)(2,1)} %convert_bitcast_fusion.1.refs_1_.refs_2_, ...), custom_call_target="tpu_custom_call" | custom-call | flops 2415919104 | bytes 6291456 | tf_op jit(solution)/shard_map/pallas_call | solution.py:506
  127.6 1.4 fusion.65
  129.0 1.6 convert_element_type.184.refs_6_
  130.6 78.2 %shard_map.436 = (f32[1024,768]{1,0:T(8,128)}, f32[1024,768]{1,0:T(8,128)}, bf16[1024,3072]{1,0:T(8,128)(2,1)}, bf16[2,16,1,48,1152]{4,3,2,1,0:T(8,128)(2,1)}, b...) custom-call(f32[1024,768]{1,0:T(8,128)} %copy-done.2, ...), custom_call_target="tpu_custom_call" | custom-call | flops 10871635968 | bytes 18874368 | tf_op jit(solution)/shard_map/pallas_call | solution.py:506
  208.8 2.3 reduce_sum.231
  213.3 2.0 copy-done.17
  215.3 3.5 convert_bitcast_fusion.k_ref.v_ref
  218.8 1.2 fusion.28.q_ref
  220.0 10.0 %shard_map.437 = (bf16[256,768]{1,0:T(8,128)(2,1)}, f32[6,2,256]{2,1,0:T(2,128)}) custom-call(bf16[2,256,384]{2,1,0:T(8,128)(2,1)} %fusion.28.q_ref, bf16[2,768,768]{2,1,0:T(8,128)(2,1)} %convert_bitcast_fusion.k_ref.v_ref, bf16[2,768,768]{2,1,0:T(8,128)(2,1)} %convert_bitcast_fusion.k_ref.v_ref, bf16[768,128]{1,0:T(8,128)(2,1)} %broadcast_in_dim.26.refs_3_.bias_ref), custom_call_target="tpu_custom_call" | custom-call | flops 603979776 | bytes 1572864 | tf_op jit(solution)/shard_map/pallas_call | solution.py:465
  229.9 11.1 %shard_map.438 = (f32[256,768]{1,0:T(8,128)}, f32[256,768]{1,0:T(8,128)}, bf16[256,3072]{1,0:T(8,128)(2,1)}) custom-call(f32[1024,768]{1,0:T(8,128)} %get-tuple-element.83.res_ref, bf16[256,768]{1,0:T(8,128)(2,1)} %get-tuple-element.84.mixed_ref.o_ref, bf16[768,768]{1,0:T(8,128)(2,1)} %bitcast.168, bf16[768,3072]{1,0:T(8,128)(2,1)} %bitcast.154, ...), custom_call_target="tpu_custom_call" | custom-call | flops 2717908992 | bytes 4718592 | tf_op jit(solution)/shard_map/pallas_call | solution.py:465
  241.1 1.4 reduce_sum.233
  242.5 1.4 multiply_reduce_fusion.9
  243.9 1.7 fusion.68
  246.5 1.6 convolution_convert_fusion.6
  248.1 1.1 multiply_reduce_fusion.7
  249.6 1.0 broadcast_add_fusion.u_ref
  250.6 18.6 %shard_map.439 = (bf16[768,3072]{1,0:T(8,128)(2,1)}, bf16[3072,768]{1,0:T(8,128)(2,1)}, bf16[768,768]{1,0:T(8,128)(2,1)}, bf16[256,768]{1,0:T(8,128)(2,1)}, f32[256,768]{1,0:T(8,128)}, /*index=5*/f32[8,768]{1,0:T(8,128)}) custom-call(f32[256,768]{1,0:T(8,128)} %broadcast_add_fusion.u_ref, f32[256,768]{1,0:T(8,128)} %get-tuple-element.89.middle_ref, ...), custom_call_target="tpu_custom_call" | custom-call | flops 5435817984 | bytes 7864320 | tf_op jit(solution)/shard_map/pallas_call | solution.py:465
  269.2 9.5 %shard_map.440 = (bf16[2,256,384]{2,1,0:T(8,128)(2,1)}, bf16[2,768,384]{2,1,0:T(8,128)(2,1)}, bf16[2,768,384]{2,1,0:T(8,128)(2,1)}) custom-call(bf16[2,256,384]{2,1,0:T(8,128)(2,1)} %fusion.28.q_ref, bf16[2,768,768]{2,1,0:T(8,128)(2,1)} %convert_bitcast_fusion.k_ref.v_ref, bf16[2,768,768]{2,1,0:T(8,128)(2,1)} %convert_bitcast_fusion.k_ref.v_ref, ...), custom_call_target="tpu_custom_call" | custom-call | flops 1509949440 | bytes 3145728 | tf_op jit(solution)/shard_map/pallas_call | solution.py:465
  278.8 2.7 fusion.25
  281.5 1.4 copy.61
  283.2 2.4 fusion.24
  285.6 1.4 copy.59
  287.5 1.4 copy.57
  289.0 1.8 convolution_bitcast_fusion
  290.8 2.5 fusion.33
  293.3 2.6 bitcast_add_fusion.2
  295.9 2.5 multiply_reduce_fusion
  298.5 1.7 fusion.61
  300.2 2.0 pad_add_fusion.refs_0_
  302.3 104.8 %shard_map.441 = (bf16[768,3072]{1,0:T(8,128)(2,1)}, bf16[3072,768]{1,0:T(8,128)(2,1)}, bf16[768,768]{1,0:T(8,128)(2,1)}, bf16[1024,768]{1,0:T(8,128)(2,1)}, f32...) custom-call(f32[1024,768]{1,0:T(8,128)} %pad_add_fusion.refs_0_, ...), custom_call_target="tpu_custom_call" | custom-call | flops 21743271936 | bytes 31457280 | tf_op jit(solution)/shard_map/pallas_call | solution.py:506
  407.1 1.4 convert_bitcast_fusion.2.refs_10_
  408.5 82.8 %shard_map.442 = (bf16[2,1024,384]{2,1,0:T(8,128)(2,1)}, bf16[2,768,384]{2,1,0:T(8,128)(2,1)}, bf16[2,768,384]{2,1,0:T(8,128)(2,1)}, f32[1,24,768]{2,1,0:T(8,128...) custom-call(bf16[2,1024,384]{2,1,0:T(8,128)(2,1)} %fusion.16.refs_0_, ...), custom_call_target="tpu_custom_call" | custom-call | flops 6039797760 | bytes 12582912 | tf_op jit(solution)/shard_map/pallas_call | solution.py:506
  491.3 2.9 fusion.30
  494.4 1.1 bitcast_add_fusion.1
  496.8 2.2 multiply_reduce_fusion.1
  499.0 1.5 fusion.60
  504.8 2.1 fusion.27
  506.9 2.4 copy.67
  509.3 2.4 fusion.26
  511.7 1.4 copy.65
  513.1 2.8 fusion.20
  516.0 1.4 copy.63
  517.4 35.2 %shard_map.443 = (f32[1,48,384]{2,1,0:T(8,128)}, f32[1,48,384]{2,1,0:T(8,128)}, f32[1,48,384]{2,1,0:T(8,128)}, f32[1,8,768]{2,1,0:T(8,128)}, f32[1,128]{1,0:T(1,128)}) custom-call(bf16[2,4,2,2,1,48,384]{6,5,4,3,2,1,0:T(8,128)(2,1)} %bitcast.153, bf16[2,4,2,2,1,48,384]{6,5,4,3,2,1,0:T(8,128)(2,1)} %bitcast.152, bf16[2,4,2,2,1,48,384]{6,5,4,3,2,1,0:T(8,128)(2,1)} %bitcast.151, ...), custom_call_target="tpu_custom_call" | custom-call | bytes 125829120 | tf_op jit(solution)/shard_map/pallas_call | solution.py:526
  552.6 1.3 add_reduce_fusion
  553.9 1.3 convert_reduce_fusion
  555.1 2.0 select_maximum_fusion
  557.8 1.3 convert_bitcast_fusion.3.refs_0_
  559.1 13.9 %shard_map.444 = (bf16[2,2,2,4,8,768]{5,4,3,2,1,0:T(8,128)(2,1)}, f32[2,2,2,4,8,128]{5,4,3,2,1,0:T(8,128)}) custom-call(bf16[8,768]{1,0:T(8,128)(2,1)} %convert_bitcast_fusion.3.refs_0_, f32[8,128]{1,0:T(8,128)} %broadcast_in_dim.33.refs_1_), custom_call_target="tpu_custom_call" | custom-call | bytes 458752 | tf_op jit(solution)/shard_map/pallas_call | solution.py:526
  573.1 1.1 slice_reduce_fusion.2
  576.8 1.3 convert_multiply_fusion
  578.2 4.8 multiply_add_fusion.1
  583.1 1.4 multiply_add_fusion.3
  585.3 1.4 multiply_add_fusion.5
  587.9 1.2 copy.72
  589.1 1.2 copy.73
  590.4 1.2 copy.74
  592.4 1.1 multiply_add_fusion.7
  (227 shorter events, 21.8 us)
Async XLA Ops:
  2.3 4.7 copy-start.63
  3.0 2.5 copy-start.71
  5.5 3.2 copy-start.2
  5.5 3.2 copy-start.54
  6.1 2.6 copy-start.65
  43.8 5.6 copy-start.18
  49.4 3.9 copy-start.84
  49.4 6.0 %copy-start.11 = (f32[2,96,768]{2,1,0:T(8,128)S(1)}, f32[2,96,768]{2,1,0:T(8,128)}, u32[]{:S(2)}) copy-start(f32[2,96,768]{2,1,0:T(8,128)} %param.48) | copy-start | bytes 1769476
  49.4 6.8 %copy-start.13 = (f32[2,24,3072]{2,1,0:T(8,128)S(1)}, f32[2,24,3072]{2,1,0:T(8,128)}, u32[]{:S(2)}) copy-start(f32[2,24,3072]{2,1,0:T(8,128)} %param.45) | copy-start | bytes 1769476
  53.4 3.6 copy-start.30
  208.8 2.8 copy-start
  212.7 2.6 copy-start.17
  213.3 5.5 copy-start.9
  241.0 2.8 copy-start.5
  241.0 4.5 copy-start.79
  241.0 4.8 copy-start.82
  241.1 5.4 copy-start.4
  241.1 5.4 copy-start.58
  241.1 5.4 copy-start.73
  287.5 3.2 copy-start.83
  290.8 2.5 copy-start.23
  293.3 2.6 copy-start.1
  293.3 2.6 copy-start.45
  293.3 2.6 copy-start.57
  293.3 2.6 copy-start.60
  295.9 2.5 copy-start.70
  491.3 2.9 copy-start.7
  491.3 3.0 copy-start.22
  494.4 2.4 copy-start.85
  496.8 2.2 copy-start.68
  500.9 2.2 copy-start.78
  500.9 2.2 copy-start.77
  500.9 2.9 copy-start.76
  500.9 2.9 copy-start.75
  501.6 3.2 copy-start.19
  573.0 5.1 copy-start.6
  578.1 4.9 copy-start.12
  578.2 4.9 copy-start.26
  578.2 4.9 copy-start.27
  578.2 4.9 copy-start.39
  578.2 4.9 copy-start.41
  583.0 2.1 copy-start.38
  583.0 2.2 copy-start.40
  584.4 2.2 copy-start.31
  584.4 2.2 copy-start.42
  584.4 2.2 copy-start.43
  584.5 2.2 copy-start.49
  584.5 2.2 copy-start.50
  585.2 2.3 copy-start.46
  585.2 2.3 copy-start.47
  585.2 2.3 copy-start.48
  585.2 2.3 copy-start.51
  585.2 2.3 copy-start.52
  585.2 2.3 copy-start.53
  585.2 2.4 copy-start.16
  585.3 2.4 copy-start.32
  585.3 2.3 copy-start.33
  587.6 4.0 copy-start.34
  587.8 3.8 copy-start.37
  587.9 3.8 copy-start.61
  587.9 3.8 copy-start.62
  587.9 4.5 copy-start.20
  587.9 4.5 copy-start.35
  587.9 4.5 copy-start.36
  (22 other events, 34.3 us)

commit v6 on v5

--- a/solution.py
+++ b/solution.py
@@ -913,6 +913,87 @@
     )
 
 
+def joined_back_kernel(
+    first, normed_ref, res_ref, mid_ref, vec_ref, w_ref, q_ref, k_ref, v_ref,
+    wq_ref, wk_ref, wv_ref, out_ref, vec_grad_ref, turned, grads,
+):
+    group, last = pl.program_id(0), pl.num_programs(0) - 1
+    rows, width = res_ref.shape
+    part = w_ref.shape[2] // 3
+    block = 256
+
+    @pl.when(group == 0)
+    def _():
+        @pl.loop(0, rows // block)
+        def _(i):
+            at = pl.ds(pl.multiple_of(i * block, block), block)
+            turned[:, at] = normed_ref[at, :].T
+
+    wq_ref[0] = matmul(turned[:, first:], q_ref[0]).astype(low_type)
+    wk_ref[0] = matmul(turned[:, :CTX], k_ref[0]).astype(low_type)
+    wv_ref[0] = matmul(turned[:, :CTX], v_ref[0]).astype(low_type)
+    for start in range(0, rows, block):
+        total = jnp.zeros((block, width), wide_type)
+        if start >= first:
+            total += matmul_nt(q_ref[0, start - first : start - first + block], w_ref[0, :, :part])
+        if start < CTX:
+            total += matmul_nt(k_ref[0, start : start + block], w_ref[0, :, part : 2 * part])
+            total += matmul_nt(v_ref[0, start : start + block], w_ref[0, :, 2 * part :])
+        at = slice(start, start + block)
+
+        @pl.when(group == 0)
+        def _():
+            grads[at] = total
+
+        @pl.when(group > 0)
+        def _():
+            grads[at] += total
+
+    @pl.when(group == last)
+    def _():
+        vec_grad_ref[...] = jnp.zeros_like(vec_grad_ref)
+        for start in range(0, rows, block):
+            at = slice(start, start + block)
+            center, spread = center_scale(res_ref[at])
+            shape = center * spread
+            here = grads[at]
+            scaled = here * vec_ref[0:1]
+            total = spread * (
+                scaled - jnp.mean(scaled, -1, keepdims=True) - shape * jnp.mean(scaled * shape, -1, keepdims=True))
+            if start >= first:
+                total += mid_ref[start - first : start - first + block]
+            out_ref[at] = total
+            vec_grad_ref[0:1] += jnp.sum(here * shape, 0, keepdims=True)
+            vec_grad_ref[1:2] += jnp.sum(here, 0, keepdims=True)
+
+
+def joined_backward(first, normed, residual, grad_middle, vec_rows, w_joined, grads):
+    groups, width, kinds = w_joined.shape
+    rows = residual.shape[0]
+
+    def whole(a):
+        return pl.BlockSpec(a.shape, lambda g: (0, 0), pipeline_mode=pl.Buffered(1))
+
+    def of_group(shape):
+        return pl.BlockSpec((1,) + shape[1:], lambda g: (g, 0, 0))
+
+    weight_shape = (groups, width, kinds // 3)
+    return pl.pallas_call(
+        functools.partial(joined_back_kernel, first),
+        grid=(groups,),
+        in_specs=[whole(a) for a in (normed, residual, grad_middle, vec_rows)] + [
+            of_group(a.shape) for a in (w_joined,) + grads],
+        out_specs=[of_group(weight_shape)] * 3 + [
+            pl.BlockSpec(shape, lambda g: (0, 0)) for shape in (residual.shape, (8, width))],
+        out_shape=(jax.ShapeDtypeStruct(weight_shape, low_type),) * 3 + (
+            jax.ShapeDtypeStruct(residual.shape, wide_type), jax.ShapeDtypeStruct((8, width), wide_type)),
+        scratch_shapes=[pltpu.VMEM((width, rows), low_type), pltpu.VMEM((rows, width), wide_type)],
+        cost_estimate=pl.CostEstimate(
+            flops=4 * rows * width * kinds * groups, bytes_accessed=rows * width * 30, transcendentals=rows),
+        compiler_params=pltpu.CompilerParams(vmem_limit_bytes=VMEM_ALL),
+    )(normed, residual, grad_middle, vec_rows, w_joined, *grads)
+
+
 def layer_forward(residual, first, vec_rows, weights, bias, asides, as_rest):
     w_joined = weights[0]
     width = w_joined.shape[2] // 3
@@ -934,6 +1015,12 @@
     grad_grow, grad_shrink, grad_mix, grad_mixed, grad_middle, mlp_vec = outs
     grad_q, grad_k, grad_v, more = attend_back(
         queries, keys_values, bias, grad_mixed, mixed, lse, make_asides(1, (grad_mix, grad_grow, grad_shrink), extra))
+
+    if first > 0:
+        *grads_joined, grad_out, norm_vec = joined_backward(
+            first, normed, residual, grad_middle, vec_rows, w_joined, (grad_q, grad_k, grad_v))
+        vec_grads = [norm_vec[0], norm_vec[1], mlp_vec[0], mlp_vec[1], mlp_vec[2], mlp_vec[3]]
+        return grad_out, (extra, more), tuple(grads_joined) + (grad_mix, grad_grow, grad_shrink), vec_grads
 
     def weight_grad(rows, grads):
         return jnp.einsum("rd,grc->gdc", rows, grads, preferred_element_type=wide_type).astype(low_type)
@@ -964,7 +1051,7 @@
 
 
 BY_CORE = (True, True, False, False)
-GATHER_ROUTES = (("zxy",), ("zxy",), ("xzy",), ("yzx",))
+GATHER_ROUTES = (("zxy",), ("zyx",), ("xzy",), ("yzx",))
 FORE_PACE, BACK_PACE = (1.0, 1.0), (1.0, 1.0)
 BY_GRAD = (True, True, True, True, False, False)
 ROUTES = (("zxy",), ("zyx",), ("zxy",), ("zyx",), ("zyx",), ("zxy",))
@@ -1084,7 +1171,7 @@
                     list(above) + [grad_head], BY_GRAD + (False,), rows_list + [w_head.shape[0] // devices],
                     ROUTES + (("zyx",),))
                 plan, operands = reduce_plan(
-                    blocks, BY_GRAD + ("group",), ROUTES + (("zyx",),), ((4, 5), (0, 1, 2, 3, 6)))
+                    blocks, BY_GRAD + ("group",), ROUTES + (("zyx",),), ((4, 5), (0, 1, 2), (3, 6)))
                 return Aside(plan, operands, 3, BACK_PACE[0])
             blocks = as_blocks(ready, BY_GRAD[3:], rows_list[3:], ROUTES[3:])
             plan, operands = reduce_plan(blocks, BY_GRAD[3:], ROUTES[3:], ((1, 2), (0,)))
@@ -1114,7 +1201,7 @@
         small = jnp.pad(small, ((0, n_small * devices - feats - vec_total), (0, 0)))
         kinds_last, routes = BY_GRAD[:3] + ("group",), ROUTES[:3] + (("zyx",),)
         blocks = as_blocks(list(big[:3]) + [small], BY_GRAD[:3] + (False,), rows_list[:3] + [n_small], routes)
-        *joined_sums, small_sum, square = reduce_scatter_layer(blocks, kinds_last, routes, ((0, 1, 2, 3),), 4)
+        *joined_sums, small_sum, square = reduce_scatter_layer(blocks, kinds_last, routes, ((0, 1), (2, 3)), 4)
         sums[0] = joined_sums + sums[0]
         scalars = jnp.stack([jnp.sum(sum(squares + [square]))] + scalars)
         scalars = jnp.broadcast_to(jnp.pad(scalars, (0, 125))[None], (8, 128))

time: 604 us -> 596 us (0.987)
  Pallas kernels: 466 us -> 480 us
  matrix products: 46.9 us -> 34.5 us
  other arithmetic: 41.7 us -> 35.2 us
    pallas_call x0 -> x1, Pallas kernels: none -> 17 us  [joined_backward(): pl.pallas_call(functools.partial(joined_back_kernel, first), grid=(groups...]
    dot_general x6 -> x3, matrix products: 13.1 us -> 6.24 us  [row_grad(): jnp.einsum('grc,gdc->rd', grads, w_joined[:, :, part * width:(part + 1) *...]
    dot_general x6 -> x3, matrix products: 13 us -> 7.37 us  [weight_grad(): jnp.einsum('rd,grc->gdc', rows, grads, preferred_element_type=wide_type)]
where the time goes in v6:
time: 596 us; the launch traced here: 590 us
  Pallas kernels  480 us (81%)
  other arithmetic  35.2 us (6%)
  matrix products  34.5 us (6%)
  local copies, waits for them, and re-layouts  31.3 us (5%)
  between operations  8.37 us (1%)
    pallas_call x4, Pallas kernels, with_aside(): pl.pallas_call(kernel, grid=grid, in_specs=list(in_specs) + plan.in_specs...  336 us
    pallas_call x3, Pallas kernels, exchange(): pl.pallas_call(kernel, out_shape=tuple(plan.out_shape()), in_specs=plan.i...  78.3 us
    pallas_call x4, Pallas kernels, with_aside(): pl.pallas_call(functools.partial(body, tick=lambda i: None), grid=grid, i...  49.4 us
    pallas_call x1, Pallas kernels, joined_backward(): pl.pallas_call(functools.partial(joined_back_kernel, first), grid=(groups...  17 us
    dot_general x4, matrix products, grouped(): jnp.einsum('rd,gdc->grc', rows, weight, preferred_element_type=wide_type)  14.1 us

profile of v6, /device:TPU:0, one launch (start us, length us, event | category | flops | bytes accessed | tf_op | source)
XLA Modules:
  0.0 589.8 jit_solution(18334827410923303072)
XLA Ops:
  0.7 1.6 slice_reduce_fusion.4
  3.7 1.8 fusion.57
  6.1 1.0 copy-done.55
  7.1 1.7 add_convert_fusion.1
  9.1 1.8 slice_reduce_fusion
  11.0 0.7 convert_element_type.159.refs_0_
  11.7 32.2 %shard_map.434 = bf16[2,16,2,24,1152]{4,3,2,1,0:T(8,128)(2,1)} custom-call(bf16[2,24,1152]{2,1,0:T(8,128)(2,1)} %convert_element_type.159.refs_0_), custom_call_target="tpu_custom_call" | custom-call | bytes 3538944 | tf_op jit(solution)/shard_map/pallas_call | solution.py:526
  44.0 5.6 convert_bitcast_fusion.1.refs_1_.refs_2_
  49.6 3.9 fusion.16.refs_0_
  54.7 0.8 broadcast_in_dim.22.refs_3_.bias_ref
  55.6 0.7 fusion.53
  56.4 0.7 fusion.54
  57.8 69.9 %shard_map.435 = (bf16[1024,768]{1,0:T(8,128)(2,1)}, f32[6,2,1024]{2,1,0:T(2,128)}, bf16[2,16,1,24,768]{4,3,2,1,0:T(8,128)(2,1)}, bf16[16,2,1,24,3072]{4,3,2,1,0:T(8,128)(2,1)}, bf16[16,2,1,96,768]{4,3,2,1,0:T(8,128)(2,1)}) custom-call(bf16[2,1024,384]{2,1,0:T(8,128)(2,1)} %fusion.16.refs_0_, bf16[2,768,768]{2,1,0:T(8,128)(2,1)} %convert_bitcast_fusion.1.refs_1_.refs_2_, ...), custom_call_target="tpu_custom_call" | custom-call | flops 2415919104 | bytes 6291456 | tf_op jit(solution)/shard_map/pallas_call | solution.py:506
  127.7 1.4 fusion.55
  129.1 1.6 convert_element_type.166.refs_6_
  130.7 75.6 %shard_map.436 = (f32[1024,768]{1,0:T(8,128)}, f32[1024,768]{1,0:T(8,128)}, bf16[1024,3072]{1,0:T(8,128)(2,1)}, bf16[2,16,1,48,1152]{4,3,2,1,0:T(8,128)(2,1)}, b...) custom-call(f32[1024,768]{1,0:T(8,128)} %copy-done, ...), custom_call_target="tpu_custom_call" | custom-call | flops 10871635968 | bytes 18874368 | tf_op jit(solution)/shard_map/pallas_call | solution.py:506
  206.4 2.3 reduce_sum.196
  210.5 2.0 copy-done.69
  212.5 3.4 convert_bitcast_fusion.k_ref.v_ref
  215.8 1.2 fusion.24.q_ref
  217.0 10.0 %shard_map.437 = (bf16[256,768]{1,0:T(8,128)(2,1)}, f32[6,2,256]{2,1,0:T(2,128)}) custom-call(bf16[2,256,384]{2,1,0:T(8,128)(2,1)} %fusion.24.q_ref, bf16[2,768,768]{2,1,0:T(8,128)(2,1)} %convert_bitcast_fusion.k_ref.v_ref, bf16[2,768,768]{2,1,0:T(8,128)(2,1)} %convert_bitcast_fusion.k_ref.v_ref, bf16[768,128]{1,0:T(8,128)(2,1)} %broadcast_in_dim.22.refs_3_.bias_ref), custom_call_target="tpu_custom_call" | custom-call | flops 603979776 | bytes 1572864 | tf_op jit(solution)/shard_map/pallas_call | solution.py:465
  227.0 11.2 %shard_map.438 = (f32[256,768]{1,0:T(8,128)}, f32[256,768]{1,0:T(8,128)}, bf16[256,3072]{1,0:T(8,128)(2,1)}) custom-call(f32[1024,768]{1,0:T(8,128)} %get-tuple-element.87.res_ref, bf16[256,768]{1,0:T(8,128)(2,1)} %get-tuple-element.89.mixed_ref.o_ref, bf16[768,768]{1,0:T(8,128)(2,1)} %bitcast.139, bf16[768,3072]{1,0:T(8,128)(2,1)} %bitcast.133, ...), custom_call_target="tpu_custom_call" | custom-call | flops 2717908992 | bytes 4718592 | tf_op jit(solution)/shard_map/pallas_call | solution.py:465
  238.2 1.3 reduce_sum.198
  239.5 1.4 multiply_reduce_fusion.7
  240.9 2.0 fusion.58
  243.8 1.5 convolution_convert_fusion.3
  245.4 1.2 multiply_reduce_fusion.5
  246.9 1.0 broadcast_add_fusion.u_ref
  247.9 18.6 %shard_map.439 = (bf16[768,3072]{1,0:T(8,128)(2,1)}, bf16[3072,768]{1,0:T(8,128)(2,1)}, bf16[768,768]{1,0:T(8,128)(2,1)}, bf16[256,768]{1,0:T(8,128)(2,1)}, f32[256,768]{1,0:T(8,128)}, /*index=5*/f32[8,768]{1,0:T(8,128)}) custom-call(f32[256,768]{1,0:T(8,128)} %broadcast_add_fusion.u_ref, f32[256,768]{1,0:T(8,128)} %get-tuple-element.94.middle_ref, ...), custom_call_target="tpu_custom_call" | custom-call | flops 5435817984 | bytes 7864320 | tf_op jit(solution)/shard_map/pallas_call | solution.py:465
  266.5 9.7 %shard_map.440 = (bf16[2,256,384]{2,1,0:T(8,128)(2,1)}, bf16[2,768,384]{2,1,0:T(8,128)(2,1)}, bf16[2,768,384]{2,1,0:T(8,128)(2,1)}) custom-call(bf16[2,256,384]{2,1,0:T(8,128)(2,1)} %fusion.24.q_ref, bf16[2,768,768]{2,1,0:T(8,128)(2,1)} %convert_bitcast_fusion.k_ref.v_ref, bf16[2,768,768]{2,1,0:T(8,128)(2,1)} %convert_bitcast_fusion.k_ref.v_ref, ...), custom_call_target="tpu_custom_call" | custom-call | flops 1509949440 | bytes 3145728 | tf_op jit(solution)/shard_map/pallas_call | solution.py:465
  276.2 17.0 %shard_map.441 = (bf16[2,768,384]{2,1,0:T(8,128)(2,1)}, bf16[2,768,384]{2,1,0:T(8,128)(2,1)}, bf16[2,768,384]{2,1,0:T(8,128)(2,1)}, f32[1024,768]{1,0:T(8,128)}, f32[8,768]{1,0:T(8,128)}) custom-call(bf16[1024,768]{1,0:T(8,128)(2,1)} %copy-done.16, f32[1024,768]{1,0:T(8,128)} %get-tuple-element.87.res_ref, f32[256,768]{1,0:T(8,128)} %get-tuple-element.96.mid_ref, ...), custom_call_target="tpu_custom_call" | custom-call | flops 7247757312 | bytes 23592960 | tf_op jit(solution)/shard_map/pallas_call | solution.py:981
  293.2 106.7 %shard_map.442 = (bf16[768,3072]{1,0:T(8,128)(2,1)}, bf16[3072,768]{1,0:T(8,128)(2,1)}, bf16[768,768]{1,0:T(8,128)(2,1)}, bf16[1024,768]{1,0:T(8,128)(2,1)}, f32...) custom-call(f32[1024,768]{1,0:T(8,128)} %get-tuple-element.102.refs_, ...), custom_call_target="tpu_custom_call" | custom-call | flops 21743271936 | bytes 31457280 | tf_op jit(solution)/shard_map/pallas_call | solution.py:506
  399.9 1.4 convert_bitcast_fusion.2.refs_10_
  401.3 83.4 %shard_map.443 = (bf16[2,1024,384]{2,1,0:T(8,128)(2,1)}, bf16[2,768,384]{2,1,0:T(8,128)(2,1)}, bf16[2,768,384]{2,1,0:T(8,128)(2,1)}, f32[1,24,768]{2,1,0:T(8,128...) custom-call(bf16[2,1024,384]{2,1,0:T(8,128)(2,1)} %fusion.16.refs_0_, ...), custom_call_target="tpu_custom_call" | custom-call | flops 6039797760 | bytes 12582912 | tf_op jit(solution)/shard_map/pallas_call | solution.py:506
  484.7 2.9 fusion.26
  487.8 1.1 bitcast_add_fusion.1
  490.2 2.2 multiply_reduce_fusion
  492.4 1.5 fusion.51
  495.7 0.8 slice.250
  496.5 0.7 slice.251
  497.2 0.7 slice.249
  498.1 0.8 pad.10
  498.9 2.1 fusion.23
  501.1 2.4 copy.60
  503.4 2.4 fusion.22
  505.8 1.4 copy.58
  507.2 2.8 fusion.19
  510.1 1.4 copy.56
  511.5 32.0 %shard_map.444 = (f32[1,48,384]{2,1,0:T(8,128)}, f32[1,48,384]{2,1,0:T(8,128)}, f32[1,48,384]{2,1,0:T(8,128)}, f32[1,8,768]{2,1,0:T(8,128)}, f32[1,128]{1,0:T(1,128)}) custom-call(bf16[2,4,2,2,1,48,384]{6,5,4,3,2,1,0:T(8,128)(2,1)} %bitcast.132, bf16[2,4,2,2,1,48,384]{6,5,4,3,2,1,0:T(8,128)(2,1)} %bitcast.131, bf16[2,4,2,2,1,48,384]{6,5,4,3,2,1,0:T(8,128)(2,1)} %bitcast.130, ...), custom_call_target="tpu_custom_call" | custom-call | bytes 125829120 | tf_op jit(solution)/shard_map/pallas_call | solution.py:526
  543.5 1.2 add_reduce_fusion
  544.7 1.3 convert_reduce_fusion
  546.0 2.0 select_maximum_fusion
  548.6 1.3 convert_bitcast_fusion.3.refs_0_
  550.0 14.0 %shard_map.445 = (bf16[2,2,2,4,8,768]{5,4,3,2,1,0:T(8,128)(2,1)}, f32[2,2,2,4,8,128]{5,4,3,2,1,0:T(8,128)}) custom-call(bf16[8,768]{1,0:T(8,128)(2,1)} %convert_bitcast_fusion.3.refs_0_, f32[8,128]{1,0:T(8,128)} %broadcast_in_dim.27.refs_1_), custom_call_target="tpu_custom_call" | custom-call | bytes 458752 | tf_op jit(solution)/shard_map/pallas_call | solution.py:526
  564.0 1.1 slice_reduce_fusion.2
  567.8 1.3 convert_multiply_fusion
  569.2 4.8 multiply_add_fusion.1
  574.1 1.4 multiply_add_fusion.3
  576.3 1.4 multiply_add_fusion.5
  577.8 0.8 multiply_add_fusion.9
  579.4 1.2 copy.65
  580.6 1.2 copy.66
  581.8 1.2 copy.67
  583.9 1.1 multiply_add_fusion.7
  (183 shorter events, 14.3 us)
Async XLA Ops:
  2.3 4.8 copy-start.51
  3.0 2.5 copy-start.57
  3.7 1.8 copy-start.65
  5.5 1.6 copy-start
  5.5 1.6 copy-start.46
  6.1 2.8 copy-start.53
  7.1 1.7 copy-start.12
  44.0 5.6 copy-start.14
  49.6 3.9 copy-start.68
  49.6 6.0 %copy-start.8 = (f32[2,96,768]{2,1,0:T(8,128)S(1)}, f32[2,96,768]{2,1,0:T(8,128)}, u32[]{:S(2)}) copy-start(f32[2,96,768]{2,1,0:T(8,128)} %param.48) | copy-start | bytes 1769476
  53.5 2.9 copy-start.10
  54.7 2.4 copy-start.24
  206.4 2.8 copy-start.2
  209.9 2.6 copy-start.69
  210.4 5.4 copy-start.16
  238.2 2.7 copy-start.3
  238.2 2.7 copy-start.48
  238.2 2.7 copy-start.59
  240.9 2.0 copy-start.64
  240.9 2.3 copy-start.67
  242.9 2.5 copy-start.4
  484.7 2.9 copy-start.6
  484.7 3.0 copy-start.18
  487.8 1.9 copy-start.1
  487.8 1.9 copy-start.47
  487.8 1.9 copy-start.52
  487.8 1.9 copy-start.54
  487.8 2.4 copy-start.70
  490.2 2.2 copy-start.56
  492.4 1.9 copy-start.7
  492.4 1.9 copy-start.58
  494.9 3.0 copy-start.63
  495.0 3.0 copy-start.62
  495.2 3.7 copy-start.15
  564.0 5.1 copy-start.5
  569.1 4.8 copy-start.9
  569.1 4.8 copy-start.20
  569.2 4.8 copy-start.21
  569.2 4.8 copy-start.33
  569.2 4.8 copy-start.35
  574.0 1.4 copy-start.11
  574.0 1.5 copy-start.22
  574.0 2.0 copy-start.23
  574.0 2.1 copy-start.32
  574.1 2.2 copy-start.34
  576.2 1.5 copy-start.25
  576.2 1.5 copy-start.36
  576.2 1.5 copy-start.37
  576.2 1.5 copy-start.41
  576.3 1.5 copy-start.42
  576.3 2.3 copy-start.38
  576.3 2.3 copy-start.39
  576.3 2.3 copy-start.40
  576.3 2.3 copy-start.43
  576.3 2.3 copy-start.44
  576.3 2.3 copy-start.45
  577.7 1.4 copy-start.27
  579.4 3.7 copy-start.28
  580.6 2.5 copy-start.31
  580.6 2.5 copy-start.49
  580.6 2.5 copy-start.50
  581.8 2.0 copy-start.17
  581.8 2.0 copy-start.29
  581.8 2.1 copy-start.30
  (7 other events, 6.7 us)
